TPU v7x, 32 devices: a whole 2x2x4 slice. The times are simulated.
32 devices in a mesh: block: 4 (over y, x), span: 2 (over core), stream: 4 (over z).
Axes of the slice: x: 2, y: 2, z: 4, core: 2. Of those that a mesh axis runs over, the one named last changes fastest.
Arguments:
- flow_state: float32 [4, 256, 16, 5, 1024], P('block', 'stream', None, None, 'span'), may hold values from -6 to 6
- wave_speed: float32 [4, 256, 16, 1024], P('block', 'stream', None, 'span'), may hold values from 0.5 to 2
- char_scale: float32 [5], replicated, may hold values from 0.002 to 4
- span_ratio: float32 [5], replicated, may hold values from 0.3 to 1
- send_tile: int32 [4, 2, 4, 8, 16], P('block', 'span', 'stream'), may hold values from 0 to 1023
- recv_tile: int32 [4, 2, 4, 8, 16], P('block', 'span', 'stream'), may hold values from 0 to 1023, as said below
- recv_live: int32 [4, 2, 4, 8, 16], P('block', 'span', 'stream'), may hold values from 0 to 1, as said below
- interp_weight: float32 [4, 2, 4, 8, 16], P('block', 'span', 'stream'), may hold values from 0.2 to 1
Outputs:
- new_state: float32 [4, 256, 16, 5, 1024], P('block', 'stream', None, None, 'span')
Inputs may be any that keep to these rules, and one draw needn't show every extreme that they name: `recv_tile`: the 128 entries of one device are all different. `recv_live`: on each device the live slots from one peer come first; every device has 16 live slots from at least one peer, and one device has 16 from every peer.
All inputs are finite; a program needn't handle non-finite values.
Results may differ from a plain program's by a relative error of at most 0.000088.
Values sent between devices are 32-bit elements; how exact they have to be, the bound alone decides.
No kernel may reach another device: no remote copies, remote signals or barrier semaphores. Data moves between devices by JAX's collectives and lax.ppermute only.
A program may use at most 256 MiB of HBM per device.

v0:
```python
import functools
import jax
import jax.numpy as jnp
from jax import lax
from jax.experimental import pallas as pl
from jax.experimental.pallas import tpu as pltpu
from jax.sharding import PartitionSpec as P


LANES = 128
SUB = 8
STEPS = 16
F32 = jnp.float32


def space(kind):
    return pl.BlockSpec(memory_space=kind)


SMEM, VMEM, HBM = pltpu.SMEM, pltpu.VMEM, pltpu.HBM

RING = ("block", "span")


def limited(first, second):
    return jnp.maximum(
        jnp.minimum(second, jnp.maximum(first, 0.0)), jnp.minimum(first, 0.0)
    )


def call(kernel, ins, outs, out_shape, scratch=(), aliases=None, limit=8 << 20, micros=0):
    return pl.pallas_call(
        kernel,
        out_shape=out_shape,
        in_specs=[space(k) for k in ins],
        out_specs=[space(k) for k in outs],
        scratch_shapes=list(scratch),
        input_output_aliases=aliases or {},
        compiler_params=pltpu.CompilerParams(vmem_limit_bytes=limit),
        cost_estimate=pl.CostEstimate(flops=0, transcendentals=0, bytes_accessed=int(micros * 3.0e6)),
    )


def present(ref, axis, distance):
    source = lax.axis_index(axis) - distance
    inside = (source >= 0) & (source < lax.axis_size(axis))
    return ref[...] * jnp.where(inside, 1.0, 0.0)


def gather_kernel(turns, send_ref, flow_ref, *refs):
    *out_refs, sem = refs
    _, capacity, _ = out_refs[0].shape
    rows_y = flow_ref.shape[2]
    place = lax.axis_index(RING)

    def copy_of(out_ref, turn, slot):
        tile = send_ref[place ^ turn, slot]
        return pltpu.make_async_copy(
            flow_ref.at[tile // rows_y, :, pl.ds(tile % rows_y, 1), :],
            out_ref.at[:, pl.ds(slot, 1), :],
            sem,
        )

    for out_ref, turn in zip(out_refs, turns):

        @pl.loop(0, capacity)
        def _(slot):
            copy_of(out_ref, turn, slot).start()

    for out_ref, turn in zip(out_refs, turns):

        @pl.loop(0, capacity)
        def _(slot):
            copy_of(out_ref, turn, slot).wait()


def growth_kernel(scale_ref, flow_hbm, speed_hbm, flow_ref, speed_ref, ratio_ref, growth_ref, total_ref, last_ref, sem):
    width_x, components, rows_y, width_z = growth_ref.shape
    speed_copy = pltpu.make_async_copy(speed_hbm, speed_ref, sem.at[0])
    flow_copy = pltpu.make_async_copy(flow_hbm, flow_ref, sem.at[1])
    speed_copy.start()
    flow_copy.start()
    speed_copy.wait()
    halves = rows_y // SUB

    @pl.loop(0, components * halves)
    def _(group):
        v = group // halves
        y = pl.ds(pl.multiple_of((group % halves) * SUB, SUB), SUB)
        scale = 100.0 * scale_ref[v]

        def step(x, run):
            rate = scale * speed_ref[x, y, :]
            ratio = 1.0 / (1.0 + rate)
            grown = ratio * run
            ratio_ref[x, v, y, :] = ratio
            growth_ref[x, v, y, :] = grown
            return rate * grown

        total_ref[v, y, :] = lax.fori_loop(0, width_x, step, jnp.ones((SUB, width_z), F32), unroll=4)
        last_ref[v, y, :] = scale * speed_ref[width_x - 1, y, :] * ratio_ref[width_x - 1, v, y, :]

    flow_copy.wait()


def fill_kernel(turns, extra, tile_ref, live_ref, weight_ref, flow_ref, *refs):
    arrived_refs = refs[: len(turns)]
    filled_ref = refs[len(turns) + extra]
    rows_y = filled_ref.shape[2]
    components, capacity, _ = arrived_refs[0].shape
    place = lax.axis_index(RING)

    for turn, arrived_ref in zip(turns, arrived_refs):
        peer = place ^ turn

        @pl.loop(0, capacity)
        def _(slot):
            @pl.when(live_ref[peer, slot] == 1)
            def _():
                tile = tile_ref[peer, slot]
                weight = weight_ref[peer, slot]
                x = tile // rows_y
                y = pl.ds(tile % rows_y, 1)
                for v in range(components):
                    old = filled_ref[x, v, y, :]
                    new = arrived_ref[v, pl.ds(slot, 1), :]
                    filled_ref[x, v, y, :] = (1.0 - weight) * old + weight * new


def last_fill_kernel(turns, extra, *refs):
    *fill_refs, rows_ref, tail_ref, head_ref = refs
    fill_kernel(turns, extra, *fill_refs)
    filled_ref = fill_refs[-1]
    width_x, components, rows_y, width_z = filled_ref.shape
    lane = lax.broadcasted_iota(jnp.int32, (rows_y, LANES), 1)
    for v in range(components):

        def pack(x, packed):
            tail, head = packed
            here = lane // 2 == x
            tail = jnp.where(
                here, pltpu.roll(filled_ref[x, v, :, width_z - LANES :], 2 * x + 2, 1), tail
            )
            head = jnp.where(here, pltpu.roll(filled_ref[x, v, :, :LANES], 2 * x + 1, 1), head)
            return tail, head

        zero = jnp.zeros((rows_y, LANES), F32)
        tail_ref[v], head_ref[v] = lax.fori_loop(0, width_x, pack, (zero, zero), unroll=32)
        for spot, x in enumerate((0, 1, width_x - 2, width_x - 1)):
            rows_ref[spot, v] = filled_ref[x, v]


def scan_kernel(
    lowest, scale_ref, span_ref, filled_ref, ratio_ref, speed_ref, tail_ref, head_ref, before_ref, after_ref,
    local_ref, out_ref, prior_ref, face_ref, diff_ref
):
    width_x, _, rows_y, width_z = local_ref.shape
    components = out_ref.shape[0]
    halves = rows_y // SUB
    blocks = width_z // LANES
    before = present(before_ref, "span", 1)
    after = present(after_ref, "span", -1)
    tail = tail_ref[...]
    head = head_ref[...]
    outer = 0.5 * (before - pltpu.roll(before, 1, 2))
    inner = 0.5 * (head - before)
    prior_ref[...] = before
    face_ref[...] = before + limited(outer, inner)
    diff_ref[...] = 0.5 * (after - tail)
    lane = lax.broadcasted_iota(jnp.int32, (SUB, LANES), 1)
    first = lane == 0
    final = lane == LANES - 1

    @pl.loop(0, components * halves)
    def _(group):
        v = lowest + group // halves
        y = pl.ds(pl.multiple_of((group % halves) * SUB, SUB), SUB)
        scale_z = 100.0 * (scale_ref[v] * span_ref[v])
        prior = prior_ref[v, y, :]
        face = face_ref[v, y, :]
        diff = diff_ref[v, y, :]
        every = range(blocks)

        def load(ref, *at):
            return [ref[(*at, y, slice(b * LANES, (b + 1) * LANES))] for b in every]

        def right(values, edge):
            moved_right = [edge] + [pltpu.roll(u, 1, 1) for u in values]
            return [jnp.where(first, moved_right[b], moved_right[b + 1]) for b in every]

        def left(values, edge):
            moved_left = [pltpu.roll(u, LANES - 1, 1) for u in values] + [edge]
            return [jnp.where(final, moved_left[b + 1], moved_left[b]) for b in every]

        def steps(k, carry):
            here, rise, inflow = carry
            start = k * STEPS
            span = range(STEPS)
            turn = [LANES - 2 * (start + i) - 1 for i in span]
            rows = [here] + [load(filled_ref, start + i, v) for i in range(1, STEPS)]
            rows.append(load(filled_ref, jnp.minimum(start + STEPS, width_x - 1), v))
            back = [right(rows[i], pltpu.roll(prior, turn[i], 1)) for i in span]
            fall = [[0.5 * (rows[i][b] - back[i][b]) for b in every] for i in span]
            grow = [left(fall[i], pltpu.roll(diff, turn[i] - 1, 1)) for i in span]
            faces = [[rows[i][b] + limited(fall[i][b], grow[i][b]) for b in every] for i in span]
            shifted = [right(faces[i], pltpu.roll(face, turn[i], 1)) for i in span]
            known = [[rows[i][b] + scale_z * (shifted[i][b] - faces[i][b]) for b in every] for i in span]
            outs = []
            for i in span:
                u = rows[i]
                ratio = load(ratio_ref, start + i, v)
                rise_later = [0.5 * (rows[i + 1][b] - u[b]) for b in every]
                slope = [limited(rise[b], rise_later[b]) for b in every]
                total = [inflow[b] + (known[i][b] + slope[b]) for b in every]
                value = [ratio[b] * total[b] for b in every]
                inflow = [total[b] - value[b] for b in every]
                rise = rise_later
                outs.append([value[b] - slope[b] for b in every])
            for i in span:
                for b in every:
                    local_ref[start + i, v, y, slice(b * LANES, (b + 1) * LANES)] = outs[i][b]
            return rows[STEPS], rise, inflow

        zeros = [jnp.zeros((SUB, LANES), F32)] * blocks
        _, _, flux = lax.fori_loop(0, width_x // STEPS, steps, (load(filled_ref, 0, v), zeros, zeros))
        for b in every:
            out_ref[v - lowest, y, slice(b * LANES, (b + 1) * LANES)] = flux[b]


def edge_kernel(
    lowest, flux_ref, total_ref, last_ref, rows_ref, behind_ref, ahead_ref, flux_out, first_out, last_out
):
    part = pl.ds(lowest, flux_ref.shape[0])
    behind = present(behind_ref.at[part], "stream", 1)
    ahead = present(ahead_ref.at[part], "stream", -1)
    row = [rows_ref[k, part] for k in range(4)]
    slope_first = limited(0.5 * (row[0] - behind), 0.5 * (row[1] - row[0]))
    slope_last = limited(0.5 * (row[3] - row[2]), 0.5 * (ahead - row[3]))
    kept = last_ref[part] * slope_last
    flux_out[...] = flux_ref[...] + total_ref[part] * slope_first + kept
    first_out[...] = slope_first
    last_out[...] = kept


def combine_kernel(lowest, begun, local_ref, growth_ref, first_ref, last_ref, *refs):
    *line_refs, out_hbm, done_ref, inflow_ref, sem = refs[begun:]
    width_x, _, _, _ = local_ref.shape
    components = first_ref.shape[0]
    count = (len(line_refs) + 1) // 2
    flux_refs, total_refs = line_refs[:count], line_refs[count:]
    inflow = first_ref[...]
    product = None
    for distance in range(1, count + 1):
        flux = present(flux_refs[distance - 1], "stream", distance)
        inflow = inflow + (flux if product is None else product * flux)
        if distance < count:
            total = total_refs[distance - 1][pl.ds(lowest, components)]
            product = total if product is None else product * total
    inflow_ref[...] = inflow
    part = 4

    def copy_of(k):
        rows = pl.ds(k * part, part)
        return pltpu.make_async_copy(
            done_ref.at[rows], out_hbm.at[rows, pl.ds(lowest, components)], sem
        )

    @pl.loop(0, width_x // part)
    def _(k):
        for v in range(components):
            inflow = inflow_ref[v]
            for i in range(part):
                x = k * part + i
                done_ref[x, v] = local_ref[x, lowest + v] + growth_ref[x, lowest + v] * inflow

        @pl.when(k == 0)
        def _():
            done_ref[0] = done_ref[0] - first_ref[...]

        @pl.when(k == width_x // part - 1)
        def _():
            done_ref[width_x - 1] = done_ref[width_x - 1] - last_ref[...]

        copy_of(k).start()

    @pl.loop(0, width_x // part)
    def _(k):
        copy_of(k).wait()


def moved(value, axis, distance):
    count = lax.axis_size(axis)
    return lax.ppermute(value, axis, [(i, (i + distance) % count) for i in range(count)])


def on_device(
    flow_state, wave_speed, char_scale, span_ratio, send_tile, recv_tile, recv_live, interp_weight
):
    _, width_x, rows_y, components, width_z = flow_state.shape
    peers, capacity = send_tile.shape[-2:]
    sections = lax.axis_size("stream")
    flow = pltpu.with_memory_space_constraint(jnp.transpose(flow_state[0], (0, 2, 1, 3)), HBM)
    speed = wave_speed[0]
    state = (width_x, components, rows_y, width_z)
    line = (components, rows_y, width_z)
    edge = (components, rows_y, LANES)
    hold = lambda shape: pltpu.VMEM(shape, F32)
    send, tile, live, weight = (
        t.reshape(peers, capacity) for t in (send_tile, recv_tile, recv_live, interp_weight)
    )
    assert peers & (peers - 1) == 0

    order = sorted(range(1, peers), key=lambda turn: (turn == 1, turn & 1, turn))
    early, late = order[: peers // 2 - 1], order[peers // 2 - 1 :] + [0]
    arrived = {}
    for turns in (early, late):
        outgoing = call(
            functools.partial(gather_kernel, turns),
            (SMEM, HBM), (VMEM,) * len(turns),
            [jax.ShapeDtypeStruct((components, capacity, width_z), F32)] * len(turns),
            [pltpu.SemaphoreType.DMA],
            micros=2,
        )(send, flow)
        for turn, tiles in zip(turns, outgoing):
            route = [(i, i ^ turn) for i in range(peers)]
            arrived[turn] = lax.ppermute(tiles, RING, route) if turn else tiles
    flow_in, speed_in, ratio, growth, total, last = call(
        growth_kernel,
        (SMEM, HBM, HBM), (VMEM,) * 6,
        [hold(state), hold(speed.shape), hold(state), hold(state), hold(line), hold(line)],
        [pltpu.SemaphoreType.DMA((2,))],
        micros=6,
    )(char_scale, flow, speed)
    totals = [moved(total, "stream", d) for d in range(1, sections - 1)]
    (partly,) = call(
        functools.partial(fill_kernel, early, 0),
        (SMEM,) * 3 + (VMEM,) * (1 + len(early)), (VMEM,),
        [hold(state)],
        aliases={3: 0},
        micros=2,
    )(tile, live, weight, flow_in, *(arrived[turn] for turn in early))
    filled, rows, tail, head = call(
        functools.partial(last_fill_kernel, late, 0),
        (SMEM,) * 3 + (VMEM,) * (1 + len(late)), (VMEM,) * 4,
        [hold(state), hold((4, *line)), hold(edge), hold(edge)],
        aliases={3: 0},
        micros=4,
    )(tile, live, weight, partly, *(arrived[turn] for turn in late))
    before = moved(tail, "span", 1)
    after = moved(head, "span", -1)
    behind = moved(rows[3], "stream", 1)
    ahead = moved(rows[0], "stream", -1)
    split = (components + 1) // 2
    state_now, parts = filled, []
    for lowest, size in ((0, split), (split, components - split)):
        some = (size, rows_y, width_z)
        state_now, flux = call(
            functools.partial(scan_kernel, lowest),
            (SMEM, SMEM) + (VMEM,) * 7, (VMEM,) * 2,
            [hold(state), hold(some)],
            [pltpu.VMEM(edge, F32)] * 3,
            aliases={2: 0},
            micros=3 * size,
        )(char_scale, span_ratio, state_now, ratio, speed_in, tail, head, before, after)
        flux, first_slope, last_slope = call(
            functools.partial(edge_kernel, lowest),
            (VMEM,) * 6, (VMEM,) * 3,
            [jax.ShapeDtypeStruct(some, F32)] * 3,
        )(flux, total, last, rows, behind, ahead)
        fluxes = [moved(flux, "stream", d) for d in range(1, sections)]
        parts.append((lowest, some, first_slope, last_slope, fluxes))
    begun = ()
    for lowest, some, first_slope, last_slope, fluxes in parts:
        begun = call(
            functools.partial(combine_kernel, lowest, len(begun)),
            (VMEM,) * 4 + (HBM,) * len(begun) + (VMEM,) * (2 * sections - 3), (HBM,),
            [jax.ShapeDtypeStruct(state, F32)],
            [
                pltpu.VMEM((width_x, *some), F32),
                pltpu.VMEM(some, F32),
                pltpu.SemaphoreType.DMA,
            ],
            aliases={4: 0} if begun else None,
            limit=10 << 20,
            micros=some[0],
        )(state_now, growth, first_slope, last_slope, *begun, *fluxes, *totals)
    (done,) = begun
    return jnp.transpose(done, (0, 2, 1, 3))[None]


def solution(mesh):
    return jax.shard_map(
        on_device,
        mesh=mesh,
        in_specs=(
            P("block", "stream", None, None, "span"),
            P("block", "stream", None, "span"),
            P(),
            P(),
            P("block", "span", "stream", None, None),
            P("block", "span", "stream", None, None),
            P("block", "span", "stream", None, None),
            P("block", "span", "stream", None, None),
        ),
        out_specs=P("block", "stream", None, None, "span"),
        check_vma=False,
    )
```

profile of v0, /device:TPU:0, one launch (start us, length us, event | category | flops | bytes accessed | tf_op | source)
XLA Modules:
  0.0 66.0 jit_solution(3089410958189470141)
XLA Ops:
  0.0 0.7 %copy-done.1 = s32[1,1,1,8,16]{4,3,2,1,0:T(8,128)S(1)} copy-done((s32[1,1,1,8,16]{4,3,2,1,0:T(8,128)S(1)}, s32[1,1,1,8,16]{4,3,2,1,0:T(8,128)}, u32[]{:S(2)}) %copy-start.1) | copy-done | bytes 536
  0.7 2.4 %shard_map.83 = (f32[5,16,512]{2,1,0:T(8,128)S(1)}, f32[5,16,512]{2,1,0:T(8,128)S(1)}, f32[5,16,512]{2,1,0:T(8,128)S(1)}) custom-call(s32[8,16]{1,0:T(8,128)S(1)} %bitcast.16, f32[64,5,16,512]{3,2,1,0:T(8,128)} %bitcast.24), custom_call_target="tpu_custom_call" | custom-call | bytes 6000000 | tf_op jit(solution)/shard_map/pallas_call | solution.py:317
  3.1 3.0 %collective-permute-start = (f32[5,16,512]{2,1,0:T(8,128)S(1)}, f32[5,16,512]{2,1,0:T(8,128)S(1)}, u32[]{:S(2)}, u32[]{:S(2)}) collective-permute-start(f32[5,16,512]{2,1,0:T(8,128)S(1)} %get-tuple-element.34), channel_id=1, source_target_pairs={{0,8},{4,12},{8,0},{12,4},{16,24},{20,28},{24,16},{28,20},{1,9},{5... | collective-permute-start | bytes 491528 | tf_op jit(solution)/shard_map/ppermute | solution.py:326
  6.1 1.5 %collective-permute-start.1 = (f32[5,16,512]{2,1,0:T(8,128)S(1)}, f32[5,16,512]{2,1,0:T(8,128)S(1)}, u32[]{:S(2)}, u32[]{:S(2)}) collective-permute-start(f32[5,16,512]{2,1,0:T(8,128)S(1)} %get-tuple-element.35), channel_id=1, source_target_pairs={{0,16},{4,20},{8,24},{12,28},{16,0},{20,4},{24,8},{28,12},{1,17},{... | collective-permute-start | bytes 491528 | tf_op jit(solution)/shard_map/ppermute | solution.py:326
  7.7 3.0 %shard_map.85 = (f32[5,16,512]{2,1,0:T(8,128)S(1)}, f32[5,16,512]{2,1,0:T(8,128)S(1)}, f32[5,16,512]{2,1,0:T(8,128)S(1)}, f32[5,16,512]{2,1,0:T(8,128)S(1)}, f32[5,16,512]{2,1,0:T(8,128)S(1)}) custom-call(s32[8,16]{1,0:T(8,128)S(1)} %bitcast.17, f32[64,5,16,512]{3,2,1,0:T(8,128)} %bitcast.25), custom_call_target="tpu_custom_call" | custom-call | bytes 6000000 | tf_op jit(solution)/shard_map/pallas_call | solution.py:317
  10.7 0.6 collective-permute-start.3
  11.3 2.6 %collective-permute-start.4 = (f32[5,16,512]{2,1,0:T(8,128)S(1)}, f32[5,16,512]{2,1,0:T(8,128)S(1)}, u32[]{:S(2)}, u32[]{:S(2)}) collective-permute-start(f32[5,16,512]{2,1,0:T(8,128)S(1)} %get-tuple-element.38), channel_id=1, source_target_pairs={{0,20},{4,16},{8,28},{12,24},{16,4},{20,0},{24,12},{28,8},{1,21},{... | collective-permute-start | bytes 491528 | tf_op jit(solution)/shard_map/ppermute | solution.py:326
  14.0 1.4 %collective-permute-done.1.refs_1_ = f32[5,16,512]{2,1,0:T(8,128)S(1)} collective-permute-done((f32[5,16,512]{2,1,0:T(8,128)S(1)}, f32[5,16,512]{2,1,0:T(8,128)S(1)}, u32[]{:S(2)}, u32[]{:S(2)}) %collective-permute-start.1) | collective-permute-done | bytes 163872 | tf_op jit(solution)/shard_map/ppermute | solution.py:326
  15.4 4.7 %shard_map.82 = (f32[64,5,16,512]{3,2,1,0:T(8,128)S(1)}, f32[64,16,512]{2,1,0:T(8,128)S(1)}, f32[64,5,16,512]{3,2,1,0:T(8,128)S(1)}, f32[64,5,16,512]{3,2,1,0:T(...) custom-call(f32[5]{0:T(128)S(1)} %copy-done.5, f32[64,5,16,512]{3,2,1,0:T(8,128)} %bitcast.26, ...), custom_call_target="tpu_custom_call" | custom-call | bytes 18000000 | tf_op jit(solution)/shard_map/pallas_call | solution.py:327
  20.1 1.9 %shard_map.84.refs_3_ = f32[64,5,16,512]{3,2,1,0:T(8,128)S(1)} custom-call(s32[8,16]{1,0:T(8,128)S(1)} %bitcast.18, s32[8,16]{1,0:T(8,128)S(1)} %bitcast.20, f32[8,16]{1,0:T(8,128)S(1)} %bitcast.22, f32[64,5,16,512]{3,2,1,0:T(8,128)S(1)} %get-tuple-element.33.flow_ref, ...), custom_call_target="tpu_custom_call", output_to_operand_aliasing={{}: (3, {})} | custom-call | bytes 6000000 | tf_op jit(solution)/shard_map/pallas_call | solution.py:335
  22.2 4.5 %shard_map.86 = (f32[64,5,16,512]{3,2,1,0:T(8,128)S(1)}, f32[4,5,16,512]{3,2,1,0:T(8,128)S(1)}, f32[5,16,128]{2,1,0:T(8,128)S(1)}, f32[5,16,128]{2,1,0:T(8,128)S(1)}) custom-call(s32[8,16]{1,0:T(8,128)S(1)} %bitcast.19, s32[8,16]{1,0:T(8,128)S(1)} %bitcast.21, f32[8,16]{1,0:T(8,128)S(1)} %bitcast.23, ...), custom_call_target="tpu_custom_call", output_to_operand_aliasing={{0}: (3, {})} | custom-call | bytes 12000000 | tf_op jit(solution)/shard_map/pallas_call | solution.py:342
  26.8 3.8 %collective-permute-start.10 = (f32[5,16,512]{2,1,0:T(8,128)S(1)}, f32[5,16,512]{2,1,0:T(8,128)S(1)}, u32[]{:S(2)}, u32[]{:S(2)}) collective-permute-start(f32[5,16,512]{2,1,0:T(8,128)S(1)} %get-tuple-element.61), channel_id=1, source_target_pairs={{0,3},{1,0},{2,1},{3,2},{4,7},{5,4},{6,5},{7,6},{8,11},{9,8},{10,9... | collective-permute-start | bytes 491528 | tf_op jit(solution)/shard_map/ppermute | solution.py:293
  30.6 1.1 %collective-permute-start.15 = (f32[5,16,512]{2,1,0:T(8,128)S(1)}, f32[5,16,512]{2,1,0:T(8,128)S(1)}, u32[]{:S(2)}, u32[]{:S(2)}) collective-permute-start(f32[5,16,512]{2,1,0:T(8,128)S(1)} %get-tuple-element.51.total_ref), channel_id=1, source_target_pairs={{0,2},{1,3},{2,0},{3,1},{4,6},{5,7},{6,4},{7,5},{8,10},{9,11},{10,... | collective-permute-start | bytes 491528 | tf_op jit(solution)/shard_map/ppermute | solution.py:293
  31.7 3.2 %collective-permute-start.14 = (f32[5,16,512]{2,1,0:T(8,128)S(1)}, f32[5,16,512]{2,1,0:T(8,128)S(1)}, u32[]{:S(2)}, u32[]{:S(2)}) collective-permute-start(f32[5,16,512]{2,1,0:T(8,128)S(1)} %get-tuple-element.51.total_ref), channel_id=1, source_target_pairs={{0,1},{1,2},{2,3},{3,0},{4,5},{5,6},{6,7},{7,4},{8,9},{9,10},{10,1... | collective-permute-start | bytes 491528 | tf_op jit(solution)/shard_map/ppermute | solution.py:293
  35.0 1.2 %collective-permute-done.8.after_ref = f32[5,16,128]{2,1,0:T(8,128)S(1)} collective-permute-done((f32[5,16,128]{2,1,0:T(8,128)S(1)}, f32[5,16,128]{2,1,0:T(8,128)S(1)}, u32[]{:S(2)}, u32[]{:S(2)}) %collective-permute-start.8) | collective-permute-done | bytes 40992 | tf_op jit(solution)/shard_map/ppermute | solution.py:293
  36.2 9.2 %shard_map.87 = (f32[64,5,16,512]{3,2,1,0:T(8,128)S(1)}, f32[3,16,512]{2,1,0:T(8,128)S(1)}) custom-call(f32[5]{0:T(128)S(1)} %copy-done.5, f32[5]{0:T(128)S(1)} %copy-done.6, f32[64,5,16,512]{3,2,1,0:T(8,128)S(1)} %get-tuple-element.42.filled_ref, f32[64,5,16,512]{3,2,1,0:T(8,128)S(1)} %get-tuple-element.43.ratio_ref, ...), custom_call_target="tpu_custom_call", output_to_operand_aliasing={{0}: (2, {})} | custom-call | bytes 27000000 | tf_op jit(solution)/shard_map/pallas_call | solution.py:357
  45.5 0.7 %collective-permute-start.13 = (f32[3,16,512]{2,1,0:T(8,128)S(1)}, f32[3,16,512]{2,1,0:T(8,128)S(1)}, u32[]{:S(2)}, u32[]{:S(2)}) collective-permute-start(f32[3,16,512]{2,1,0:T(8,128)S(1)} %get-tuple-element.59), channel_id=1, source_target_pairs={{0,3},{1,0},{2,1},{3,2},{4,7},{5,4},{6,5},{7,6},{8,11},{9,8},{10,9... | collective-permute-start | bytes 294920 | tf_op jit(solution)/shard_map/ppermute | solution.py:293
  46.2 0.8 %collective-permute-start.12 = (f32[3,16,512]{2,1,0:T(8,128)S(1)}, f32[3,16,512]{2,1,0:T(8,128)S(1)}, u32[]{:S(2)}, u32[]{:S(2)}) collective-permute-start(f32[3,16,512]{2,1,0:T(8,128)S(1)} %get-tuple-element.59), channel_id=1, source_target_pairs={{0,2},{1,3},{2,0},{3,1},{4,6},{5,7},{6,4},{7,5},{8,10},{9,11},{10,... | collective-permute-start | bytes 294920 | tf_op jit(solution)/shard_map/ppermute | solution.py:293
  47.6 6.3 %shard_map.88 = (f32[64,5,16,512]{3,2,1,0:T(8,128)S(1)}, f32[2,16,512]{2,1,0:T(8,128)S(1)}) custom-call(f32[5]{0:T(128)S(1)} %copy-done.5, f32[5]{0:T(128)S(1)} %copy-done.6, f32[64,5,16,512]{3,2,1,0:T(8,128)S(1)} %get-tuple-element.47.filled_ref, f32[64,5,16,512]{3,2,1,0:T(8,128)S(1)} %get-tuple-element.43.ratio_ref, ...), custom_call_target="tpu_custom_call", output_to_operand_aliasing={{0}: (2, {})} | custom-call | bytes 18000000 | tf_op jit(solution)/shard_map/pallas_call | solution.py:357
  54.0 3.3 %collective-permute-start.18 = (f32[2,16,512]{2,1,0:T(8,128)S(1)}, f32[2,16,512]{2,1,0:T(8,128)S(1)}, u32[]{:S(2)}, u32[]{:S(2)}) collective-permute-start(f32[2,16,512]{2,1,0:T(8,128)S(1)} %get-tuple-element.60), channel_id=1, source_target_pairs={{0,3},{1,0},{2,1},{3,2},{4,7},{5,4},{6,5},{7,6},{8,11},{9,8},{10,9... | collective-permute-start | bytes 196616 | tf_op jit(solution)/shard_map/ppermute | solution.py:293
  57.6 1.4 %collective-permute-start.16 = (f32[2,16,512]{2,1,0:T(8,128)S(1)}, f32[2,16,512]{2,1,0:T(8,128)S(1)}, u32[]{:S(2)}, u32[]{:S(2)}) collective-permute-start(f32[2,16,512]{2,1,0:T(8,128)S(1)} %get-tuple-element.60), channel_id=1, source_target_pairs={{0,1},{1,2},{2,3},{3,0},{4,5},{5,6},{6,7},{7,4},{8,9},{9,10},{10,1... | collective-permute-start | bytes 196616 | tf_op jit(solution)/shard_map/ppermute | solution.py:293
  59.0 2.8 %shard_map.91.refs_0_ = f32[64,5,16,512]{3,2,1,0:T(8,128)} custom-call(f32[64,5,16,512]{3,2,1,0:T(8,128)S(1)} %get-tuple-element.48.local_ref, f32[64,5,16,512]{3,2,1,0:T(8,128)S(1)} %get-tuple-element.49.growth_ref, f32[3,16,512]{2,1,0:T(8,128)S(1)} %get-tuple-element.57.first_ref, f32[3,16,512]{2,1,0:T(8,128)S(1)} %get-tuple-element.58.last_ref, ...), custom_call_target="tpu_custom_call" | custom-call | bytes 9000000 | tf_op jit(solution)/shard_map/pallas_call | solution.py:374
  61.7 2.2 %collective-permute-done.17.refs_2_ = f32[2,16,512]{2,1,0:T(8,128)S(1)} collective-permute-done((f32[2,16,512]{2,1,0:T(8,128)S(1)}, f32[2,16,512]{2,1,0:T(8,128)S(1)}, u32[]{:S(2)}, u32[]{:S(2)}) %collective-permute-start.17) | collective-permute-done | bytes 65568 | tf_op jit(solution)/shard_map/ppermute | solution.py:293
  63.9 2.1 %shard_map.92 = f32[64,5,16,512]{3,2,1,0:T(8,128)} custom-call(f32[64,5,16,512]{3,2,1,0:T(8,128)S(1)} %get-tuple-element.48.local_ref, f32[64,5,16,512]{3,2,1,0:T(8,128)S(1)} %get-tuple-element.49.growth_ref, f32[2,16,512]{2,1,0:T(8,128)S(1)} %get-tuple-element.54.first_ref, ...), custom_call_target="tpu_custom_call", output_to_operand_aliasing={{}: (4, {})} | custom-call | bytes 6000000 | tf_op jit(solution)/shard_map/pallas_call | solution.py:374
  (40 shorter events, 1.4 us)
Async XLA Ops:
  0.7 14.7 %copy-start = (f32[1,64,16,512]{3,2,1,0:T(8,128)S(1)}, f32[1,64,16,512]{3,2,1,0:T(8,128)}, u32[]{:S(2)}) copy-start(f32[1,64,16,512]{3,2,1,0:T(8,128)} %param.9) | copy-start | bytes 6291460
  0.7 14.7 %copy-start.5 = (f32[5]{0:T(128)S(1)}, f32[5]{0:T(128)}, u32[]{:S(2)}) copy-start(f32[5]{0:T(128)} %scale_ref.5) | copy-start | bytes 64
  3.1 10.9 %collective-permute-start = (f32[5,16,512]{2,1,0:T(8,128)S(1)}, f32[5,16,512]{2,1,0:T(8,128)S(1)}, u32[]{:S(2)}, u32[]{:S(2)}) collective-permute-start(f32[5,16,512]{2,1,0:T(8,128)S(1)} %get-tuple-element.34), channel_id=1, source_target_pairs={{0,8},{4,12},{8,0},{12,4},{16,24},{20,28},{24,16},{28,20},{1,9},{5... | collective-permute-start | bytes 491528 | tf_op jit(solution)/shard_map/ppermute | solution.py:326
  6.1 9.2 %collective-permute-start.1 = (f32[5,16,512]{2,1,0:T(8,128)S(1)}, f32[5,16,512]{2,1,0:T(8,128)S(1)}, u32[]{:S(2)}, u32[]{:S(2)}) collective-permute-start(f32[5,16,512]{2,1,0:T(8,128)S(1)} %get-tuple-element.35), channel_id=1, source_target_pairs={{0,16},{4,20},{8,24},{12,28},{16,0},{20,4},{24,8},{28,12},{1,17},{... | collective-permute-start | bytes 491528 | tf_op jit(solution)/shard_map/ppermute | solution.py:326
  7.6 12.4 %copy-start.3 = (s32[1,1,1,8,16]{4,3,2,1,0:T(8,128)S(1)}, s32[1,1,1,8,16]{4,3,2,1,0:T(8,128)}, u32[]{:S(2)}) copy-start(s32[1,1,1,8,16]{4,3,2,1,0:T(8,128)} %param.14) | copy-start | bytes 1540
  7.6 12.4 %copy-start.4 = (f32[1,1,1,8,16]{4,3,2,1,0:T(8,128)S(1)}, f32[1,1,1,8,16]{4,3,2,1,0:T(8,128)}, u32[]{:S(2)}) copy-start(f32[1,1,1,8,16]{4,3,2,1,0:T(8,128)} %param.15) | copy-start | bytes 1540
  7.6 12.4 %collective-permute-start.2 = (f32[5,16,512]{2,1,0:T(8,128)S(1)}, f32[5,16,512]{2,1,0:T(8,128)S(1)}, u32[]{:S(2)}, u32[]{:S(2)}) collective-permute-start(f32[5,16,512]{2,1,0:T(8,128)S(1)} %get-tuple-element.36), channel_id=1, source_target_pairs={{0,24},{4,28},{8,16},{12,20},{16,8},{20,12},{24,0},{28,4},{1,25},{... | collective-permute-start | bytes 491528 | tf_op jit(solution)/shard_map/ppermute | solution.py:326
  10.7 11.3 %collective-permute-start.3 = (f32[5,16,512]{2,1,0:T(8,128)S(1)}, f32[5,16,512]{2,1,0:T(8,128)S(1)}, u32[]{:S(2)}, u32[]{:S(2)}) collective-permute-start(f32[5,16,512]{2,1,0:T(8,128)S(1)} %get-tuple-element.37), channel_id=1, source_target_pairs={{0,12},{4,8},{8,4},{12,0},{16,28},{20,24},{24,20},{28,16},{1,13},{... | collective-permute-start | bytes 491528 | tf_op jit(solution)/shard_map/ppermute | solution.py:326
  11.3 10.7 %collective-permute-start.4 = (f32[5,16,512]{2,1,0:T(8,128)S(1)}, f32[5,16,512]{2,1,0:T(8,128)S(1)}, u32[]{:S(2)}, u32[]{:S(2)}) collective-permute-start(f32[5,16,512]{2,1,0:T(8,128)S(1)} %get-tuple-element.38), channel_id=1, source_target_pairs={{0,20},{4,16},{8,28},{12,24},{16,4},{20,0},{24,12},{28,8},{1,21},{... | collective-permute-start | bytes 491528 | tf_op jit(solution)/shard_map/ppermute | solution.py:326
  14.0 8.3 %collective-permute-start.5 = (f32[5,16,512]{2,1,0:T(8,128)S(1)}, f32[5,16,512]{2,1,0:T(8,128)S(1)}, u32[]{:S(2)}, u32[]{:S(2)}) collective-permute-start(f32[5,16,512]{2,1,0:T(8,128)S(1)} %get-tuple-element.39), channel_id=1, source_target_pairs={{0,28},{4,24},{8,20},{12,16},{16,12},{20,8},{24,4},{28,0},{1,29},{... | collective-permute-start | bytes 491528 | tf_op jit(solution)/shard_map/ppermute | solution.py:326
  15.3 6.9 %collective-permute-start.6 = (f32[5,16,512]{2,1,0:T(8,128)S(1)}, f32[5,16,512]{2,1,0:T(8,128)S(1)}, u32[]{:S(2)}, u32[]{:S(2)}) collective-permute-start(f32[5,16,512]{2,1,0:T(8,128)S(1)} %get-tuple-element.40), channel_id=1, source_target_pairs={{0,4},{4,0},{8,12},{12,8},{16,20},{20,16},{24,28},{28,24},{1,5},{5... | collective-permute-start | bytes 491528 | tf_op jit(solution)/shard_map/ppermute | solution.py:326
  22.0 14.2 %copy-start.6 = (f32[5]{0:T(128)S(1)}, f32[5]{0:T(128)}, u32[]{:S(2)}) copy-start(f32[5]{0:T(128)} %span_ref.3) | copy-start | bytes 64
  26.8 18.6 %collective-permute-start.10 = (f32[5,16,512]{2,1,0:T(8,128)S(1)}, f32[5,16,512]{2,1,0:T(8,128)S(1)}, u32[]{:S(2)}, u32[]{:S(2)}) collective-permute-start(f32[5,16,512]{2,1,0:T(8,128)S(1)} %get-tuple-element.61), channel_id=1, source_target_pairs={{0,3},{1,0},{2,1},{3,2},{4,7},{5,4},{6,5},{7,6},{8,11},{9,8},{10,9... | collective-permute-start | bytes 491528 | tf_op jit(solution)/shard_map/ppermute | solution.py:293
  30.6 14.8 %collective-permute-start.9 = (f32[5,16,512]{2,1,0:T(8,128)S(1)}, f32[5,16,512]{2,1,0:T(8,128)S(1)}, u32[]{:S(2)}, u32[]{:S(2)}) collective-permute-start(f32[5,16,512]{2,1,0:T(8,128)S(1)} %get-tuple-element.62), channel_id=1, source_target_pairs={{0,1},{1,2},{2,3},{3,0},{4,5},{5,6},{6,7},{7,4},{8,9},{9,10},{10,1... | collective-permute-start | bytes 491528 | tf_op jit(solution)/shard_map/ppermute | solution.py:293
  30.6 4.4 %collective-permute-start.7 = (f32[5,16,128]{2,1,0:T(8,128)S(1)}, f32[5,16,128]{2,1,0:T(8,128)S(1)}, u32[]{:S(2)}, u32[]{:S(2)}) collective-permute-start(f32[5,16,128]{2,1,0:T(8,128)S(1)} %get-tuple-element.45.tail_ref), channel_id=1, source_target_pairs={{0,4},{4,0},{1,5},{5,1},{2,6},{6,2},{3,7},{7,3},{8,12},{12,8},{9,1... | collective-permute-start | bytes 122888 | tf_op jit(solution)/shard_map/ppermute | solution.py:293
  30.6 23.4 %collective-permute-start.15 = (f32[5,16,512]{2,1,0:T(8,128)S(1)}, f32[5,16,512]{2,1,0:T(8,128)S(1)}, u32[]{:S(2)}, u32[]{:S(2)}) collective-permute-start(f32[5,16,512]{2,1,0:T(8,128)S(1)} %get-tuple-element.51.total_ref), channel_id=1, source_target_pairs={{0,2},{1,3},{2,0},{3,1},{4,6},{5,7},{6,4},{7,5},{8,10},{9,11},{10,... | collective-permute-start | bytes 491528 | tf_op jit(solution)/shard_map/ppermute | solution.py:293
  31.7 25.6 %collective-permute-start.14 = (f32[5,16,512]{2,1,0:T(8,128)S(1)}, f32[5,16,512]{2,1,0:T(8,128)S(1)}, u32[]{:S(2)}, u32[]{:S(2)}) collective-permute-start(f32[5,16,512]{2,1,0:T(8,128)S(1)} %get-tuple-element.51.total_ref), channel_id=1, source_target_pairs={{0,1},{1,2},{2,3},{3,0},{4,5},{5,6},{6,7},{7,4},{8,9},{9,10},{10,1... | collective-permute-start | bytes 491528 | tf_op jit(solution)/shard_map/ppermute | solution.py:293
  35.0 1.2 %collective-permute-start.8 = (f32[5,16,128]{2,1,0:T(8,128)S(1)}, f32[5,16,128]{2,1,0:T(8,128)S(1)}, u32[]{:S(2)}, u32[]{:S(2)}) collective-permute-start(f32[5,16,128]{2,1,0:T(8,128)S(1)} %get-tuple-element.46.head_ref), channel_id=1, source_target_pairs={{0,4},{4,0},{1,5},{5,1},{2,6},{6,2},{3,7},{7,3},{8,12},{12,8},{9,1... | collective-permute-start | bytes 122888 | tf_op jit(solution)/shard_map/ppermute | solution.py:293
  45.5 12.1 %collective-permute-start.13 = (f32[3,16,512]{2,1,0:T(8,128)S(1)}, f32[3,16,512]{2,1,0:T(8,128)S(1)}, u32[]{:S(2)}, u32[]{:S(2)}) collective-permute-start(f32[3,16,512]{2,1,0:T(8,128)S(1)} %get-tuple-element.59), channel_id=1, source_target_pairs={{0,3},{1,0},{2,1},{3,2},{4,7},{5,4},{6,5},{7,6},{8,11},{9,8},{10,9... | collective-permute-start | bytes 294920 | tf_op jit(solution)/shard_map/ppermute | solution.py:293
  46.2 12.8 %collective-permute-start.12 = (f32[3,16,512]{2,1,0:T(8,128)S(1)}, f32[3,16,512]{2,1,0:T(8,128)S(1)}, u32[]{:S(2)}, u32[]{:S(2)}) collective-permute-start(f32[3,16,512]{2,1,0:T(8,128)S(1)} %get-tuple-element.59), channel_id=1, source_target_pairs={{0,2},{1,3},{2,0},{3,1},{4,6},{5,7},{6,4},{7,5},{8,10},{9,11},{10,... | collective-permute-start | bytes 294920 | tf_op jit(solution)/shard_map/ppermute | solution.py:293
  47.0 12.0 %collective-permute-start.11 = (f32[3,16,512]{2,1,0:T(8,128)S(1)}, f32[3,16,512]{2,1,0:T(8,128)S(1)}, u32[]{:S(2)}, u32[]{:S(2)}) collective-permute-start(f32[3,16,512]{2,1,0:T(8,128)S(1)} %get-tuple-element.59), channel_id=1, source_target_pairs={{0,1},{1,2},{2,3},{3,0},{4,5},{5,6},{6,7},{7,4},{8,9},{9,10},{10,1... | collective-permute-start | bytes 294920 | tf_op jit(solution)/shard_map/ppermute | solution.py:293
  54.0 7.8 %collective-permute-start.18 = (f32[2,16,512]{2,1,0:T(8,128)S(1)}, f32[2,16,512]{2,1,0:T(8,128)S(1)}, u32[]{:S(2)}, u32[]{:S(2)}) collective-permute-start(f32[2,16,512]{2,1,0:T(8,128)S(1)} %get-tuple-element.60), channel_id=1, source_target_pairs={{0,3},{1,0},{2,1},{3,2},{4,7},{5,4},{6,5},{7,6},{8,11},{9,8},{10,9... | collective-permute-start | bytes 196616 | tf_op jit(solution)/shard_map/ppermute | solution.py:293
  57.3 6.6 %collective-permute-start.17 = (f32[2,16,512]{2,1,0:T(8,128)S(1)}, f32[2,16,512]{2,1,0:T(8,128)S(1)}, u32[]{:S(2)}, u32[]{:S(2)}) collective-permute-start(f32[2,16,512]{2,1,0:T(8,128)S(1)} %get-tuple-element.60), channel_id=1, source_target_pairs={{0,2},{1,3},{2,0},{3,1},{4,6},{5,7},{6,4},{7,5},{8,10},{9,11},{10,... | collective-permute-start | bytes 196616 | tf_op jit(solution)/shard_map/ppermute | solution.py:293
  57.6 6.3 %collective-permute-start.16 = (f32[2,16,512]{2,1,0:T(8,128)S(1)}, f32[2,16,512]{2,1,0:T(8,128)S(1)}, u32[]{:S(2)}, u32[]{:S(2)}) collective-permute-start(f32[2,16,512]{2,1,0:T(8,128)S(1)} %get-tuple-element.60), channel_id=1, source_target_pairs={{0,1},{1,2},{2,3},{3,0},{4,5},{5,6},{6,7},{7,4},{8,9},{9,10},{10,1... | collective-permute-start | bytes 196616 | tf_op jit(solution)/shard_map/ppermute | solution.py:293
  (2 other events, 13.1 us)
where the time goes:
time: 66.3 us; the launch traced here: 66 us
  Pallas kernels  36.9 us (56%)
  starting transfers between devices  23.1 us (35%)
  waiting for transfers between devices  4.99 us (8%)
  local copies, waits for them, and re-layouts  0.73 us (1%)
    pallas_call x2, Pallas kernels, on_device(): call(functools.partial(scan_kernel, lowest), (SMEM, SMEM) + (VMEM,) * 7,...  15.5 us
    ppermute x12, starting transfers between devices, moved(): lax.ppermute(value, axis, [(i, (i + distance) % count) for i in range(cou...  15.3 us
    ppermute x7, starting transfers between devices, on_device(): arrived[turn] = lax.ppermute(tiles, RING, route) if turn else tiles  7.85 us
    pallas_call x2, Pallas kernels, on_device(): call(functools.partial(gather_kernel, turns), (SMEM, HBM), (VMEM,) * len(...  5.41 us
    pallas_call x2, Pallas kernels, on_device(): call(functools.partial(combine_kernel, lowest, len(begun)), (VMEM,) * 4 +...  4.83 us
    pallas_call x1, Pallas kernels, on_device(): call(growth_kernel, (SMEM, HBM, HBM), (VMEM,) * 6, [hold(state), hold(spe...  4.68 us
    pallas_call x1, Pallas kernels, on_device(): call(functools.partial(last_fill_kernel, late, 0), (SMEM,) * 3 + (VMEM,)...  4.49 us
    ppermute x12, waiting for transfers between devices, moved(): lax.ppermute(value, axis, [(i, (i + distance) % count) for i in range(cou...  3.4 us
  transfers between devices with their start and end apart: 19, of which 4 were waited for; matrix products, arithmetic and copies ran while one was open for 0% of the time, Pallas kernels for 42%

commit v1 on v0

--- a/solution.py
+++ b/solution.py
@@ -53,29 +53,20 @@
     rows_y = flow_ref.shape[2]
     place = lax.axis_index(RING)
 
-    def copy_of(out_ref, turn, slot):
-        tile = send_ref[place ^ turn, slot]
-        return pltpu.make_async_copy(
-            flow_ref.at[tile // rows_y, :, pl.ds(tile % rows_y, 1), :],
-            out_ref.at[:, pl.ds(slot, 1), :],
-            sem,
-        )
-
-    for out_ref, turn in zip(out_refs, turns):
-
-        @pl.loop(0, capacity)
-        def _(slot):
-            copy_of(out_ref, turn, slot).start()
-
-    for out_ref, turn in zip(out_refs, turns):
-
-        @pl.loop(0, capacity)
-        def _(slot):
-            copy_of(out_ref, turn, slot).wait()
-
-
-def growth_kernel(scale_ref, flow_hbm, speed_hbm, flow_ref, speed_ref, ratio_ref, growth_ref, total_ref, last_ref, sem):
-    width_x, components, rows_y, width_z = growth_ref.shape
+    for k, (out_ref, turn) in enumerate(zip(out_refs, turns)):
+        for slot in range(capacity):
+            tile = send_ref[place ^ turn, slot]
+            pltpu.make_async_copy(
+                flow_ref.at[tile // rows_y, :, pl.ds(tile % rows_y, 1), :],
+                out_ref.at[:, slot : slot + 1, :],
+                sem.at[k],
+            ).start()
+    for k, out_ref in enumerate(out_refs):
+        pltpu.make_async_copy(out_ref, out_ref, sem.at[k]).wait()
+
+
+def growth_kernel(scale_ref, flow_hbm, speed_hbm, flow_ref, speed_ref, ratio_ref, total_ref, last_ref, sem):
+    width_x, components, rows_y, width_z = ratio_ref.shape
     speed_copy = pltpu.make_async_copy(speed_hbm, speed_ref, sem.at[0])
     flow_copy = pltpu.make_async_copy(flow_hbm, flow_ref, sem.at[1])
     speed_copy.start()
@@ -89,23 +80,25 @@
         y = pl.ds(pl.multiple_of((group % halves) * SUB, SUB), SUB)
         scale = 100.0 * scale_ref[v]
 
-        def step(x, run):
-            rate = scale * speed_ref[x, y, :]
-            ratio = 1.0 / (1.0 + rate)
-            grown = ratio * run
-            ratio_ref[x, v, y, :] = ratio
-            growth_ref[x, v, y, :] = grown
-            return rate * grown
-
-        total_ref[v, y, :] = lax.fori_loop(0, width_x, step, jnp.ones((SUB, width_z), F32), unroll=4)
-        last_ref[v, y, :] = scale * speed_ref[width_x - 1, y, :] * ratio_ref[width_x - 1, v, y, :]
+        def step(k, run):
+            speeds = [speed_ref[k * STEPS + i, y, :] for i in range(STEPS)]
+            ratios = [1.0 / (1.0 + scale * speed) for speed in speeds]
+            for ratio in ratios:
+                run = run - ratio * run
+            for i in range(STEPS):
+                ratio_ref[k * STEPS + i, v, y, :] = ratios[i]
+            return run
+
+        start = jnp.ones((SUB, width_z), F32)
+        total_ref[v, y, :] = lax.fori_loop(0, width_x // STEPS, step, start)
+        last_ref[v, y, :] = 1.0 - ratio_ref[width_x - 1, v, y, :]
 
     flow_copy.wait()
 
 
-def fill_kernel(turns, extra, tile_ref, live_ref, weight_ref, flow_ref, *refs):
+def fill_kernel(turns, tile_ref, live_ref, weight_ref, flow_ref, *refs):
     arrived_refs = refs[: len(turns)]
-    filled_ref = refs[len(turns) + extra]
+    filled_ref = refs[len(turns)]
     rows_y = filled_ref.shape[2]
     components, capacity, _ = arrived_refs[0].shape
     place = lax.axis_index(RING)
@@ -113,25 +106,37 @@
     for turn, arrived_ref in zip(turns, arrived_refs):
         peer = place ^ turn
 
-        @pl.loop(0, capacity)
-        def _(slot):
-            @pl.when(live_ref[peer, slot] == 1)
-            def _():
-                tile = tile_ref[peer, slot]
-                weight = weight_ref[peer, slot]
-                x = tile // rows_y
-                y = pl.ds(tile % rows_y, 1)
-                for v in range(components):
-                    old = filled_ref[x, v, y, :]
-                    new = arrived_ref[v, pl.ds(slot, 1), :]
-                    filled_ref[x, v, y, :] = (1.0 - weight) * old + weight * new
-
-
-def last_fill_kernel(turns, extra, *refs):
-    *fill_refs, rows_ref, tail_ref, head_ref = refs
-    fill_kernel(turns, extra, *fill_refs)
+        count = live_ref[peer, 0]
+        for slot in range(1, capacity):
+            count = count + live_ref[peer, slot]
+
+        @pl.loop(0, (count + 1) // 2)
+        def _(pair):
+            slots = [2 * pair, 2 * pair + 1]
+            tiles = [tile_ref[peer, slot] for slot in slots]
+            spots = [(tile // rows_y, pl.ds(tile % rows_y, 1)) for tile in tiles]
+            weights = [
+                jnp.where(live_ref[peer, slot] == 1, weight_ref[peer, slot], 0.0) for slot in slots
+            ]
+            mixed = [
+                (1.0 - weight) * filled_ref[x, v, y, :] + weight * arrived_ref[v, pl.ds(slot, 1), :]
+                for v in range(components)
+                for slot, (x, y), weight in zip(slots, spots, weights)
+            ]
+            for v in range(components):
+                for i, (x, y) in enumerate(spots):
+                    filled_ref[x, v, y, :] = mixed[2 * v + i]
+
+
+def last_fill_kernel(turns, total_ref, *refs):
+    *fill_refs, rows_ref, up_ref, down_ref, tail_ref, head_ref = refs
+    fill_kernel(turns, *fill_refs)
     filled_ref = fill_refs[-1]
     width_x, components, rows_y, width_z = filled_ref.shape
+    up_ref[0] = filled_ref[width_x - 1]
+    up_ref[1] = total_ref[...]
+    down_ref[0] = filled_ref[0]
+    down_ref[1] = total_ref[...]
     lane = lax.broadcasted_iota(jnp.int32, (rows_y, LANES), 1)
     for v in range(components):
 
@@ -228,35 +233,30 @@
 
 
 def edge_kernel(
-    lowest, flux_ref, total_ref, last_ref, rows_ref, behind_ref, ahead_ref, flux_out, first_out, last_out
+    lowest, flux_ref, total_ref, last_ref, rows_ref, behind_ref, ahead_ref,
+    flux_out, beyond_out, first_out, last_out,
 ):
     part = pl.ds(lowest, flux_ref.shape[0])
-    behind = present(behind_ref.at[part], "stream", 1)
-    ahead = present(ahead_ref.at[part], "stream", -1)
+    behind = present(behind_ref.at[0, part], "stream", 1)
+    ahead = present(ahead_ref.at[0, part], "stream", -1)
     row = [rows_ref[k, part] for k in range(4)]
     slope_first = limited(0.5 * (row[0] - behind), 0.5 * (row[1] - row[0]))
     slope_last = limited(0.5 * (row[3] - row[2]), 0.5 * (ahead - row[3]))
     kept = last_ref[part] * slope_last
-    flux_out[...] = flux_ref[...] + total_ref[part] * slope_first + kept
+    flux = flux_ref[...] + total_ref[part] * slope_first + kept
+    flux_out[...] = flux
+    beyond_out[...] = ahead_ref[1, part] * flux
     first_out[...] = slope_first
     last_out[...] = kept
 
 
-def combine_kernel(lowest, begun, local_ref, growth_ref, first_ref, last_ref, *refs):
-    *line_refs, out_hbm, done_ref, inflow_ref, sem = refs[begun:]
+def combine_kernel(lowest, begun, local_ref, ratio_ref, first_ref, last_ref, behind_ref, *refs):
+    *flux_refs, out_hbm, done_ref, inflow_ref, sem = refs[begun:]
     width_x, _, _, _ = local_ref.shape
     components = first_ref.shape[0]
-    count = (len(line_refs) + 1) // 2
-    flux_refs, total_refs = line_refs[:count], line_refs[count:]
-    inflow = first_ref[...]
-    product = None
-    for distance in range(1, count + 1):
-        flux = present(flux_refs[distance - 1], "stream", distance)
-        inflow = inflow + (flux if product is None else product * flux)
-        if distance < count:
-            total = total_refs[distance - 1][pl.ds(lowest, components)]
-            product = total if product is None else product * total
-    inflow_ref[...] = inflow
+    flux = [present(ref, "stream", i + 1) for i, ref in enumerate(flux_refs)]
+    beyond = sum(flux[2:], flux[1]) if len(flux) > 1 else 0.0
+    inflow_ref[...] = first_ref[...] + flux[0] + behind_ref[1, pl.ds(lowest, components)] * beyond
     part = 4
 
     def copy_of(k):
@@ -269,9 +269,14 @@
     def _(k):
         for v in range(components):
             inflow = inflow_ref[v]
+            outs = []
             for i in range(part):
-                x = k * part + i
-                done_ref[x, v] = local_ref[x, lowest + v] + growth_ref[x, lowest + v] * inflow
+                gain = ratio_ref[k * part + i, lowest + v] * inflow
+                outs.append(local_ref[k * part + i, lowest + v] + gain)
+                inflow = inflow - gain
+            for i in range(part):
+                done_ref[k * part + i, v] = outs[i]
+            inflow_ref[v] = inflow
 
         @pl.when(k == 0)
         def _():
@@ -318,38 +323,38 @@
             functools.partial(gather_kernel, turns),
             (SMEM, HBM), (VMEM,) * len(turns),
             [jax.ShapeDtypeStruct((components, capacity, width_z), F32)] * len(turns),
-            [pltpu.SemaphoreType.DMA],
+            [pltpu.SemaphoreType.DMA((len(turns),))],
             micros=2,
         )(send, flow)
         for turn, tiles in zip(turns, outgoing):
             route = [(i, i ^ turn) for i in range(peers)]
             arrived[turn] = lax.ppermute(tiles, RING, route) if turn else tiles
-    flow_in, speed_in, ratio, growth, total, last = call(
+    flow_in, speed_in, ratio, total, last = call(
         growth_kernel,
-        (SMEM, HBM, HBM), (VMEM,) * 6,
-        [hold(state), hold(speed.shape), hold(state), hold(state), hold(line), hold(line)],
+        (SMEM, HBM, HBM), (VMEM,) * 5,
+        [hold(state), hold(speed.shape), hold(state), hold(line), hold(line)],
         [pltpu.SemaphoreType.DMA((2,))],
         micros=6,
     )(char_scale, flow, speed)
-    totals = [moved(total, "stream", d) for d in range(1, sections - 1)]
     (partly,) = call(
-        functools.partial(fill_kernel, early, 0),
+        functools.partial(fill_kernel, early),
         (SMEM,) * 3 + (VMEM,) * (1 + len(early)), (VMEM,),
         [hold(state)],
         aliases={3: 0},
         micros=2,
     )(tile, live, weight, flow_in, *(arrived[turn] for turn in early))
-    filled, rows, tail, head = call(
-        functools.partial(last_fill_kernel, late, 0),
-        (SMEM,) * 3 + (VMEM,) * (1 + len(late)), (VMEM,) * 4,
-        [hold(state), hold((4, *line)), hold(edge), hold(edge)],
-        aliases={3: 0},
+    filled, rows, up, down, tail, head = call(
+        functools.partial(last_fill_kernel, late),
+        (VMEM,) + (SMEM,) * 3 + (VMEM,) * (1 + len(late)), (VMEM,) * 6,
+        [hold(state), hold((4, *line)), hold((2, *line)), hold((2, *line)), hold(edge), hold(edge)],
+        aliases={4: 0},
         micros=4,
-    )(tile, live, weight, partly, *(arrived[turn] for turn in late))
+    )(total, tile, live, weight, partly, *(arrived[turn] for turn in late))
+    behind = moved(up, "stream", 1)
+    ahead = moved(down, "stream", -1)
     before = moved(tail, "span", 1)
     after = moved(head, "span", -1)
-    behind = moved(rows[3], "stream", 1)
-    ahead = moved(rows[0], "stream", -1)
+    assert sections <= 4
     split = (components + 1) // 2
     state_now, parts = filled, []
     for lowest, size in ((0, split), (split, components - split)):
@@ -362,28 +367,28 @@
             aliases={2: 0},
             micros=3 * size,
         )(char_scale, span_ratio, state_now, ratio, speed_in, tail, head, before, after)
-        flux, first_slope, last_slope = call(
+        flux, beyond, first_slope, last_slope = call(
             functools.partial(edge_kernel, lowest),
-            (VMEM,) * 6, (VMEM,) * 3,
-            [jax.ShapeDtypeStruct(some, F32)] * 3,
+            (VMEM,) * 6, (VMEM,) * 4,
+            [jax.ShapeDtypeStruct(some, F32)] * 4,
         )(flux, total, last, rows, behind, ahead)
-        fluxes = [moved(flux, "stream", d) for d in range(1, sections)]
+        fluxes = [moved(flux if d < 3 else beyond, "stream", d) for d in range(1, sections)]
         parts.append((lowest, some, first_slope, last_slope, fluxes))
     begun = ()
     for lowest, some, first_slope, last_slope, fluxes in parts:
         begun = call(
             functools.partial(combine_kernel, lowest, len(begun)),
-            (VMEM,) * 4 + (HBM,) * len(begun) + (VMEM,) * (2 * sections - 3), (HBM,),
+            (VMEM,) * 5 + (HBM,) * len(begun) + (VMEM,) * (sections - 1), (HBM,),
             [jax.ShapeDtypeStruct(state, F32)],
             [
                 pltpu.VMEM((width_x, *some), F32),
                 pltpu.VMEM(some, F32),
                 pltpu.SemaphoreType.DMA,
             ],
-            aliases={4: 0} if begun else None,
+            aliases={5: 0} if begun else None,
             limit=10 << 20,
             micros=some[0],
-        )(state_now, growth, first_slope, last_slope, *begun, *fluxes, *totals)
+        )(state_now, ratio, first_slope, last_slope, behind, *begun, *fluxes)
     (done,) = begun
     return jnp.transpose(done, (0, 2, 1, 3))[None]
 

time: 66.3 us -> 65.9 us (level)
  waiting for transfers between devices: 4.99 us -> 10.5 us
  starting transfers between devices: 23.1 us -> 19.5 us
  Pallas kernels: 36.9 us -> 34.7 us
    ppermute x12 -> x10, waiting for transfers between devices: 3.4 us -> 8.31 us  [moved(): lax.ppermute(value, axis, [(i, (i + distance) % count) for i in range(cou...]
    ppermute x12 -> x10, starting transfers between devices: 15.3 us -> 11.7 us  [moved(): lax.ppermute(value, axis, [(i, (i + distance) % count) for i in range(cou...]
    pallas_call x7, Pallas kernels: 16.1 us -> 14.6 us  [the longest x2 4.82 us: on_device(): call(functools.partial(combine_kernel, lowest, len(begun)), (VMEM,) * 5 +...]
    pallas_call x2, Pallas kernels: 5.41 us -> 4.6 us  [on_device(): call(functools.partial(gather_kernel, turns), (SMEM, HBM), (VMEM,) * len(...]
  transfers between devices with their start and end apart: 19 -> 17, of which waited for: 4 -> 7; matrix products, arithmetic and copies ran while one was open for 0% -> 0% of each run, Pallas kernels for 42% -> 41%
where the time goes in v1:
time: 65.9 us; the launch traced here: 65.6 us
  Pallas kernels  34.7 us (53%)
  starting transfers between devices  19.5 us (30%)
  waiting for transfers between devices  10.5 us (16%)
  local copies, waits for them, and re-layouts  0.71 us (1%)
    pallas_call x2, Pallas kernels, on_device(): call(functools.partial(scan_kernel, lowest), (SMEM, SMEM) + (VMEM,) * 7,...  15.5 us
    ppermute x10, starting transfers between devices, moved(): lax.ppermute(value, axis, [(i, (i + distance) % count) for i in range(cou...  11.7 us
    ppermute x10, waiting for transfers between devices, moved(): lax.ppermute(value, axis, [(i, (i + distance) % count) for i in range(cou...  8.31 us
    ppermute x7, starting transfers between devices, on_device(): arrived[turn] = lax.ppermute(tiles, RING, route) if turn else tiles  7.85 us
    pallas_call x2, Pallas kernels, on_device(): call(functools.partial(combine_kernel, lowest, len(begun)), (VMEM,) * 5 +...  4.82 us
    pallas_call x1, Pallas kernels, on_device(): call(growth_kernel, (SMEM, HBM, HBM), (VMEM,) * 5, [hold(state), hold(spe...  4.68 us
    pallas_call x2, Pallas kernels, on_device(): call(functools.partial(gather_kernel, turns), (SMEM, HBM), (VMEM,) * len(...  4.6 us
    pallas_call x1, Pallas kernels, on_device(): call(functools.partial(last_fill_kernel, late), (VMEM,) + (SMEM,) * 3 + (...  3.57 us
  transfers between devices with their start and end apart: 17, of which 7 were waited for; matrix products, arithmetic and copies ran while one was open for 0% of the time, Pallas kernels for 41%

profile of v1, /device:TPU:0, one launch (start us, length us, event | category | flops | bytes accessed | tf_op | source)
XLA Modules:
  0.0 65.6 jit_solution(9505230374175837595)
XLA Ops:
  0.0 0.7 %copy-done.1 = s32[1,1,1,8,16]{4,3,2,1,0:T(8,128)S(1)} copy-done((s32[1,1,1,8,16]{4,3,2,1,0:T(8,128)S(1)}, s32[1,1,1,8,16]{4,3,2,1,0:T(8,128)}, u32[]{:S(2)}) %copy-start.1) | copy-done | bytes 536
  0.7 2.1 %shard_map.83 = (f32[5,16,512]{2,1,0:T(8,128)S(1)}, f32[5,16,512]{2,1,0:T(8,128)S(1)}, f32[5,16,512]{2,1,0:T(8,128)S(1)}) custom-call(s32[8,16]{1,0:T(8,128)S(1)} %bitcast.12, f32[64,5,16,512]{3,2,1,0:T(8,128)} %bitcast.20), custom_call_target="tpu_custom_call" | custom-call | bytes 6000000 | tf_op jit(solution)/shard_map/pallas_call | solution.py:322
  2.8 3.0 %collective-permute-start = (f32[5,16,512]{2,1,0:T(8,128)S(1)}, f32[5,16,512]{2,1,0:T(8,128)S(1)}, u32[]{:S(2)}, u32[]{:S(2)}) collective-permute-start(f32[5,16,512]{2,1,0:T(8,128)S(1)} %get-tuple-element.38), channel_id=1, source_target_pairs={{0,8},{4,12},{8,0},{12,4},{16,24},{20,28},{24,16},{28,20},{1,9},{5... | collective-permute-start | bytes 491528 | tf_op jit(solution)/shard_map/ppermute | solution.py:331
  5.8 1.5 %collective-permute-start.1 = (f32[5,16,512]{2,1,0:T(8,128)S(1)}, f32[5,16,512]{2,1,0:T(8,128)S(1)}, u32[]{:S(2)}, u32[]{:S(2)}) collective-permute-start(f32[5,16,512]{2,1,0:T(8,128)S(1)} %get-tuple-element.39), channel_id=1, source_target_pairs={{0,16},{4,20},{8,24},{12,28},{16,0},{20,4},{24,8},{28,12},{1,17},{... | collective-permute-start | bytes 491528 | tf_op jit(solution)/shard_map/ppermute | solution.py:331
  7.4 2.5 %shard_map.85 = (f32[5,16,512]{2,1,0:T(8,128)S(1)}, f32[5,16,512]{2,1,0:T(8,128)S(1)}, f32[5,16,512]{2,1,0:T(8,128)S(1)}, f32[5,16,512]{2,1,0:T(8,128)S(1)}, f32[5,16,512]{2,1,0:T(8,128)S(1)}) custom-call(s32[8,16]{1,0:T(8,128)S(1)} %bitcast.13, f32[64,5,16,512]{3,2,1,0:T(8,128)} %bitcast.21), custom_call_target="tpu_custom_call" | custom-call | bytes 6000000 | tf_op jit(solution)/shard_map/pallas_call | solution.py:322
  10.5 2.6 %collective-permute-start.4 = (f32[5,16,512]{2,1,0:T(8,128)S(1)}, f32[5,16,512]{2,1,0:T(8,128)S(1)}, u32[]{:S(2)}, u32[]{:S(2)}) collective-permute-start(f32[5,16,512]{2,1,0:T(8,128)S(1)} %get-tuple-element.42), channel_id=1, source_target_pairs={{0,20},{4,16},{8,28},{12,24},{16,4},{20,0},{24,12},{28,8},{1,21},{... | collective-permute-start | bytes 491528 | tf_op jit(solution)/shard_map/ppermute | solution.py:331
  13.2 2.0 %collective-permute-done.1.refs_1_ = f32[5,16,512]{2,1,0:T(8,128)S(1)} collective-permute-done((f32[5,16,512]{2,1,0:T(8,128)S(1)}, f32[5,16,512]{2,1,0:T(8,128)S(1)}, u32[]{:S(2)}, u32[]{:S(2)}) %collective-permute-start.1) | collective-permute-done | bytes 163872 | tf_op jit(solution)/shard_map/ppermute | solution.py:331
  15.2 4.7 %shard_map.82 = (f32[64,5,16,512]{3,2,1,0:T(8,128)S(1)}, f32[64,16,512]{2,1,0:T(8,128)S(1)}, f32[64,5,16,512]{3,2,1,0:T(8,128)S(1)}, f32[5,16,512]{2,1,0:T(8,128)S(1)}, f32[5,16,512]{2,1,0:T(8,128)S(1)}) custom-call(f32[5]{0:T(128)S(1)} %copy-done.5, f32[64,5,16,512]{3,2,1,0:T(8,128)} %bitcast.22, f32[64,16,512]{2,1,0:T(8,128)S(1)} %bitcast.11), custom_call_target="tpu_custom_call" | custom-call | bytes 18000000 | tf_op jit(solution)/shard_map/pallas_call | solution.py:332
  19.9 1.4 %shard_map.84.refs_3_ = f32[64,5,16,512]{3,2,1,0:T(8,128)S(1)} custom-call(s32[8,16]{1,0:T(8,128)S(1)} %bitcast.14, s32[8,16]{1,0:T(8,128)S(1)} %bitcast.16, f32[8,16]{1,0:T(8,128)S(1)} %bitcast.18, f32[64,5,16,512]{3,2,1,0:T(8,128)S(1)} %get-tuple-element.37.flow_ref, ...), custom_call_target="tpu_custom_call", output_to_operand_aliasing={{}: (3, {})} | custom-call | bytes 6000000 | tf_op jit(solution)/shard_map/pallas_call | solution.py:339
  21.5 3.6 %shard_map.86 = (f32[64,5,16,512]{3,2,1,0:T(8,128)S(1)}, f32[4,5,16,512]{3,2,1,0:T(8,128)S(1)}, f32[2,5,16,512]{3,2,1,0:T(8,128)S(1)}, f32[2,5,16,512]{3,2,1,0:T...) custom-call(f32[5,16,512]{2,1,0:T(8,128)S(1)} %get-tuple-element.36.total_ref, ...), custom_call_target="tpu_custom_call", output_to_operand_aliasing={{0}: (4, {})} | custom-call | bytes 12000000 | tf_op jit(solution)/shard_map/pallas_call | solution.py:346
  25.1 2.1 %collective-permute-start.9 = (f32[2,5,16,512]{3,2,1,0:T(8,128)S(1)}, f32[2,5,16,512]{3,2,1,0:T(8,128)S(1)}, u32[]{:S(2)}, u32[]{:S(2)}) collective-permute-start(f32[2,5,16,512]{3,2,1,0:T(8,128)S(1)} %get-tuple-element.56), channel_id=1, source_target_pairs={{0,1},{1,2},{2,3},{3,0},{4,5},{5,6},{6,7},{7,4},{8,9},{9,10},{10,1... | collective-permute-start | bytes 983048 | tf_op jit(solution)/shard_map/ppermute | solution.py:298
  27.2 1.7 %collective-permute-start.10 = (f32[2,5,16,512]{3,2,1,0:T(8,128)S(1)}, f32[2,5,16,512]{3,2,1,0:T(8,128)S(1)}, u32[]{:S(2)}, u32[]{:S(2)}) collective-permute-start(f32[2,5,16,512]{3,2,1,0:T(8,128)S(1)} %get-tuple-element.57), channel_id=1, source_target_pairs={{0,3},{1,0},{2,1},{3,2},{4,7},{5,4},{6,5},{7,6},{8,11},{9,8},{10,9... | collective-permute-start | bytes 983048 | tf_op jit(solution)/shard_map/ppermute | solution.py:298
  29.5 0.7 %collective-permute-done.7.before_ref = f32[5,16,128]{2,1,0:T(8,128)S(1)} collective-permute-done((f32[5,16,128]{2,1,0:T(8,128)S(1)}, f32[5,16,128]{2,1,0:T(8,128)S(1)}, u32[]{:S(2)}, u32[]{:S(2)}) %collective-permute-start.7) | collective-permute-done | bytes 40992 | tf_op jit(solution)/shard_map/ppermute | solution.py:298
  30.3 9.2 %shard_map.87 = (f32[64,5,16,512]{3,2,1,0:T(8,128)S(1)}, f32[3,16,512]{2,1,0:T(8,128)S(1)}) custom-call(f32[5]{0:T(128)S(1)} %copy-done.5, f32[5]{0:T(128)S(1)} %copy-done.6, f32[64,5,16,512]{3,2,1,0:T(8,128)S(1)} %get-tuple-element.46.filled_ref, f32[64,5,16,512]{3,2,1,0:T(8,128)S(1)} %get-tuple-element.47.ratio_ref, ...), custom_call_target="tpu_custom_call", output_to_operand_aliasing={{0}: (2, {})} | custom-call | bytes 27000000 | tf_op jit(solution)/shard_map/pallas_call | solution.py:362
  39.5 4.1 %collective-permute-done.10.ahead_ref = f32[2,5,16,512]{3,2,1,0:T(8,128)S(1)} collective-permute-done((f32[2,5,16,512]{3,2,1,0:T(8,128)S(1)}, f32[2,5,16,512]{3,2,1,0:T(8,128)S(1)}, u32[]{:S(2)}, u32[]{:S(2)}) %collective-permute-start.10) | collective-permute-done | bytes 327712 | tf_op jit(solution)/shard_map/ppermute | solution.py:298
  43.7 2.3 %collective-permute-start.13 = (f32[3,16,512]{2,1,0:T(8,128)S(1)}, f32[3,16,512]{2,1,0:T(8,128)S(1)}, u32[]{:S(2)}, u32[]{:S(2)}) collective-permute-start(f32[3,16,512]{2,1,0:T(8,128)S(1)} %get-tuple-element.64), channel_id=1, source_target_pairs={{0,3},{1,0},{2,1},{3,2},{4,7},{5,4},{6,5},{7,6},{8,11},{9,8},{10,9... | collective-permute-start | bytes 294920 | tf_op jit(solution)/shard_map/ppermute | solution.py:298
  46.3 0.9 %collective-permute-start.11 = (f32[3,16,512]{2,1,0:T(8,128)S(1)}, f32[3,16,512]{2,1,0:T(8,128)S(1)}, u32[]{:S(2)}, u32[]{:S(2)}) collective-permute-start(f32[3,16,512]{2,1,0:T(8,128)S(1)} %get-tuple-element.63), channel_id=1, source_target_pairs={{0,1},{1,2},{2,3},{3,0},{4,5},{5,6},{6,7},{7,4},{8,9},{9,10},{10,1... | collective-permute-start | bytes 294920 | tf_op jit(solution)/shard_map/ppermute | solution.py:298
  47.2 6.3 %shard_map.88 = (f32[64,5,16,512]{3,2,1,0:T(8,128)S(1)}, f32[2,16,512]{2,1,0:T(8,128)S(1)}) custom-call(f32[5]{0:T(128)S(1)} %copy-done.5, f32[5]{0:T(128)S(1)} %copy-done.6, f32[64,5,16,512]{3,2,1,0:T(8,128)S(1)} %get-tuple-element.51.filled_ref, f32[64,5,16,512]{3,2,1,0:T(8,128)S(1)} %get-tuple-element.47.ratio_ref, ...), custom_call_target="tpu_custom_call", output_to_operand_aliasing={{0}: (2, {})} | custom-call | bytes 18000000 | tf_op jit(solution)/shard_map/pallas_call | solution.py:362
  53.6 3.0 %collective-permute-start.16 = (f32[2,16,512]{2,1,0:T(8,128)S(1)}, f32[2,16,512]{2,1,0:T(8,128)S(1)}, u32[]{:S(2)}, u32[]{:S(2)}) collective-permute-start(f32[2,16,512]{2,1,0:T(8,128)S(1)} %get-tuple-element.66), channel_id=1, source_target_pairs={{0,3},{1,0},{2,1},{3,2},{4,7},{5,4},{6,5},{7,6},{8,11},{9,8},{10,9... | collective-permute-start | bytes 196616 | tf_op jit(solution)/shard_map/ppermute | solution.py:298
  56.6 0.8 %collective-permute-start.15 = (f32[2,16,512]{2,1,0:T(8,128)S(1)}, f32[2,16,512]{2,1,0:T(8,128)S(1)}, u32[]{:S(2)}, u32[]{:S(2)}) collective-permute-start(f32[2,16,512]{2,1,0:T(8,128)S(1)} %get-tuple-element.65), channel_id=1, source_target_pairs={{0,2},{1,3},{2,0},{3,1},{4,6},{5,7},{6,4},{7,5},{8,10},{9,11},{10,... | collective-permute-start | bytes 196616 | tf_op jit(solution)/shard_map/ppermute | solution.py:298
  57.5 2.8 %shard_map.91.refs_0_ = f32[64,5,16,512]{3,2,1,0:T(8,128)} custom-call(f32[64,5,16,512]{3,2,1,0:T(8,128)S(1)} %get-tuple-element.52.local_ref, f32[64,5,16,512]{3,2,1,0:T(8,128)S(1)} %get-tuple-element.47.ratio_ref, f32[3,16,512]{2,1,0:T(8,128)S(1)} %get-tuple-element.61.first_ref, f32[3,16,512]{2,1,0:T(8,128)S(1)} %get-tuple-element.62.last_ref, ...), custom_call_target="tpu_custom_call" | custom-call | bytes 9000000 | tf_op jit(solution)/shard_map/pallas_call | solution.py:379
  60.2 2.3 %collective-permute-done.15.refs_2_ = f32[2,16,512]{2,1,0:T(8,128)S(1)} collective-permute-done((f32[2,16,512]{2,1,0:T(8,128)S(1)}, f32[2,16,512]{2,1,0:T(8,128)S(1)}, u32[]{:S(2)}, u32[]{:S(2)}) %collective-permute-start.15) | collective-permute-done | bytes 65568 | tf_op jit(solution)/shard_map/ppermute | solution.py:298
  62.5 1.0 %collective-permute-done.14.refs_1_ = f32[2,16,512]{2,1,0:T(8,128)S(1)} collective-permute-done((f32[2,16,512]{2,1,0:T(8,128)S(1)}, f32[2,16,512]{2,1,0:T(8,128)S(1)}, u32[]{:S(2)}, u32[]{:S(2)}) %collective-permute-start.14) | collective-permute-done | bytes 65568 | tf_op jit(solution)/shard_map/ppermute | solution.py:298
  63.5 2.1 %shard_map.92 = f32[64,5,16,512]{3,2,1,0:T(8,128)} custom-call(f32[64,5,16,512]{3,2,1,0:T(8,128)S(1)} %get-tuple-element.52.local_ref, f32[64,5,16,512]{3,2,1,0:T(8,128)S(1)} %get-tuple-element.47.ratio_ref, f32[2,16,512]{2,1,0:T(8,128)S(1)} %get-tuple-element.58.first_ref, ...), custom_call_target="tpu_custom_call", output_to_operand_aliasing={{}: (5, {})} | custom-call | bytes 6000000 | tf_op jit(solution)/shard_map/pallas_call | solution.py:379
  (35 shorter events, 2.0 us)
Async XLA Ops:
  0.0 0.7 %copy-start.1 = (s32[1,1,1,8,16]{4,3,2,1,0:T(8,128)S(1)}, s32[1,1,1,8,16]{4,3,2,1,0:T(8,128)}, u32[]{:S(2)}) copy-start(s32[1,1,1,8,16]{4,3,2,1,0:T(8,128)} %param.12) | copy-start | bytes 1540
  0.7 14.5 %copy-start = (f32[1,64,16,512]{3,2,1,0:T(8,128)S(1)}, f32[1,64,16,512]{3,2,1,0:T(8,128)}, u32[]{:S(2)}) copy-start(f32[1,64,16,512]{3,2,1,0:T(8,128)} %param.9) | copy-start | bytes 6291460
  0.7 14.5 %copy-start.5 = (f32[5]{0:T(128)S(1)}, f32[5]{0:T(128)}, u32[]{:S(2)}) copy-start(f32[5]{0:T(128)} %scale_ref.5) | copy-start | bytes 64
  2.8 10.4 %collective-permute-start = (f32[5,16,512]{2,1,0:T(8,128)S(1)}, f32[5,16,512]{2,1,0:T(8,128)S(1)}, u32[]{:S(2)}, u32[]{:S(2)}) collective-permute-start(f32[5,16,512]{2,1,0:T(8,128)S(1)} %get-tuple-element.38), channel_id=1, source_target_pairs={{0,8},{4,12},{8,0},{12,4},{16,24},{20,28},{24,16},{28,20},{1,9},{5... | collective-permute-start | bytes 491528 | tf_op jit(solution)/shard_map/ppermute | solution.py:331
  5.8 9.4 %collective-permute-start.1 = (f32[5,16,512]{2,1,0:T(8,128)S(1)}, f32[5,16,512]{2,1,0:T(8,128)S(1)}, u32[]{:S(2)}, u32[]{:S(2)}) collective-permute-start(f32[5,16,512]{2,1,0:T(8,128)S(1)} %get-tuple-element.39), channel_id=1, source_target_pairs={{0,16},{4,20},{8,24},{12,28},{16,0},{20,4},{24,8},{28,12},{1,17},{... | collective-permute-start | bytes 491528 | tf_op jit(solution)/shard_map/ppermute | solution.py:331
  7.3 12.6 %copy-start.2 = (s32[1,1,1,8,16]{4,3,2,1,0:T(8,128)S(1)}, s32[1,1,1,8,16]{4,3,2,1,0:T(8,128)}, u32[]{:S(2)}) copy-start(s32[1,1,1,8,16]{4,3,2,1,0:T(8,128)} %param.13) | copy-start | bytes 1540
  7.3 12.6 %copy-start.3 = (s32[1,1,1,8,16]{4,3,2,1,0:T(8,128)S(1)}, s32[1,1,1,8,16]{4,3,2,1,0:T(8,128)}, u32[]{:S(2)}) copy-start(s32[1,1,1,8,16]{4,3,2,1,0:T(8,128)} %param.14) | copy-start | bytes 1540
  7.3 12.6 %copy-start.4 = (f32[1,1,1,8,16]{4,3,2,1,0:T(8,128)S(1)}, f32[1,1,1,8,16]{4,3,2,1,0:T(8,128)}, u32[]{:S(2)}) copy-start(f32[1,1,1,8,16]{4,3,2,1,0:T(8,128)} %param.15) | copy-start | bytes 1540
  7.3 12.6 %collective-permute-start.2 = (f32[5,16,512]{2,1,0:T(8,128)S(1)}, f32[5,16,512]{2,1,0:T(8,128)S(1)}, u32[]{:S(2)}, u32[]{:S(2)}) collective-permute-start(f32[5,16,512]{2,1,0:T(8,128)S(1)} %get-tuple-element.40), channel_id=1, source_target_pairs={{0,24},{4,28},{8,16},{12,20},{16,8},{20,12},{24,0},{28,4},{1,25},{... | collective-permute-start | bytes 491528 | tf_op jit(solution)/shard_map/ppermute | solution.py:331
  9.9 11.4 %collective-permute-start.3 = (f32[5,16,512]{2,1,0:T(8,128)S(1)}, f32[5,16,512]{2,1,0:T(8,128)S(1)}, u32[]{:S(2)}, u32[]{:S(2)}) collective-permute-start(f32[5,16,512]{2,1,0:T(8,128)S(1)} %get-tuple-element.41), channel_id=1, source_target_pairs={{0,12},{4,8},{8,4},{12,0},{16,28},{20,24},{24,20},{28,16},{1,13},{... | collective-permute-start | bytes 491528 | tf_op jit(solution)/shard_map/ppermute | solution.py:331
  10.5 10.8 %collective-permute-start.4 = (f32[5,16,512]{2,1,0:T(8,128)S(1)}, f32[5,16,512]{2,1,0:T(8,128)S(1)}, u32[]{:S(2)}, u32[]{:S(2)}) collective-permute-start(f32[5,16,512]{2,1,0:T(8,128)S(1)} %get-tuple-element.42), channel_id=1, source_target_pairs={{0,20},{4,16},{8,28},{12,24},{16,4},{20,0},{24,12},{28,8},{1,21},{... | collective-permute-start | bytes 491528 | tf_op jit(solution)/shard_map/ppermute | solution.py:331
  13.1 8.3 %collective-permute-start.5 = (f32[5,16,512]{2,1,0:T(8,128)S(1)}, f32[5,16,512]{2,1,0:T(8,128)S(1)}, u32[]{:S(2)}, u32[]{:S(2)}) collective-permute-start(f32[5,16,512]{2,1,0:T(8,128)S(1)} %get-tuple-element.43), channel_id=1, source_target_pairs={{0,28},{4,24},{8,20},{12,16},{16,12},{20,8},{24,4},{28,0},{1,29},{... | collective-permute-start | bytes 491528 | tf_op jit(solution)/shard_map/ppermute | solution.py:331
  15.2 6.3 %collective-permute-start.6 = (f32[5,16,512]{2,1,0:T(8,128)S(1)}, f32[5,16,512]{2,1,0:T(8,128)S(1)}, u32[]{:S(2)}, u32[]{:S(2)}) collective-permute-start(f32[5,16,512]{2,1,0:T(8,128)S(1)} %get-tuple-element.44), channel_id=1, source_target_pairs={{0,4},{4,0},{8,12},{12,8},{16,20},{20,16},{24,28},{28,24},{1,5},{5... | collective-permute-start | bytes 491528 | tf_op jit(solution)/shard_map/ppermute | solution.py:331
  21.3 9.0 %copy-start.6 = (f32[5]{0:T(128)S(1)}, f32[5]{0:T(128)}, u32[]{:S(2)}) copy-start(f32[5]{0:T(128)} %span_ref.3) | copy-start | bytes 64
  25.1 14.4 %collective-permute-start.9 = (f32[2,5,16,512]{3,2,1,0:T(8,128)S(1)}, f32[2,5,16,512]{3,2,1,0:T(8,128)S(1)}, u32[]{:S(2)}, u32[]{:S(2)}) collective-permute-start(f32[2,5,16,512]{3,2,1,0:T(8,128)S(1)} %get-tuple-element.56), channel_id=1, source_target_pairs={{0,1},{1,2},{2,3},{3,0},{4,5},{5,6},{6,7},{7,4},{8,9},{9,10},{10,1... | collective-permute-start | bytes 983048 | tf_op jit(solution)/shard_map/ppermute | solution.py:298
  27.2 16.5 %collective-permute-start.10 = (f32[2,5,16,512]{3,2,1,0:T(8,128)S(1)}, f32[2,5,16,512]{3,2,1,0:T(8,128)S(1)}, u32[]{:S(2)}, u32[]{:S(2)}) collective-permute-start(f32[2,5,16,512]{3,2,1,0:T(8,128)S(1)} %get-tuple-element.57), channel_id=1, source_target_pairs={{0,3},{1,0},{2,1},{3,2},{4,7},{5,4},{6,5},{7,6},{8,11},{9,8},{10,9... | collective-permute-start | bytes 983048 | tf_op jit(solution)/shard_map/ppermute | solution.py:298
  28.9 1.2 %collective-permute-start.7 = (f32[5,16,128]{2,1,0:T(8,128)S(1)}, f32[5,16,128]{2,1,0:T(8,128)S(1)}, u32[]{:S(2)}, u32[]{:S(2)}) collective-permute-start(f32[5,16,128]{2,1,0:T(8,128)S(1)} %get-tuple-element.49.tail_ref), channel_id=1, source_target_pairs={{0,4},{4,0},{1,5},{5,1},{2,6},{6,2},{3,7},{7,3},{8,12},{12,8},{9,1... | collective-permute-start | bytes 122888 | tf_op jit(solution)/shard_map/ppermute | solution.py:298
  29.0 1.3 %collective-permute-start.8 = (f32[5,16,128]{2,1,0:T(8,128)S(1)}, f32[5,16,128]{2,1,0:T(8,128)S(1)}, u32[]{:S(2)}, u32[]{:S(2)}) collective-permute-start(f32[5,16,128]{2,1,0:T(8,128)S(1)} %get-tuple-element.50.head_ref), channel_id=1, source_target_pairs={{0,4},{4,0},{1,5},{5,1},{2,6},{6,2},{3,7},{7,3},{8,12},{12,8},{9,1... | collective-permute-start | bytes 122888 | tf_op jit(solution)/shard_map/ppermute | solution.py:298
  43.7 13.7 %collective-permute-start.13 = (f32[3,16,512]{2,1,0:T(8,128)S(1)}, f32[3,16,512]{2,1,0:T(8,128)S(1)}, u32[]{:S(2)}, u32[]{:S(2)}) collective-permute-start(f32[3,16,512]{2,1,0:T(8,128)S(1)} %get-tuple-element.64), channel_id=1, source_target_pairs={{0,3},{1,0},{2,1},{3,2},{4,7},{5,4},{6,5},{7,6},{8,11},{9,8},{10,9... | collective-permute-start | bytes 294920 | tf_op jit(solution)/shard_map/ppermute | solution.py:298
  46.0 11.4 %collective-permute-start.12 = (f32[3,16,512]{2,1,0:T(8,128)S(1)}, f32[3,16,512]{2,1,0:T(8,128)S(1)}, u32[]{:S(2)}, u32[]{:S(2)}) collective-permute-start(f32[3,16,512]{2,1,0:T(8,128)S(1)} %get-tuple-element.63), channel_id=1, source_target_pairs={{0,2},{1,3},{2,0},{3,1},{4,6},{5,7},{6,4},{7,5},{8,10},{9,11},{10,... | collective-permute-start | bytes 294920 | tf_op jit(solution)/shard_map/ppermute | solution.py:298
  46.3 11.1 %collective-permute-start.11 = (f32[3,16,512]{2,1,0:T(8,128)S(1)}, f32[3,16,512]{2,1,0:T(8,128)S(1)}, u32[]{:S(2)}, u32[]{:S(2)}) collective-permute-start(f32[3,16,512]{2,1,0:T(8,128)S(1)} %get-tuple-element.63), channel_id=1, source_target_pairs={{0,1},{1,2},{2,3},{3,0},{4,5},{5,6},{6,7},{7,4},{8,9},{9,10},{10,1... | collective-permute-start | bytes 294920 | tf_op jit(solution)/shard_map/ppermute | solution.py:298
  53.6 6.6 %collective-permute-start.16 = (f32[2,16,512]{2,1,0:T(8,128)S(1)}, f32[2,16,512]{2,1,0:T(8,128)S(1)}, u32[]{:S(2)}, u32[]{:S(2)}) collective-permute-start(f32[2,16,512]{2,1,0:T(8,128)S(1)} %get-tuple-element.66), channel_id=1, source_target_pairs={{0,3},{1,0},{2,1},{3,2},{4,7},{5,4},{6,5},{7,6},{8,11},{9,8},{10,9... | collective-permute-start | bytes 196616 | tf_op jit(solution)/shard_map/ppermute | solution.py:298
  56.6 5.9 %collective-permute-start.15 = (f32[2,16,512]{2,1,0:T(8,128)S(1)}, f32[2,16,512]{2,1,0:T(8,128)S(1)}, u32[]{:S(2)}, u32[]{:S(2)}) collective-permute-start(f32[2,16,512]{2,1,0:T(8,128)S(1)} %get-tuple-element.65), channel_id=1, source_target_pairs={{0,2},{1,3},{2,0},{3,1},{4,6},{5,7},{6,4},{7,5},{8,10},{9,11},{10,... | collective-permute-start | bytes 196616 | tf_op jit(solution)/shard_map/ppermute | solution.py:298
  57.4 6.1 %collective-permute-start.14 = (f32[2,16,512]{2,1,0:T(8,128)S(1)}, f32[2,16,512]{2,1,0:T(8,128)S(1)}, u32[]{:S(2)}, u32[]{:S(2)}) collective-permute-start(f32[2,16,512]{2,1,0:T(8,128)S(1)} %get-tuple-element.65), channel_id=1, source_target_pairs={{0,1},{1,2},{2,3},{3,0},{4,5},{5,6},{6,7},{7,4},{8,9},{9,10},{10,1... | collective-permute-start | bytes 196616 | tf_op jit(solution)/shard_map/ppermute | solution.py:298

commit v2 on v1

--- a/solution.py
+++ b/solution.py
@@ -41,10 +41,18 @@
     )
 
 
+def inside(axis, distance):
+    source = lax.axis_index(axis) - distance
+    return jnp.where((source >= 0) & (source < lax.axis_size(axis)), 1.0, 0.0)
+
+
 def present(ref, axis, distance):
-    source = lax.axis_index(axis) - distance
-    inside = (source >= 0) & (source < lax.axis_size(axis))
-    return ref[...] * jnp.where(inside, 1.0, 0.0)
+    return ref[...] * inside(axis, distance)
+
+
+def beside(side, even_ref, odd_ref):
+    odd = lax.axis_index("stream") % 2
+    return jnp.where(odd == (1 if side == "behind" else 0), even_ref[...], odd_ref[...])
 
 
 def gather_kernel(turns, send_ref, flow_ref, *refs):
@@ -129,14 +137,15 @@
 
 
 def last_fill_kernel(turns, total_ref, *refs):
-    *fill_refs, rows_ref, up_ref, down_ref, tail_ref, head_ref = refs
+    *fill_refs, rows_ref, even_ref, odd_ref, tail_ref, head_ref = refs
     fill_kernel(turns, *fill_refs)
     filled_ref = fill_refs[-1]
     width_x, components, rows_y, width_z = filled_ref.shape
-    up_ref[0] = filled_ref[width_x - 1]
-    up_ref[1] = total_ref[...]
-    down_ref[0] = filled_ref[0]
-    down_ref[1] = total_ref[...]
+    odd = lax.axis_index("stream") % 2
+    even_ref[0] = filled_ref[(width_x - 1) * (1 - odd)]
+    odd_ref[0] = filled_ref[(width_x - 1) * odd]
+    even_ref[1] = total_ref[...]
+    odd_ref[1] = total_ref[...]
     lane = lax.broadcasted_iota(jnp.int32, (rows_y, LANES), 1)
     for v in range(components):
 
@@ -233,30 +242,31 @@
 
 
 def edge_kernel(
-    lowest, flux_ref, total_ref, last_ref, rows_ref, behind_ref, ahead_ref,
+    lowest, flux_ref, total_ref, last_ref, rows_ref, even_ref, odd_ref,
     flux_out, beyond_out, first_out, last_out,
 ):
     part = pl.ds(lowest, flux_ref.shape[0])
-    behind = present(behind_ref.at[0, part], "stream", 1)
-    ahead = present(ahead_ref.at[0, part], "stream", -1)
+    behind = beside("behind", even_ref.at[0, part], odd_ref.at[0, part]) * inside("stream", 1)
+    ahead = beside("ahead", even_ref.at[0, part], odd_ref.at[0, part]) * inside("stream", -1)
     row = [rows_ref[k, part] for k in range(4)]
     slope_first = limited(0.5 * (row[0] - behind), 0.5 * (row[1] - row[0]))
     slope_last = limited(0.5 * (row[3] - row[2]), 0.5 * (ahead - row[3]))
     kept = last_ref[part] * slope_last
     flux = flux_ref[...] + total_ref[part] * slope_first + kept
     flux_out[...] = flux
-    beyond_out[...] = ahead_ref[1, part] * flux
+    beyond_out[...] = beside("ahead", even_ref.at[1, part], odd_ref.at[1, part]) * flux
     first_out[...] = slope_first
     last_out[...] = kept
 
 
-def combine_kernel(lowest, begun, local_ref, ratio_ref, first_ref, last_ref, behind_ref, *refs):
+def combine_kernel(lowest, begun, local_ref, ratio_ref, first_ref, last_ref, even_ref, odd_ref, *refs):
     *flux_refs, out_hbm, done_ref, inflow_ref, sem = refs[begun:]
     width_x, _, _, _ = local_ref.shape
     components = first_ref.shape[0]
     flux = [present(ref, "stream", i + 1) for i, ref in enumerate(flux_refs)]
     beyond = sum(flux[2:], flux[1]) if len(flux) > 1 else 0.0
-    inflow_ref[...] = first_ref[...] + flux[0] + behind_ref[1, pl.ds(lowest, components)] * beyond
+    behind = beside("behind", *(ref.at[1, pl.ds(lowest, components)] for ref in (even_ref, odd_ref)))
+    inflow_ref[...] = first_ref[...] + flux[0] + behind * beyond
     part = 4
 
     def copy_of(k):
@@ -316,25 +326,27 @@
     assert peers & (peers - 1) == 0
 
     order = sorted(range(1, peers), key=lambda turn: (turn == 1, turn & 1, turn))
-    early, late = order[: peers // 2 - 1], order[peers // 2 - 1 :] + [0]
+    near = peers // 2 - 1
     arrived = {}
-    for turns in (early, late):
+    groups = [order[:1], order[1:near], order[near:] + [0]]
+    for turns in groups:
         outgoing = call(
             functools.partial(gather_kernel, turns),
             (SMEM, HBM), (VMEM,) * len(turns),
             [jax.ShapeDtypeStruct((components, capacity, width_z), F32)] * len(turns),
             [pltpu.SemaphoreType.DMA((len(turns),))],
-            micros=2,
+            micros=1,
         )(send, flow)
         for turn, tiles in zip(turns, outgoing):
             route = [(i, i ^ turn) for i in range(peers)]
             arrived[turn] = lax.ppermute(tiles, RING, route) if turn else tiles
+    early, late = order[:near] + [1, 0], order[near:-1]
     flow_in, speed_in, ratio, total, last = call(
         growth_kernel,
         (SMEM, HBM, HBM), (VMEM,) * 5,
         [hold(state), hold(speed.shape), hold(state), hold(line), hold(line)],
         [pltpu.SemaphoreType.DMA((2,))],
-        micros=6,
+        micros=5,
     )(char_scale, flow, speed)
     (partly,) = call(
         functools.partial(fill_kernel, early),
@@ -343,15 +355,22 @@
         aliases={3: 0},
         micros=2,
     )(tile, live, weight, flow_in, *(arrived[turn] for turn in early))
-    filled, rows, up, down, tail, head = call(
+    filled, rows, even, odd, tail, head = call(
         functools.partial(last_fill_kernel, late),
         (VMEM,) + (SMEM,) * 3 + (VMEM,) * (1 + len(late)), (VMEM,) * 6,
         [hold(state), hold((4, *line)), hold((2, *line)), hold((2, *line)), hold(edge), hold(edge)],
         aliases={4: 0},
         micros=4,
     )(total, tile, live, weight, partly, *(arrived[turn] for turn in late))
-    behind = moved(up, "stream", 1)
-    ahead = moved(down, "stream", -1)
+    pairs = [[i ^ 1 for i in range(sections)], [((i + 1) ^ 1) - 1 for i in range(sections)]]
+    even, odd = (
+        lax.ppermute(
+            message,
+            "stream",
+            [(i, other if 0 <= other < sections else i) for i, other in enumerate(others)],
+        )
+        for message, others in zip((even, odd), pairs)
+    )
     before = moved(tail, "span", 1)
     after = moved(head, "span", -1)
     assert sections <= 4
@@ -371,24 +390,24 @@
             functools.partial(edge_kernel, lowest),
             (VMEM,) * 6, (VMEM,) * 4,
             [jax.ShapeDtypeStruct(some, F32)] * 4,
-        )(flux, total, last, rows, behind, ahead)
+        )(flux, total, last, rows, even, odd)
         fluxes = [moved(flux if d < 3 else beyond, "stream", d) for d in range(1, sections)]
         parts.append((lowest, some, first_slope, last_slope, fluxes))
     begun = ()
     for lowest, some, first_slope, last_slope, fluxes in parts:
         begun = call(
             functools.partial(combine_kernel, lowest, len(begun)),
-            (VMEM,) * 5 + (HBM,) * len(begun) + (VMEM,) * (sections - 1), (HBM,),
+            (VMEM,) * 6 + (HBM,) * len(begun) + (VMEM,) * (sections - 1), (HBM,),
             [jax.ShapeDtypeStruct(state, F32)],
             [
                 pltpu.VMEM((width_x, *some), F32),
                 pltpu.VMEM(some, F32),
                 pltpu.SemaphoreType.DMA,
             ],
-            aliases={5: 0} if begun else None,
+            aliases={6: 0} if begun else None,
             limit=10 << 20,
             micros=some[0],
-        )(state_now, ratio, first_slope, last_slope, behind, *begun, *fluxes)
+        )(state_now, ratio, first_slope, last_slope, even, odd, *begun, *fluxes)
     (done,) = begun
     return jnp.transpose(done, (0, 2, 1, 3))[None]
 

time: 65.9 us -> 64.9 us (0.985)
  waiting for transfers between devices: 10.5 us -> 5.76 us
  starting transfers between devices: 19.5 us -> 21.7 us
  Pallas kernels: 34.7 us -> 36 us
    ppermute x10 -> x8, waiting for transfers between devices: 8.31 us -> 3.8 us  [moved(): lax.ppermute(value, axis, [(i, (i + distance) % count) for i in range(cou...]
    ppermute x0 -> x2, starting transfers between devices: none -> 2.68 us  [on_device(): lax.ppermute(message, 'stream', [(i, other if 0 <= other < sections else...]
    pallas_call x2 -> x3, Pallas kernels: 4.6 us -> 5.97 us  [on_device(): call(functools.partial(gather_kernel, turns), (SMEM, HBM), (VMEM,) * len(...]
    ppermute x10 -> x8, starting transfers between devices: 11.7 us -> 11.1 us  [moved(): lax.ppermute(value, axis, [(i, (i + distance) % count) for i in range(cou...]
  transfers between devices with their start and end apart: 17 -> 17, of which waited for: 7 -> 6; matrix products, arithmetic and copies ran while one was open for 0% -> 0% of each run, Pallas kernels for 41% -> 45%
where the time goes in v2:
time: 64.9 us; the launch traced here: 64.5 us
  Pallas kernels  36 us (55%)
  starting transfers between devices  21.7 us (33%)
  waiting for transfers between devices  5.76 us (9%)
  local copies, waits for them, and re-layouts  0.72 us (1%)
    pallas_call x2, Pallas kernels, on_device(): call(functools.partial(scan_kernel, lowest), (SMEM, SMEM) + (VMEM,) * 7,...  15.5 us
    ppermute x8, starting transfers between devices, moved(): lax.ppermute(value, axis, [(i, (i + distance) % count) for i in range(cou...  11.1 us
    ppermute x7, starting transfers between devices, on_device(): arrived[turn] = lax.ppermute(tiles, RING, route) if turn else tiles  7.96 us
    pallas_call x3, Pallas kernels, on_device(): call(functools.partial(gather_kernel, turns), (SMEM, HBM), (VMEM,) * len(...  5.97 us
    pallas_call x2, Pallas kernels, on_device(): call(functools.partial(combine_kernel, lowest, len(begun)), (VMEM,) * 6 +...  4.81 us
    pallas_call x1, Pallas kernels, on_device(): call(growth_kernel, (SMEM, HBM, HBM), (VMEM,) * 5, [hold(state), hold(spe...  4.68 us
    ppermute x8, waiting for transfers between devices, moved(): lax.ppermute(value, axis, [(i, (i + distance) % count) for i in range(cou...  3.8 us
    pallas_call x1, Pallas kernels, on_device(): call(functools.partial(last_fill_kernel, late), (VMEM,) + (SMEM,) * 3 + (...  3.11 us
  transfers between devices with their start and end apart: 17, of which 6 were waited for; matrix products, arithmetic and copies ran while one was open for 0% of the time, Pallas kernels for 45%

profile of v2, /device:TPU:0, one launch (start us, length us, event | category | flops | bytes accessed | tf_op | source)
XLA Modules:
  0.0 64.5 jit_solution(10456900788796445000)
XLA Ops:
  0.0 0.7 %copy-done.1 = s32[1,1,1,8,16]{4,3,2,1,0:T(8,128)S(1)} copy-done((s32[1,1,1,8,16]{4,3,2,1,0:T(8,128)S(1)}, s32[1,1,1,8,16]{4,3,2,1,0:T(8,128)}, u32[]{:S(2)}) %copy-start.1) | copy-done | bytes 536
  0.7 1.6 %shard_map.83 = f32[5,16,512]{2,1,0:T(8,128)S(1)} custom-call(s32[8,16]{1,0:T(8,128)S(1)} %bitcast.12, f32[64,5,16,512]{3,2,1,0:T(8,128)} %bitcast.21), custom_call_target="tpu_custom_call" | custom-call | bytes 3000000 | tf_op jit(solution)/shard_map/pallas_call | solution.py:333
  2.3 3.0 %collective-permute-start = (f32[5,16,512]{2,1,0:T(8,128)S(1)}, f32[5,16,512]{2,1,0:T(8,128)S(1)}, u32[]{:S(2)}, u32[]{:S(2)}) collective-permute-start(f32[5,16,512]{2,1,0:T(8,128)S(1)} %shard_map.83), channel_id=1, source_target_pairs={{0,8},{4,12},{8,0},{12,4},{16,24},{20,28},{24,16},{28,20},{1,9},{5... | collective-permute-start | bytes 491528 | tf_op jit(solution)/shard_map/ppermute | solution.py:342
  5.3 1.9 %shard_map.84 = (f32[5,16,512]{2,1,0:T(8,128)S(1)}, f32[5,16,512]{2,1,0:T(8,128)S(1)}) custom-call(s32[8,16]{1,0:T(8,128)S(1)} %bitcast.13, f32[64,5,16,512]{3,2,1,0:T(8,128)} %bitcast.22), custom_call_target="tpu_custom_call" | custom-call | bytes 3000000 | tf_op jit(solution)/shard_map/pallas_call | solution.py:333
  7.2 1.6 %collective-permute-start.1 = (f32[5,16,512]{2,1,0:T(8,128)S(1)}, f32[5,16,512]{2,1,0:T(8,128)S(1)}, u32[]{:S(2)}, u32[]{:S(2)}) collective-permute-start(f32[5,16,512]{2,1,0:T(8,128)S(1)} %get-tuple-element.37), channel_id=1, source_target_pairs={{0,16},{4,20},{8,24},{12,28},{16,0},{20,4},{24,8},{28,12},{1,17},{... | collective-permute-start | bytes 491528 | tf_op jit(solution)/shard_map/ppermute | solution.py:342
  8.9 2.5 %shard_map.85 = (f32[5,16,512]{2,1,0:T(8,128)S(1)}, f32[5,16,512]{2,1,0:T(8,128)S(1)}, f32[5,16,512]{2,1,0:T(8,128)S(1)}, f32[5,16,512]{2,1,0:T(8,128)S(1)}, f32[5,16,512]{2,1,0:T(8,128)S(1)}) custom-call(s32[8,16]{1,0:T(8,128)S(1)} %bitcast.14, f32[64,5,16,512]{3,2,1,0:T(8,128)} %bitcast.23), custom_call_target="tpu_custom_call" | custom-call | bytes 3000000 | tf_op jit(solution)/shard_map/pallas_call | solution.py:333
  11.5 2.0 %collective-permute-start.4 = (f32[5,16,512]{2,1,0:T(8,128)S(1)}, f32[5,16,512]{2,1,0:T(8,128)S(1)}, u32[]{:S(2)}, u32[]{:S(2)}) collective-permute-start(f32[5,16,512]{2,1,0:T(8,128)S(1)} %get-tuple-element.41), channel_id=1, source_target_pairs={{0,12},{4,8},{8,4},{12,0},{16,28},{20,24},{24,20},{28,16},{1,13},{... | collective-permute-start | bytes 491528 | tf_op jit(solution)/shard_map/ppermute | solution.py:342
  13.5 1.2 %collective-permute-start.5 = (f32[5,16,512]{2,1,0:T(8,128)S(1)}, f32[5,16,512]{2,1,0:T(8,128)S(1)}, u32[]{:S(2)}, u32[]{:S(2)}) collective-permute-start(f32[5,16,512]{2,1,0:T(8,128)S(1)} %get-tuple-element.42), channel_id=1, source_target_pairs={{0,20},{4,16},{8,28},{12,24},{16,4},{20,0},{24,12},{28,8},{1,21},{... | collective-permute-start | bytes 491528 | tf_op jit(solution)/shard_map/ppermute | solution.py:342
  14.7 1.7 %collective-permute-done.1.refs_1_ = f32[5,16,512]{2,1,0:T(8,128)S(1)} collective-permute-done((f32[5,16,512]{2,1,0:T(8,128)S(1)}, f32[5,16,512]{2,1,0:T(8,128)S(1)}, u32[]{:S(2)}, u32[]{:S(2)}) %collective-permute-start.1) | collective-permute-done | bytes 163872 | tf_op jit(solution)/shard_map/ppermute | solution.py:342
  16.4 4.7 %shard_map.82 = (f32[64,5,16,512]{3,2,1,0:T(8,128)S(1)}, f32[64,16,512]{2,1,0:T(8,128)S(1)}, f32[64,5,16,512]{3,2,1,0:T(8,128)S(1)}, f32[5,16,512]{2,1,0:T(8,128)S(1)}, f32[5,16,512]{2,1,0:T(8,128)S(1)}) custom-call(f32[5]{0:T(128)S(1)} %copy-done.5, f32[64,5,16,512]{3,2,1,0:T(8,128)} %bitcast.24, f32[64,16,512]{2,1,0:T(8,128)S(1)} %bitcast.11), custom_call_target="tpu_custom_call" | custom-call | bytes 15000000 | tf_op jit(solution)/shard_map/pallas_call | solution.py:344
  21.2 1.8 %shard_map.86.refs_3_ = f32[64,5,16,512]{3,2,1,0:T(8,128)S(1)} custom-call(s32[8,16]{1,0:T(8,128)S(1)} %bitcast.15, s32[8,16]{1,0:T(8,128)S(1)} %bitcast.17, f32[8,16]{1,0:T(8,128)S(1)} %bitcast.19, f32[64,5,16,512]{3,2,1,0:T(8,128)S(1)} %get-tuple-element.36.flow_ref, ...), custom_call_target="tpu_custom_call", output_to_operand_aliasing={{}: (3, {})} | custom-call | bytes 6000000 | tf_op jit(solution)/shard_map/pallas_call | solution.py:351
  23.2 3.1 %shard_map.87 = (f32[64,5,16,512]{3,2,1,0:T(8,128)S(1)}, f32[4,5,16,512]{3,2,1,0:T(8,128)S(1)}, f32[2,5,16,512]{3,2,1,0:T(8,128)S(1)}, f32[2,5,16,512]{3,2,1,0:T...) custom-call(f32[5,16,512]{2,1,0:T(8,128)S(1)} %get-tuple-element.35.total_ref, ...), custom_call_target="tpu_custom_call", output_to_operand_aliasing={{0}: (4, {})} | custom-call | bytes 12000000 | tf_op jit(solution)/shard_map/pallas_call | solution.py:358
  26.4 2.0 %collective-permute-start.9 = (f32[2,5,16,512]{3,2,1,0:T(8,128)S(1)}, f32[2,5,16,512]{3,2,1,0:T(8,128)S(1)}, u32[]{:S(2)}, u32[]{:S(2)}) collective-permute-start(f32[2,5,16,512]{3,2,1,0:T(8,128)S(1)} %get-tuple-element.54), channel_id=1, source_target_pairs={{0,1},{1,0},{2,3},{3,2},{4,5},{5,4},{6,7},{7,6},{8,9},{9,8},{10,11... | collective-permute-start | bytes 983048 | tf_op jit(solution)/shard_map/ppermute | solution.py:367
  29.1 1.0 %collective-permute-start.7 = (f32[5,16,128]{2,1,0:T(8,128)S(1)}, f32[5,16,128]{2,1,0:T(8,128)S(1)}, u32[]{:S(2)}, u32[]{:S(2)}) collective-permute-start(f32[5,16,128]{2,1,0:T(8,128)S(1)} %get-tuple-element.47.tail_ref), channel_id=1, source_target_pairs={{0,4},{4,0},{1,5},{5,1},{2,6},{6,2},{3,7},{7,3},{8,12},{12,8},{9,1... | collective-permute-start | bytes 122888 | tf_op jit(solution)/shard_map/ppermute | solution.py:308
  30.1 0.8 %collective-permute-done.7.before_ref = f32[5,16,128]{2,1,0:T(8,128)S(1)} collective-permute-done((f32[5,16,128]{2,1,0:T(8,128)S(1)}, f32[5,16,128]{2,1,0:T(8,128)S(1)}, u32[]{:S(2)}, u32[]{:S(2)}) %collective-permute-start.7) | collective-permute-done | bytes 40992 | tf_op jit(solution)/shard_map/ppermute | solution.py:308
  31.3 9.2 %shard_map.88 = (f32[64,5,16,512]{3,2,1,0:T(8,128)S(1)}, f32[3,16,512]{2,1,0:T(8,128)S(1)}) custom-call(f32[5]{0:T(128)S(1)} %copy-done.5, f32[5]{0:T(128)S(1)} %copy-done.6, f32[64,5,16,512]{3,2,1,0:T(8,128)S(1)} %get-tuple-element.44.filled_ref, f32[64,5,16,512]{3,2,1,0:T(8,128)S(1)} %get-tuple-element.45.ratio_ref, ...), custom_call_target="tpu_custom_call", output_to_operand_aliasing={{0}: (2, {})} | custom-call | bytes 27000000 | tf_op jit(solution)/shard_map/pallas_call | solution.py:381
  40.6 2.6 %collective-permute-start.13 = (f32[3,16,512]{2,1,0:T(8,128)S(1)}, f32[3,16,512]{2,1,0:T(8,128)S(1)}, u32[]{:S(2)}, u32[]{:S(2)}) collective-permute-start(f32[3,16,512]{2,1,0:T(8,128)S(1)} %get-tuple-element.62), channel_id=1, source_target_pairs={{0,3},{1,0},{2,1},{3,2},{4,7},{5,4},{6,5},{7,6},{8,11},{9,8},{10,9... | collective-permute-start | bytes 294920 | tf_op jit(solution)/shard_map/ppermute | solution.py:308
  43.2 2.8 %collective-permute-start.12 = (f32[3,16,512]{2,1,0:T(8,128)S(1)}, f32[3,16,512]{2,1,0:T(8,128)S(1)}, u32[]{:S(2)}, u32[]{:S(2)}) collective-permute-start(f32[3,16,512]{2,1,0:T(8,128)S(1)} %get-tuple-element.61), channel_id=1, source_target_pairs={{0,2},{1,3},{2,0},{3,1},{4,6},{5,7},{6,4},{7,5},{8,10},{9,11},{10,... | collective-permute-start | bytes 294920 | tf_op jit(solution)/shard_map/ppermute | solution.py:308
  46.3 6.3 %shard_map.89 = (f32[64,5,16,512]{3,2,1,0:T(8,128)S(1)}, f32[2,16,512]{2,1,0:T(8,128)S(1)}) custom-call(f32[5]{0:T(128)S(1)} %copy-done.5, f32[5]{0:T(128)S(1)} %copy-done.6, f32[64,5,16,512]{3,2,1,0:T(8,128)S(1)} %get-tuple-element.49.filled_ref, f32[64,5,16,512]{3,2,1,0:T(8,128)S(1)} %get-tuple-element.45.ratio_ref, ...), custom_call_target="tpu_custom_call", output_to_operand_aliasing={{0}: (2, {})} | custom-call | bytes 18000000 | tf_op jit(solution)/shard_map/pallas_call | solution.py:381
  52.7 3.6 %collective-permute-start.16 = (f32[2,16,512]{2,1,0:T(8,128)S(1)}, f32[2,16,512]{2,1,0:T(8,128)S(1)}, u32[]{:S(2)}, u32[]{:S(2)}) collective-permute-start(f32[2,16,512]{2,1,0:T(8,128)S(1)} %get-tuple-element.64), channel_id=1, source_target_pairs={{0,3},{1,0},{2,1},{3,2},{4,7},{5,4},{6,5},{7,6},{8,11},{9,8},{10,9... | collective-permute-start | bytes 196616 | tf_op jit(solution)/shard_map/ppermute | solution.py:308
  57.0 2.7 %shard_map.92.refs_0_ = f32[64,5,16,512]{3,2,1,0:T(8,128)} custom-call(f32[64,5,16,512]{3,2,1,0:T(8,128)S(1)} %get-tuple-element.50.local_ref, f32[64,5,16,512]{3,2,1,0:T(8,128)S(1)} %get-tuple-element.45.ratio_ref, f32[3,16,512]{2,1,0:T(8,128)S(1)} %get-tuple-element.59.first_ref, f32[3,16,512]{2,1,0:T(8,128)S(1)} %get-tuple-element.60.last_ref, ...), custom_call_target="tpu_custom_call" | custom-call | bytes 9000000 | tf_op jit(solution)/shard_map/pallas_call | solution.py:398
  59.7 1.8 %collective-permute-done.15.refs_2_ = f32[2,16,512]{2,1,0:T(8,128)S(1)} collective-permute-done((f32[2,16,512]{2,1,0:T(8,128)S(1)}, f32[2,16,512]{2,1,0:T(8,128)S(1)}, u32[]{:S(2)}, u32[]{:S(2)}) %collective-permute-start.15) | collective-permute-done | bytes 65568 | tf_op jit(solution)/shard_map/ppermute | solution.py:308
  61.5 0.9 %collective-permute-done.14.refs_1_ = f32[2,16,512]{2,1,0:T(8,128)S(1)} collective-permute-done((f32[2,16,512]{2,1,0:T(8,128)S(1)}, f32[2,16,512]{2,1,0:T(8,128)S(1)}, u32[]{:S(2)}, u32[]{:S(2)}) %collective-permute-start.14) | collective-permute-done | bytes 65568 | tf_op jit(solution)/shard_map/ppermute | solution.py:308
  62.4 2.1 %shard_map.93 = f32[64,5,16,512]{3,2,1,0:T(8,128)} custom-call(f32[64,5,16,512]{3,2,1,0:T(8,128)S(1)} %get-tuple-element.50.local_ref, f32[64,5,16,512]{3,2,1,0:T(8,128)S(1)} %get-tuple-element.45.ratio_ref, f32[2,16,512]{2,1,0:T(8,128)S(1)} %get-tuple-element.56.first_ref, ...), custom_call_target="tpu_custom_call", output_to_operand_aliasing={{}: (6, {})} | custom-call | bytes 6000000 | tf_op jit(solution)/shard_map/pallas_call | solution.py:398
  (36 shorter events, 2.6 us)
Async XLA Ops:
  0.0 0.7 %copy-start.1 = (s32[1,1,1,8,16]{4,3,2,1,0:T(8,128)S(1)}, s32[1,1,1,8,16]{4,3,2,1,0:T(8,128)}, u32[]{:S(2)}) copy-start(s32[1,1,1,8,16]{4,3,2,1,0:T(8,128)} %param.12) | copy-start | bytes 1540
  2.3 14.2 %copy-start = (f32[1,64,16,512]{3,2,1,0:T(8,128)S(1)}, f32[1,64,16,512]{3,2,1,0:T(8,128)}, u32[]{:S(2)}) copy-start(f32[1,64,16,512]{3,2,1,0:T(8,128)} %param.9) | copy-start | bytes 6291460
  2.3 14.1 %copy-start.5 = (f32[5]{0:T(128)S(1)}, f32[5]{0:T(128)}, u32[]{:S(2)}) copy-start(f32[5]{0:T(128)} %scale_ref.5) | copy-start | bytes 64
  2.3 11.2 %collective-permute-start = (f32[5,16,512]{2,1,0:T(8,128)S(1)}, f32[5,16,512]{2,1,0:T(8,128)S(1)}, u32[]{:S(2)}, u32[]{:S(2)}) collective-permute-start(f32[5,16,512]{2,1,0:T(8,128)S(1)} %shard_map.83), channel_id=1, source_target_pairs={{0,8},{4,12},{8,0},{12,4},{16,24},{20,28},{24,16},{28,20},{1,9},{5... | collective-permute-start | bytes 491528 | tf_op jit(solution)/shard_map/ppermute | solution.py:342
  7.2 9.2 %collective-permute-start.1 = (f32[5,16,512]{2,1,0:T(8,128)S(1)}, f32[5,16,512]{2,1,0:T(8,128)S(1)}, u32[]{:S(2)}, u32[]{:S(2)}) collective-permute-start(f32[5,16,512]{2,1,0:T(8,128)S(1)} %get-tuple-element.37), channel_id=1, source_target_pairs={{0,16},{4,20},{8,24},{12,28},{16,0},{20,4},{24,8},{28,12},{1,17},{... | collective-permute-start | bytes 491528 | tf_op jit(solution)/shard_map/ppermute | solution.py:342
  8.8 12.4 %copy-start.2 = (s32[1,1,1,8,16]{4,3,2,1,0:T(8,128)S(1)}, s32[1,1,1,8,16]{4,3,2,1,0:T(8,128)}, u32[]{:S(2)}) copy-start(s32[1,1,1,8,16]{4,3,2,1,0:T(8,128)} %param.13) | copy-start | bytes 1540
  8.8 12.4 %copy-start.3 = (s32[1,1,1,8,16]{4,3,2,1,0:T(8,128)S(1)}, s32[1,1,1,8,16]{4,3,2,1,0:T(8,128)}, u32[]{:S(2)}) copy-start(s32[1,1,1,8,16]{4,3,2,1,0:T(8,128)} %param.14) | copy-start | bytes 1540
  8.8 12.4 %copy-start.4 = (f32[1,1,1,8,16]{4,3,2,1,0:T(8,128)S(1)}, f32[1,1,1,8,16]{4,3,2,1,0:T(8,128)}, u32[]{:S(2)}) copy-start(f32[1,1,1,8,16]{4,3,2,1,0:T(8,128)} %param.15) | copy-start | bytes 1540
  8.8 12.3 %collective-permute-start.2 = (f32[5,16,512]{2,1,0:T(8,128)S(1)}, f32[5,16,512]{2,1,0:T(8,128)S(1)}, u32[]{:S(2)}, u32[]{:S(2)}) collective-permute-start(f32[5,16,512]{2,1,0:T(8,128)S(1)} %get-tuple-element.38), channel_id=1, source_target_pairs={{0,24},{4,28},{8,16},{12,20},{16,8},{20,12},{24,0},{28,4},{1,25},{... | collective-permute-start | bytes 491528 | tf_op jit(solution)/shard_map/ppermute | solution.py:342
  11.4 9.7 %collective-permute-start.3 = (f32[5,16,512]{2,1,0:T(8,128)S(1)}, f32[5,16,512]{2,1,0:T(8,128)S(1)}, u32[]{:S(2)}, u32[]{:S(2)}) collective-permute-start(f32[5,16,512]{2,1,0:T(8,128)S(1)} %get-tuple-element.39), channel_id=1, source_target_pairs={{0,4},{4,0},{8,12},{12,8},{16,20},{20,16},{24,28},{28,24},{1,5},{5... | collective-permute-start | bytes 491528 | tf_op jit(solution)/shard_map/ppermute | solution.py:342
  11.5 11.5 %collective-permute-start.4 = (f32[5,16,512]{2,1,0:T(8,128)S(1)}, f32[5,16,512]{2,1,0:T(8,128)S(1)}, u32[]{:S(2)}, u32[]{:S(2)}) collective-permute-start(f32[5,16,512]{2,1,0:T(8,128)S(1)} %get-tuple-element.41), channel_id=1, source_target_pairs={{0,12},{4,8},{8,4},{12,0},{16,28},{20,24},{24,20},{28,16},{1,13},{... | collective-permute-start | bytes 491528 | tf_op jit(solution)/shard_map/ppermute | solution.py:342
  13.5 9.7 %collective-permute-start.5 = (f32[5,16,512]{2,1,0:T(8,128)S(1)}, f32[5,16,512]{2,1,0:T(8,128)S(1)}, u32[]{:S(2)}, u32[]{:S(2)}) collective-permute-start(f32[5,16,512]{2,1,0:T(8,128)S(1)} %get-tuple-element.42), channel_id=1, source_target_pairs={{0,20},{4,16},{8,28},{12,24},{16,4},{20,0},{24,12},{28,8},{1,21},{... | collective-permute-start | bytes 491528 | tf_op jit(solution)/shard_map/ppermute | solution.py:342
  16.4 6.8 %collective-permute-start.6 = (f32[5,16,512]{2,1,0:T(8,128)S(1)}, f32[5,16,512]{2,1,0:T(8,128)S(1)}, u32[]{:S(2)}, u32[]{:S(2)}) collective-permute-start(f32[5,16,512]{2,1,0:T(8,128)S(1)} %get-tuple-element.43), channel_id=1, source_target_pairs={{0,28},{4,24},{8,20},{12,16},{16,12},{20,8},{24,4},{28,0},{1,29},{... | collective-permute-start | bytes 491528 | tf_op jit(solution)/shard_map/ppermute | solution.py:342
  23.0 8.3 %copy-start.6 = (f32[5]{0:T(128)S(1)}, f32[5]{0:T(128)}, u32[]{:S(2)}) copy-start(f32[5]{0:T(128)} %span_ref.3) | copy-start | bytes 64
  26.4 14.1 %collective-permute-start.9 = (f32[2,5,16,512]{3,2,1,0:T(8,128)S(1)}, f32[2,5,16,512]{3,2,1,0:T(8,128)S(1)}, u32[]{:S(2)}, u32[]{:S(2)}) collective-permute-start(f32[2,5,16,512]{3,2,1,0:T(8,128)S(1)} %get-tuple-element.54), channel_id=1, source_target_pairs={{0,1},{1,0},{2,3},{3,2},{4,5},{5,4},{6,7},{7,6},{8,9},{9,8},{10,11... | collective-permute-start | bytes 983048 | tf_op jit(solution)/shard_map/ppermute | solution.py:367
  28.4 12.1 %collective-permute-start.10 = (f32[2,5,16,512]{3,2,1,0:T(8,128)S(1)}, f32[2,5,16,512]{3,2,1,0:T(8,128)S(1)}, u32[]{:S(2)}, u32[]{:S(2)}) collective-permute-start(f32[2,5,16,512]{3,2,1,0:T(8,128)S(1)} %get-tuple-element.55), channel_id=1, source_target_pairs={{0,0},{1,2},{2,1},{3,3},{4,4},{5,6},{6,5},{7,7},{8,8},{9,10},{10,9... | collective-permute-start | bytes 983048 | tf_op jit(solution)/shard_map/ppermute | solution.py:367
  29.1 1.9 %collective-permute-start.7 = (f32[5,16,128]{2,1,0:T(8,128)S(1)}, f32[5,16,128]{2,1,0:T(8,128)S(1)}, u32[]{:S(2)}, u32[]{:S(2)}) collective-permute-start(f32[5,16,128]{2,1,0:T(8,128)S(1)} %get-tuple-element.47.tail_ref), channel_id=1, source_target_pairs={{0,4},{4,0},{1,5},{5,1},{2,6},{6,2},{3,7},{7,3},{8,12},{12,8},{9,1... | collective-permute-start | bytes 122888 | tf_op jit(solution)/shard_map/ppermute | solution.py:308
  30.0 1.2 %collective-permute-start.8 = (f32[5,16,128]{2,1,0:T(8,128)S(1)}, f32[5,16,128]{2,1,0:T(8,128)S(1)}, u32[]{:S(2)}, u32[]{:S(2)}) collective-permute-start(f32[5,16,128]{2,1,0:T(8,128)S(1)} %get-tuple-element.48.head_ref), channel_id=1, source_target_pairs={{0,4},{4,0},{1,5},{5,1},{2,6},{6,2},{3,7},{7,3},{8,12},{12,8},{9,1... | collective-permute-start | bytes 122888 | tf_op jit(solution)/shard_map/ppermute | solution.py:308
  40.6 15.8 %collective-permute-start.13 = (f32[3,16,512]{2,1,0:T(8,128)S(1)}, f32[3,16,512]{2,1,0:T(8,128)S(1)}, u32[]{:S(2)}, u32[]{:S(2)}) collective-permute-start(f32[3,16,512]{2,1,0:T(8,128)S(1)} %get-tuple-element.62), channel_id=1, source_target_pairs={{0,3},{1,0},{2,1},{3,2},{4,7},{5,4},{6,5},{7,6},{8,11},{9,8},{10,9... | collective-permute-start | bytes 294920 | tf_op jit(solution)/shard_map/ppermute | solution.py:308
  43.2 13.8 %collective-permute-start.12 = (f32[3,16,512]{2,1,0:T(8,128)S(1)}, f32[3,16,512]{2,1,0:T(8,128)S(1)}, u32[]{:S(2)}, u32[]{:S(2)}) collective-permute-start(f32[3,16,512]{2,1,0:T(8,128)S(1)} %get-tuple-element.61), channel_id=1, source_target_pairs={{0,2},{1,3},{2,0},{3,1},{4,6},{5,7},{6,4},{7,5},{8,10},{9,11},{10,... | collective-permute-start | bytes 294920 | tf_op jit(solution)/shard_map/ppermute | solution.py:308
  46.0 10.9 %collective-permute-start.11 = (f32[3,16,512]{2,1,0:T(8,128)S(1)}, f32[3,16,512]{2,1,0:T(8,128)S(1)}, u32[]{:S(2)}, u32[]{:S(2)}) collective-permute-start(f32[3,16,512]{2,1,0:T(8,128)S(1)} %get-tuple-element.61), channel_id=1, source_target_pairs={{0,1},{1,2},{2,3},{3,0},{4,5},{5,6},{6,7},{7,4},{8,9},{9,10},{10,1... | collective-permute-start | bytes 294920 | tf_op jit(solution)/shard_map/ppermute | solution.py:308
  52.7 7.0 %collective-permute-start.16 = (f32[2,16,512]{2,1,0:T(8,128)S(1)}, f32[2,16,512]{2,1,0:T(8,128)S(1)}, u32[]{:S(2)}, u32[]{:S(2)}) collective-permute-start(f32[2,16,512]{2,1,0:T(8,128)S(1)} %get-tuple-element.64), channel_id=1, source_target_pairs={{0,3},{1,0},{2,1},{3,2},{4,7},{5,4},{6,5},{7,6},{8,11},{9,8},{10,9... | collective-permute-start | bytes 196616 | tf_op jit(solution)/shard_map/ppermute | solution.py:308
  56.3 5.2 %collective-permute-start.15 = (f32[2,16,512]{2,1,0:T(8,128)S(1)}, f32[2,16,512]{2,1,0:T(8,128)S(1)}, u32[]{:S(2)}, u32[]{:S(2)}) collective-permute-start(f32[2,16,512]{2,1,0:T(8,128)S(1)} %get-tuple-element.63), channel_id=1, source_target_pairs={{0,2},{1,3},{2,0},{3,1},{4,6},{5,7},{6,4},{7,5},{8,10},{9,11},{10,... | collective-permute-start | bytes 196616 | tf_op jit(solution)/shard_map/ppermute | solution.py:308
  56.3 6.1 %collective-permute-start.14 = (f32[2,16,512]{2,1,0:T(8,128)S(1)}, f32[2,16,512]{2,1,0:T(8,128)S(1)}, u32[]{:S(2)}, u32[]{:S(2)}) collective-permute-start(f32[2,16,512]{2,1,0:T(8,128)S(1)} %get-tuple-element.63), channel_id=1, source_target_pairs={{0,1},{1,2},{2,3},{3,0},{4,5},{5,6},{6,7},{7,4},{8,9},{9,10},{10,1... | collective-permute-start | bytes 196616 | tf_op jit(solution)/shard_map/ppermute | solution.py:308

commit v3 on v2

--- a/solution.py
+++ b/solution.py
@@ -328,7 +328,7 @@
     order = sorted(range(1, peers), key=lambda turn: (turn == 1, turn & 1, turn))
     near = peers // 2 - 1
     arrived = {}
-    groups = [order[:1], order[1:near], order[near:] + [0]]
+    groups = [order[:near], order[near:] + [0]]
     for turns in groups:
         outgoing = call(
             functools.partial(gather_kernel, turns),
@@ -340,7 +340,8 @@
         for turn, tiles in zip(turns, outgoing):
             route = [(i, i ^ turn) for i in range(peers)]
             arrived[turn] = lax.ppermute(tiles, RING, route) if turn else tiles
-    early, late = order[:near] + [1, 0], order[near:-1]
+    late = order[near:-1][-2:]
+    early = [turn for turn in order + [0] if turn not in late]
     flow_in, speed_in, ratio, total, last = call(
         growth_kernel,
         (SMEM, HBM, HBM), (VMEM,) * 5,
@@ -362,6 +363,8 @@
         aliases={4: 0},
         micros=4,
     )(total, tile, live, weight, partly, *(arrived[turn] for turn in late))
+    before = moved(tail, "span", 1)
+    after = moved(head, "span", -1)
     pairs = [[i ^ 1 for i in range(sections)], [((i + 1) ^ 1) - 1 for i in range(sections)]]
     even, odd = (
         lax.ppermute(
@@ -371,8 +374,6 @@
         )
         for message, others in zip((even, odd), pairs)
     )
-    before = moved(tail, "span", 1)
-    after = moved(head, "span", -1)
     assert sections <= 4
     split = (components + 1) // 2
     state_now, parts = filled, []

time: 64.9 us -> 63.2 us (0.974)
  Pallas kernels: 36 us -> 34.7 us
    pallas_call x3 -> x2, Pallas kernels: 5.97 us -> 4.6 us  [on_device(): call(functools.partial(gather_kernel, turns), (SMEM, HBM), (VMEM,) * len(...]
  transfers between devices with their start and end apart: 17 -> 17, of which waited for: 6 -> 6; matrix products, arithmetic and copies ran while one was open for 0% -> 0% of each run, Pallas kernels for 45% -> 44%
where the time goes in v3:
time: 63.2 us; the launch traced here: 62.9 us
  Pallas kernels  34.7 us (55%)
  starting transfers between devices  21.4 us (34%)
  waiting for transfers between devices  5.86 us (9%)
  local copies, waits for them, and re-layouts  0.71 us (1%)
    pallas_call x2, Pallas kernels, on_device(): call(functools.partial(scan_kernel, lowest), (SMEM, SMEM) + (VMEM,) * 7,...  15.5 us
    ppermute x8, starting transfers between devices, moved(): lax.ppermute(value, axis, [(i, (i + distance) % count) for i in range(cou...  11 us
    ppermute x7, starting transfers between devices, on_device(): arrived[turn] = lax.ppermute(tiles, RING, route) if turn else tiles  7.83 us
    pallas_call x2, Pallas kernels, on_device(): call(functools.partial(combine_kernel, lowest, len(begun)), (VMEM,) * 6 +...  4.81 us
    pallas_call x1, Pallas kernels, on_device(): call(growth_kernel, (SMEM, HBM, HBM), (VMEM,) * 5, [hold(state), hold(spe...  4.68 us
    pallas_call x2, Pallas kernels, on_device(): call(functools.partial(gather_kernel, turns), (SMEM, HBM), (VMEM,) * len(...  4.6 us
    ppermute x8, waiting for transfers between devices, moved(): lax.ppermute(value, axis, [(i, (i + distance) % count) for i in range(cou...  3.8 us
    pallas_call x1, Pallas kernels, on_device(): call(functools.partial(last_fill_kernel, late), (VMEM,) + (SMEM,) * 3 + (...  2.92 us
  transfers between devices with their start and end apart: 17, of which 6 were waited for; matrix products, arithmetic and copies ran while one was open for 0% of the time, Pallas kernels for 44%

profile of v3, /device:TPU:0, one launch (start us, length us, event | category | flops | bytes accessed | tf_op | source)
XLA Modules:
  0.0 62.9 jit_solution(17125708205751039022)
XLA Ops:
  0.0 0.7 %copy-done.1 = s32[1,1,1,8,16]{4,3,2,1,0:T(8,128)S(1)} copy-done((s32[1,1,1,8,16]{4,3,2,1,0:T(8,128)S(1)}, s32[1,1,1,8,16]{4,3,2,1,0:T(8,128)}, u32[]{:S(2)}) %copy-start.1) | copy-done | bytes 536
  0.7 2.1 %shard_map.83 = (f32[5,16,512]{2,1,0:T(8,128)S(1)}, f32[5,16,512]{2,1,0:T(8,128)S(1)}, f32[5,16,512]{2,1,0:T(8,128)S(1)}) custom-call(s32[8,16]{1,0:T(8,128)S(1)} %bitcast.12, f32[64,5,16,512]{3,2,1,0:T(8,128)} %bitcast.20), custom_call_target="tpu_custom_call" | custom-call | bytes 3000000 | tf_op jit(solution)/shard_map/pallas_call | solution.py:333
  2.8 3.0 %collective-permute-start = (f32[5,16,512]{2,1,0:T(8,128)S(1)}, f32[5,16,512]{2,1,0:T(8,128)S(1)}, u32[]{:S(2)}, u32[]{:S(2)}) collective-permute-start(f32[5,16,512]{2,1,0:T(8,128)S(1)} %get-tuple-element.38), channel_id=1, source_target_pairs={{0,8},{4,12},{8,0},{12,4},{16,24},{20,28},{24,16},{28,20},{1,9},{5... | collective-permute-start | bytes 491528 | tf_op jit(solution)/shard_map/ppermute | solution.py:342
  5.8 1.5 %collective-permute-start.1 = (f32[5,16,512]{2,1,0:T(8,128)S(1)}, f32[5,16,512]{2,1,0:T(8,128)S(1)}, u32[]{:S(2)}, u32[]{:S(2)}) collective-permute-start(f32[5,16,512]{2,1,0:T(8,128)S(1)} %get-tuple-element.39), channel_id=1, source_target_pairs={{0,16},{4,20},{8,24},{12,28},{16,0},{20,4},{24,8},{28,12},{1,17},{... | collective-permute-start | bytes 491528 | tf_op jit(solution)/shard_map/ppermute | solution.py:342
  7.4 2.5 %shard_map.84 = (f32[5,16,512]{2,1,0:T(8,128)S(1)}, f32[5,16,512]{2,1,0:T(8,128)S(1)}, f32[5,16,512]{2,1,0:T(8,128)S(1)}, f32[5,16,512]{2,1,0:T(8,128)S(1)}, f32[5,16,512]{2,1,0:T(8,128)S(1)}) custom-call(s32[8,16]{1,0:T(8,128)S(1)} %bitcast.13, f32[64,5,16,512]{3,2,1,0:T(8,128)} %bitcast.21), custom_call_target="tpu_custom_call" | custom-call | bytes 3000000 | tf_op jit(solution)/shard_map/pallas_call | solution.py:333
  10.5 1.5 %collective-permute-start.4 = (f32[5,16,512]{2,1,0:T(8,128)S(1)}, f32[5,16,512]{2,1,0:T(8,128)S(1)}, u32[]{:S(2)}, u32[]{:S(2)}) collective-permute-start(f32[5,16,512]{2,1,0:T(8,128)S(1)} %get-tuple-element.42), channel_id=1, source_target_pairs={{0,4},{4,0},{8,12},{12,8},{16,20},{20,16},{24,28},{28,24},{1,5},{5... | collective-permute-start | bytes 491528 | tf_op jit(solution)/shard_map/ppermute | solution.py:342
  12.0 1.1 %collective-permute-start.5 = (f32[5,16,512]{2,1,0:T(8,128)S(1)}, f32[5,16,512]{2,1,0:T(8,128)S(1)}, u32[]{:S(2)}, u32[]{:S(2)}) collective-permute-start(f32[5,16,512]{2,1,0:T(8,128)S(1)} %get-tuple-element.44), channel_id=1, source_target_pairs={{0,20},{4,16},{8,28},{12,24},{16,4},{20,0},{24,12},{28,8},{1,21},{... | collective-permute-start | bytes 491528 | tf_op jit(solution)/shard_map/ppermute | solution.py:342
  13.1 1.6 %collective-permute-done.1.refs_1_ = f32[5,16,512]{2,1,0:T(8,128)S(1)} collective-permute-done((f32[5,16,512]{2,1,0:T(8,128)S(1)}, f32[5,16,512]{2,1,0:T(8,128)S(1)}, u32[]{:S(2)}, u32[]{:S(2)}) %collective-permute-start.1) | collective-permute-done | bytes 163872 | tf_op jit(solution)/shard_map/ppermute | solution.py:342
  14.8 4.7 %shard_map.82 = (f32[64,5,16,512]{3,2,1,0:T(8,128)S(1)}, f32[64,16,512]{2,1,0:T(8,128)S(1)}, f32[64,5,16,512]{3,2,1,0:T(8,128)S(1)}, f32[5,16,512]{2,1,0:T(8,128)S(1)}, f32[5,16,512]{2,1,0:T(8,128)S(1)}) custom-call(f32[5]{0:T(128)S(1)} %copy-done.5, f32[64,5,16,512]{3,2,1,0:T(8,128)} %bitcast.22, f32[64,16,512]{2,1,0:T(8,128)S(1)} %bitcast.11), custom_call_target="tpu_custom_call" | custom-call | bytes 15000000 | tf_op jit(solution)/shard_map/pallas_call | solution.py:345
  19.5 2.0 %shard_map.85.refs_3_ = f32[64,5,16,512]{3,2,1,0:T(8,128)S(1)} custom-call(s32[8,16]{1,0:T(8,128)S(1)} %bitcast.14, s32[8,16]{1,0:T(8,128)S(1)} %bitcast.16, f32[8,16]{1,0:T(8,128)S(1)} %bitcast.18, f32[64,5,16,512]{3,2,1,0:T(8,128)S(1)} %get-tuple-element.37.flow_ref, ...), custom_call_target="tpu_custom_call", output_to_operand_aliasing={{}: (3, {})} | custom-call | bytes 6000000 | tf_op jit(solution)/shard_map/pallas_call | solution.py:352
  22.0 2.9 %shard_map.86 = (f32[64,5,16,512]{3,2,1,0:T(8,128)S(1)}, f32[4,5,16,512]{3,2,1,0:T(8,128)S(1)}, f32[2,5,16,512]{3,2,1,0:T(8,128)S(1)}, f32[2,5,16,512]{3,2,1,0:T...) custom-call(f32[5,16,512]{2,1,0:T(8,128)S(1)} %get-tuple-element.36.total_ref, ...), custom_call_target="tpu_custom_call", output_to_operand_aliasing={{0}: (4, {})} | custom-call | bytes 12000000 | tf_op jit(solution)/shard_map/pallas_call | solution.py:359
  24.9 1.9 %collective-permute-start.9 = (f32[2,5,16,512]{3,2,1,0:T(8,128)S(1)}, f32[2,5,16,512]{3,2,1,0:T(8,128)S(1)}, u32[]{:S(2)}, u32[]{:S(2)}) collective-permute-start(f32[2,5,16,512]{3,2,1,0:T(8,128)S(1)} %get-tuple-element.56), channel_id=1, source_target_pairs={{0,1},{1,0},{2,3},{3,2},{4,5},{5,4},{6,7},{7,6},{8,9},{9,8},{10,11... | collective-permute-start | bytes 983048 | tf_op jit(solution)/shard_map/ppermute | solution.py:370
  26.8 0.7 %collective-permute-start.10 = (f32[2,5,16,512]{3,2,1,0:T(8,128)S(1)}, f32[2,5,16,512]{3,2,1,0:T(8,128)S(1)}, u32[]{:S(2)}, u32[]{:S(2)}) collective-permute-start(f32[2,5,16,512]{3,2,1,0:T(8,128)S(1)} %get-tuple-element.57), channel_id=1, source_target_pairs={{0,0},{1,2},{2,1},{3,3},{4,4},{5,6},{6,5},{7,7},{8,8},{9,10},{10,9... | collective-permute-start | bytes 983048 | tf_op jit(solution)/shard_map/ppermute | solution.py:370
  27.5 0.9 %collective-permute-start.7 = (f32[5,16,128]{2,1,0:T(8,128)S(1)}, f32[5,16,128]{2,1,0:T(8,128)S(1)}, u32[]{:S(2)}, u32[]{:S(2)}) collective-permute-start(f32[5,16,128]{2,1,0:T(8,128)S(1)} %get-tuple-element.49.tail_ref), channel_id=1, source_target_pairs={{0,4},{4,0},{1,5},{5,1},{2,6},{6,2},{3,7},{7,3},{8,12},{12,8},{9,1... | collective-permute-start | bytes 122888 | tf_op jit(solution)/shard_map/ppermute | solution.py:308
  28.5 0.8 %collective-permute-done.7.before_ref = f32[5,16,128]{2,1,0:T(8,128)S(1)} collective-permute-done((f32[5,16,128]{2,1,0:T(8,128)S(1)}, f32[5,16,128]{2,1,0:T(8,128)S(1)}, u32[]{:S(2)}, u32[]{:S(2)}) %collective-permute-start.7) | collective-permute-done | bytes 40992 | tf_op jit(solution)/shard_map/ppermute | solution.py:308
  29.7 9.2 %shard_map.87 = (f32[64,5,16,512]{3,2,1,0:T(8,128)S(1)}, f32[3,16,512]{2,1,0:T(8,128)S(1)}) custom-call(f32[5]{0:T(128)S(1)} %copy-done.5, f32[5]{0:T(128)S(1)} %copy-done.6, f32[64,5,16,512]{3,2,1,0:T(8,128)S(1)} %get-tuple-element.46.filled_ref, f32[64,5,16,512]{3,2,1,0:T(8,128)S(1)} %get-tuple-element.47.ratio_ref, ...), custom_call_target="tpu_custom_call", output_to_operand_aliasing={{0}: (2, {})} | custom-call | bytes 27000000 | tf_op jit(solution)/shard_map/pallas_call | solution.py:382
  39.0 2.6 %collective-permute-start.13 = (f32[3,16,512]{2,1,0:T(8,128)S(1)}, f32[3,16,512]{2,1,0:T(8,128)S(1)}, u32[]{:S(2)}, u32[]{:S(2)}) collective-permute-start(f32[3,16,512]{2,1,0:T(8,128)S(1)} %get-tuple-element.64), channel_id=1, source_target_pairs={{0,3},{1,0},{2,1},{3,2},{4,7},{5,4},{6,5},{7,6},{8,11},{9,8},{10,9... | collective-permute-start | bytes 294920 | tf_op jit(solution)/shard_map/ppermute | solution.py:308
  41.6 2.8 %collective-permute-start.12 = (f32[3,16,512]{2,1,0:T(8,128)S(1)}, f32[3,16,512]{2,1,0:T(8,128)S(1)}, u32[]{:S(2)}, u32[]{:S(2)}) collective-permute-start(f32[3,16,512]{2,1,0:T(8,128)S(1)} %get-tuple-element.63), channel_id=1, source_target_pairs={{0,2},{1,3},{2,0},{3,1},{4,6},{5,7},{6,4},{7,5},{8,10},{9,11},{10,... | collective-permute-start | bytes 294920 | tf_op jit(solution)/shard_map/ppermute | solution.py:308
  44.7 6.3 %shard_map.88 = (f32[64,5,16,512]{3,2,1,0:T(8,128)S(1)}, f32[2,16,512]{2,1,0:T(8,128)S(1)}) custom-call(f32[5]{0:T(128)S(1)} %copy-done.5, f32[5]{0:T(128)S(1)} %copy-done.6, f32[64,5,16,512]{3,2,1,0:T(8,128)S(1)} %get-tuple-element.51.filled_ref, f32[64,5,16,512]{3,2,1,0:T(8,128)S(1)} %get-tuple-element.47.ratio_ref, ...), custom_call_target="tpu_custom_call", output_to_operand_aliasing={{0}: (2, {})} | custom-call | bytes 18000000 | tf_op jit(solution)/shard_map/pallas_call | solution.py:382
  51.1 3.6 %collective-permute-start.16 = (f32[2,16,512]{2,1,0:T(8,128)S(1)}, f32[2,16,512]{2,1,0:T(8,128)S(1)}, u32[]{:S(2)}, u32[]{:S(2)}) collective-permute-start(f32[2,16,512]{2,1,0:T(8,128)S(1)} %get-tuple-element.66), channel_id=1, source_target_pairs={{0,3},{1,0},{2,1},{3,2},{4,7},{5,4},{6,5},{7,6},{8,11},{9,8},{10,9... | collective-permute-start | bytes 196616 | tf_op jit(solution)/shard_map/ppermute | solution.py:308
  55.4 2.7 %shard_map.91.refs_0_ = f32[64,5,16,512]{3,2,1,0:T(8,128)} custom-call(f32[64,5,16,512]{3,2,1,0:T(8,128)S(1)} %get-tuple-element.52.local_ref, f32[64,5,16,512]{3,2,1,0:T(8,128)S(1)} %get-tuple-element.47.ratio_ref, f32[3,16,512]{2,1,0:T(8,128)S(1)} %get-tuple-element.61.first_ref, f32[3,16,512]{2,1,0:T(8,128)S(1)} %get-tuple-element.62.last_ref, ...), custom_call_target="tpu_custom_call" | custom-call | bytes 9000000 | tf_op jit(solution)/shard_map/pallas_call | solution.py:399
  58.1 1.8 %collective-permute-done.15.refs_2_ = f32[2,16,512]{2,1,0:T(8,128)S(1)} collective-permute-done((f32[2,16,512]{2,1,0:T(8,128)S(1)}, f32[2,16,512]{2,1,0:T(8,128)S(1)}, u32[]{:S(2)}, u32[]{:S(2)}) %collective-permute-start.15) | collective-permute-done | bytes 65568 | tf_op jit(solution)/shard_map/ppermute | solution.py:308
  59.9 0.9 %collective-permute-done.14.refs_1_ = f32[2,16,512]{2,1,0:T(8,128)S(1)} collective-permute-done((f32[2,16,512]{2,1,0:T(8,128)S(1)}, f32[2,16,512]{2,1,0:T(8,128)S(1)}, u32[]{:S(2)}, u32[]{:S(2)}) %collective-permute-start.14) | collective-permute-done | bytes 65568 | tf_op jit(solution)/shard_map/ppermute | solution.py:308
  60.8 2.1 %shard_map.92 = f32[64,5,16,512]{3,2,1,0:T(8,128)} custom-call(f32[64,5,16,512]{3,2,1,0:T(8,128)S(1)} %get-tuple-element.52.local_ref, f32[64,5,16,512]{3,2,1,0:T(8,128)S(1)} %get-tuple-element.47.ratio_ref, f32[2,16,512]{2,1,0:T(8,128)S(1)} %get-tuple-element.58.first_ref, ...), custom_call_target="tpu_custom_call", output_to_operand_aliasing={{}: (6, {})} | custom-call | bytes 6000000 | tf_op jit(solution)/shard_map/pallas_call | solution.py:399
  (35 shorter events, 2.6 us)
Async XLA Ops:
  0.0 0.7 %copy-start.1 = (s32[1,1,1,8,16]{4,3,2,1,0:T(8,128)S(1)}, s32[1,1,1,8,16]{4,3,2,1,0:T(8,128)}, u32[]{:S(2)}) copy-start(s32[1,1,1,8,16]{4,3,2,1,0:T(8,128)} %param.12) | copy-start | bytes 1540
  0.7 14.1 %copy-start = (f32[1,64,16,512]{3,2,1,0:T(8,128)S(1)}, f32[1,64,16,512]{3,2,1,0:T(8,128)}, u32[]{:S(2)}) copy-start(f32[1,64,16,512]{3,2,1,0:T(8,128)} %param.9) | copy-start | bytes 6291460
  0.7 14.1 %copy-start.5 = (f32[5]{0:T(128)S(1)}, f32[5]{0:T(128)}, u32[]{:S(2)}) copy-start(f32[5]{0:T(128)} %scale_ref.5) | copy-start | bytes 64
  2.8 9.3 %collective-permute-start = (f32[5,16,512]{2,1,0:T(8,128)S(1)}, f32[5,16,512]{2,1,0:T(8,128)S(1)}, u32[]{:S(2)}, u32[]{:S(2)}) collective-permute-start(f32[5,16,512]{2,1,0:T(8,128)S(1)} %get-tuple-element.38), channel_id=1, source_target_pairs={{0,8},{4,12},{8,0},{12,4},{16,24},{20,28},{24,16},{28,20},{1,9},{5... | collective-permute-start | bytes 491528 | tf_op jit(solution)/shard_map/ppermute | solution.py:342
  5.8 9.0 %collective-permute-start.1 = (f32[5,16,512]{2,1,0:T(8,128)S(1)}, f32[5,16,512]{2,1,0:T(8,128)S(1)}, u32[]{:S(2)}, u32[]{:S(2)}) collective-permute-start(f32[5,16,512]{2,1,0:T(8,128)S(1)} %get-tuple-element.39), channel_id=1, source_target_pairs={{0,16},{4,20},{8,24},{12,28},{16,0},{20,4},{24,8},{28,12},{1,17},{... | collective-permute-start | bytes 491528 | tf_op jit(solution)/shard_map/ppermute | solution.py:342
  7.3 12.2 %copy-start.2 = (s32[1,1,1,8,16]{4,3,2,1,0:T(8,128)S(1)}, s32[1,1,1,8,16]{4,3,2,1,0:T(8,128)}, u32[]{:S(2)}) copy-start(s32[1,1,1,8,16]{4,3,2,1,0:T(8,128)} %param.13) | copy-start | bytes 1540
  7.3 12.2 %copy-start.3 = (s32[1,1,1,8,16]{4,3,2,1,0:T(8,128)S(1)}, s32[1,1,1,8,16]{4,3,2,1,0:T(8,128)}, u32[]{:S(2)}) copy-start(s32[1,1,1,8,16]{4,3,2,1,0:T(8,128)} %param.14) | copy-start | bytes 1540
  7.3 12.2 %copy-start.4 = (f32[1,1,1,8,16]{4,3,2,1,0:T(8,128)S(1)}, f32[1,1,1,8,16]{4,3,2,1,0:T(8,128)}, u32[]{:S(2)}) copy-start(f32[1,1,1,8,16]{4,3,2,1,0:T(8,128)} %param.15) | copy-start | bytes 1540
  7.3 12.2 %collective-permute-start.2 = (f32[5,16,512]{2,1,0:T(8,128)S(1)}, f32[5,16,512]{2,1,0:T(8,128)S(1)}, u32[]{:S(2)}, u32[]{:S(2)}) collective-permute-start(f32[5,16,512]{2,1,0:T(8,128)S(1)} %get-tuple-element.40), channel_id=1, source_target_pairs={{0,24},{4,28},{8,16},{12,20},{16,8},{20,12},{24,0},{28,4},{1,25},{... | collective-permute-start | bytes 491528 | tf_op jit(solution)/shard_map/ppermute | solution.py:342
  9.9 9.6 %collective-permute-start.3 = (f32[5,16,512]{2,1,0:T(8,128)S(1)}, f32[5,16,512]{2,1,0:T(8,128)S(1)}, u32[]{:S(2)}, u32[]{:S(2)}) collective-permute-start(f32[5,16,512]{2,1,0:T(8,128)S(1)} %get-tuple-element.41), channel_id=1, source_target_pairs={{0,12},{4,8},{8,4},{12,0},{16,28},{20,24},{24,20},{28,16},{1,13},{... | collective-permute-start | bytes 491528 | tf_op jit(solution)/shard_map/ppermute | solution.py:342
  10.5 9.0 %collective-permute-start.4 = (f32[5,16,512]{2,1,0:T(8,128)S(1)}, f32[5,16,512]{2,1,0:T(8,128)S(1)}, u32[]{:S(2)}, u32[]{:S(2)}) collective-permute-start(f32[5,16,512]{2,1,0:T(8,128)S(1)} %get-tuple-element.42), channel_id=1, source_target_pairs={{0,4},{4,0},{8,12},{12,8},{16,20},{20,16},{24,28},{28,24},{1,5},{5... | collective-permute-start | bytes 491528 | tf_op jit(solution)/shard_map/ppermute | solution.py:342
  12.0 10.0 %collective-permute-start.5 = (f32[5,16,512]{2,1,0:T(8,128)S(1)}, f32[5,16,512]{2,1,0:T(8,128)S(1)}, u32[]{:S(2)}, u32[]{:S(2)}) collective-permute-start(f32[5,16,512]{2,1,0:T(8,128)S(1)} %get-tuple-element.44), channel_id=1, source_target_pairs={{0,20},{4,16},{8,28},{12,24},{16,4},{20,0},{24,12},{28,8},{1,21},{... | collective-permute-start | bytes 491528 | tf_op jit(solution)/shard_map/ppermute | solution.py:342
  14.8 7.2 %collective-permute-start.6 = (f32[5,16,512]{2,1,0:T(8,128)S(1)}, f32[5,16,512]{2,1,0:T(8,128)S(1)}, u32[]{:S(2)}, u32[]{:S(2)}) collective-permute-start(f32[5,16,512]{2,1,0:T(8,128)S(1)} %get-tuple-element.45), channel_id=1, source_target_pairs={{0,28},{4,24},{8,20},{12,16},{16,12},{20,8},{24,4},{28,0},{1,29},{... | collective-permute-start | bytes 491528 | tf_op jit(solution)/shard_map/ppermute | solution.py:342
  21.6 8.1 %copy-start.6 = (f32[5]{0:T(128)S(1)}, f32[5]{0:T(128)}, u32[]{:S(2)}) copy-start(f32[5]{0:T(128)} %span_ref.3) | copy-start | bytes 64
  24.9 13.9 %collective-permute-start.9 = (f32[2,5,16,512]{3,2,1,0:T(8,128)S(1)}, f32[2,5,16,512]{3,2,1,0:T(8,128)S(1)}, u32[]{:S(2)}, u32[]{:S(2)}) collective-permute-start(f32[2,5,16,512]{3,2,1,0:T(8,128)S(1)} %get-tuple-element.56), channel_id=1, source_target_pairs={{0,1},{1,0},{2,3},{3,2},{4,5},{5,4},{6,7},{7,6},{8,9},{9,8},{10,11... | collective-permute-start | bytes 983048 | tf_op jit(solution)/shard_map/ppermute | solution.py:370
  26.8 12.0 %collective-permute-start.10 = (f32[2,5,16,512]{3,2,1,0:T(8,128)S(1)}, f32[2,5,16,512]{3,2,1,0:T(8,128)S(1)}, u32[]{:S(2)}, u32[]{:S(2)}) collective-permute-start(f32[2,5,16,512]{3,2,1,0:T(8,128)S(1)} %get-tuple-element.57), channel_id=1, source_target_pairs={{0,0},{1,2},{2,1},{3,3},{4,4},{5,6},{6,5},{7,7},{8,8},{9,10},{10,9... | collective-permute-start | bytes 983048 | tf_op jit(solution)/shard_map/ppermute | solution.py:370
  27.5 1.8 %collective-permute-start.7 = (f32[5,16,128]{2,1,0:T(8,128)S(1)}, f32[5,16,128]{2,1,0:T(8,128)S(1)}, u32[]{:S(2)}, u32[]{:S(2)}) collective-permute-start(f32[5,16,128]{2,1,0:T(8,128)S(1)} %get-tuple-element.49.tail_ref), channel_id=1, source_target_pairs={{0,4},{4,0},{1,5},{5,1},{2,6},{6,2},{3,7},{7,3},{8,12},{12,8},{9,1... | collective-permute-start | bytes 122888 | tf_op jit(solution)/shard_map/ppermute | solution.py:308
  28.4 1.2 %collective-permute-start.8 = (f32[5,16,128]{2,1,0:T(8,128)S(1)}, f32[5,16,128]{2,1,0:T(8,128)S(1)}, u32[]{:S(2)}, u32[]{:S(2)}) collective-permute-start(f32[5,16,128]{2,1,0:T(8,128)S(1)} %get-tuple-element.50.head_ref), channel_id=1, source_target_pairs={{0,4},{4,0},{1,5},{5,1},{2,6},{6,2},{3,7},{7,3},{8,12},{12,8},{9,1... | collective-permute-start | bytes 122888 | tf_op jit(solution)/shard_map/ppermute | solution.py:308
  39.0 15.8 %collective-permute-start.13 = (f32[3,16,512]{2,1,0:T(8,128)S(1)}, f32[3,16,512]{2,1,0:T(8,128)S(1)}, u32[]{:S(2)}, u32[]{:S(2)}) collective-permute-start(f32[3,16,512]{2,1,0:T(8,128)S(1)} %get-tuple-element.64), channel_id=1, source_target_pairs={{0,3},{1,0},{2,1},{3,2},{4,7},{5,4},{6,5},{7,6},{8,11},{9,8},{10,9... | collective-permute-start | bytes 294920 | tf_op jit(solution)/shard_map/ppermute | solution.py:308
  41.6 13.8 %collective-permute-start.12 = (f32[3,16,512]{2,1,0:T(8,128)S(1)}, f32[3,16,512]{2,1,0:T(8,128)S(1)}, u32[]{:S(2)}, u32[]{:S(2)}) collective-permute-start(f32[3,16,512]{2,1,0:T(8,128)S(1)} %get-tuple-element.63), channel_id=1, source_target_pairs={{0,2},{1,3},{2,0},{3,1},{4,6},{5,7},{6,4},{7,5},{8,10},{9,11},{10,... | collective-permute-start | bytes 294920 | tf_op jit(solution)/shard_map/ppermute | solution.py:308
  44.4 10.9 %collective-permute-start.11 = (f32[3,16,512]{2,1,0:T(8,128)S(1)}, f32[3,16,512]{2,1,0:T(8,128)S(1)}, u32[]{:S(2)}, u32[]{:S(2)}) collective-permute-start(f32[3,16,512]{2,1,0:T(8,128)S(1)} %get-tuple-element.63), channel_id=1, source_target_pairs={{0,1},{1,2},{2,3},{3,0},{4,5},{5,6},{6,7},{7,4},{8,9},{9,10},{10,1... | collective-permute-start | bytes 294920 | tf_op jit(solution)/shard_map/ppermute | solution.py:308
  51.1 7.0 %collective-permute-start.16 = (f32[2,16,512]{2,1,0:T(8,128)S(1)}, f32[2,16,512]{2,1,0:T(8,128)S(1)}, u32[]{:S(2)}, u32[]{:S(2)}) collective-permute-start(f32[2,16,512]{2,1,0:T(8,128)S(1)} %get-tuple-element.66), channel_id=1, source_target_pairs={{0,3},{1,0},{2,1},{3,2},{4,7},{5,4},{6,5},{7,6},{8,11},{9,8},{10,9... | collective-permute-start | bytes 196616 | tf_op jit(solution)/shard_map/ppermute | solution.py:308
  54.7 5.2 %collective-permute-start.15 = (f32[2,16,512]{2,1,0:T(8,128)S(1)}, f32[2,16,512]{2,1,0:T(8,128)S(1)}, u32[]{:S(2)}, u32[]{:S(2)}) collective-permute-start(f32[2,16,512]{2,1,0:T(8,128)S(1)} %get-tuple-element.65), channel_id=1, source_target_pairs={{0,2},{1,3},{2,0},{3,1},{4,6},{5,7},{6,4},{7,5},{8,10},{9,11},{10,... | collective-permute-start | bytes 196616 | tf_op jit(solution)/shard_map/ppermute | solution.py:308
  54.7 6.1 %collective-permute-start.14 = (f32[2,16,512]{2,1,0:T(8,128)S(1)}, f32[2,16,512]{2,1,0:T(8,128)S(1)}, u32[]{:S(2)}, u32[]{:S(2)}) collective-permute-start(f32[2,16,512]{2,1,0:T(8,128)S(1)} %get-tuple-element.65), channel_id=1, source_target_pairs={{0,1},{1,2},{2,3},{3,0},{4,5},{5,6},{6,7},{7,4},{8,9},{9,10},{10,1... | collective-permute-start | bytes 196616 | tf_op jit(solution)/shard_map/ppermute | solution.py:308

commit v4 on v3

--- a/solution.py
+++ b/solution.py
@@ -10,6 +10,7 @@
 LANES = 128
 SUB = 8
 STEPS = 16
+LAG = 6
 F32 = jnp.float32
 
 
@@ -206,39 +207,41 @@
             moved_left = [pltpu.roll(u, LANES - 1, 1) for u in values] + [edge]
             return [jnp.where(final, moved_left[b + 1], moved_left[b]) for b in every]
 
-        def steps(k, carry):
-            here, rise, inflow = carry
-            start = k * STEPS
-            span = range(STEPS)
-            turn = [LANES - 2 * (start + i) - 1 for i in span]
-            rows = [here] + [load(filled_ref, start + i, v) for i in range(1, STEPS)]
-            rows.append(load(filled_ref, jnp.minimum(start + STEPS, width_x - 1), v))
-            back = [right(rows[i], pltpu.roll(prior, turn[i], 1)) for i in span]
-            fall = [[0.5 * (rows[i][b] - back[i][b]) for b in every] for i in span]
-            grow = [left(fall[i], pltpu.roll(diff, turn[i] - 1, 1)) for i in span]
-            faces = [[rows[i][b] + limited(fall[i][b], grow[i][b]) for b in every] for i in span]
-            shifted = [right(faces[i], pltpu.roll(face, turn[i], 1)) for i in span]
-            known = [[rows[i][b] + scale_z * (shifted[i][b] - faces[i][b]) for b in every] for i in span]
-            outs = []
-            for i in span:
-                u = rows[i]
-                ratio = load(ratio_ref, start + i, v)
-                rise_later = [0.5 * (rows[i + 1][b] - u[b]) for b in every]
+        inflow = [jnp.zeros((SUB, LANES), F32)] * blocks
+        rise = inflow
+        rows, falls, faces, known = {}, {}, {}, {}
+        for tick in range(width_x + 3 * LAG):
+            i = tick
+            if i < width_x:
+                rows[i] = load(filled_ref, i, v)
+                back = right(rows[i], pltpu.roll(prior, LANES - 2 * i - 1, 1))
+                falls[i] = [0.5 * (rows[i][b] - back[b]) for b in every]
+            i = tick - LAG
+            if 0 <= i < width_x:
+                fall = falls.pop(i)
+                grow = left(fall, pltpu.roll(diff, LANES - 2 * i - 2, 1))
+                faces[i] = [rows[i][b] + limited(fall[b], grow[b]) for b in every]
+            i = tick - 2 * LAG
+            if 0 <= i < width_x:
+                flat = faces.pop(i)
+                shifted = right(flat, pltpu.roll(face, LANES - 2 * i - 1, 1))
+                known[i] = [rows[i][b] + scale_z * (shifted[b] - flat[b]) for b in every]
+            i = tick - 3 * LAG
+            if i >= 0:
+                u = rows.pop(i)
+                later = rows.get(i + 1, u)
+                rise_later = [0.5 * (later[b] - u[b]) for b in every]
+                ratio = load(ratio_ref, i, v)
+                cross = known.pop(i)
                 slope = [limited(rise[b], rise_later[b]) for b in every]
-                total = [inflow[b] + (known[i][b] + slope[b]) for b in every]
+                total = [inflow[b] + (cross[b] + slope[b]) for b in every]
                 value = [ratio[b] * total[b] for b in every]
                 inflow = [total[b] - value[b] for b in every]
                 rise = rise_later
-                outs.append([value[b] - slope[b] for b in every])
-            for i in span:
                 for b in every:
-                    local_ref[start + i, v, y, slice(b * LANES, (b + 1) * LANES)] = outs[i][b]
-            return rows[STEPS], rise, inflow
-
-        zeros = [jnp.zeros((SUB, LANES), F32)] * blocks
-        _, _, flux = lax.fori_loop(0, width_x // STEPS, steps, (load(filled_ref, 0, v), zeros, zeros))
+                    local_ref[i, v, y, slice(b * LANES, (b + 1) * LANES)] = value[b] - slope[b]
         for b in every:
-            out_ref[v - lowest, y, slice(b * LANES, (b + 1) * LANES)] = flux[b]
+            out_ref[v - lowest, y, slice(b * LANES, (b + 1) * LANES)] = inflow[b]
 
 
 def edge_kernel(
@@ -365,15 +368,12 @@
     )(total, tile, live, weight, partly, *(arrived[turn] for turn in late))
     before = moved(tail, "span", 1)
     after = moved(head, "span", -1)
-    pairs = [[i ^ 1 for i in range(sections)], [((i + 1) ^ 1) - 1 for i in range(sections)]]
-    even, odd = (
-        lax.ppermute(
-            message,
-            "stream",
-            [(i, other if 0 <= other < sections else i) for i, other in enumerate(others)],
-        )
-        for message, others in zip((even, odd), pairs)
-    )
+    met = []
+    for message, shift in ((odd, 1), (even, 0)):
+        others = [((i + shift) ^ 1) - shift for i in range(sections)]
+        route = [(i, k if 0 <= k < sections else i) for i, k in enumerate(others)]
+        met.append(lax.ppermute(message, "stream", route))
+    odd, even = met
     assert sections <= 4
     split = (components + 1) // 2
     state_now, parts = filled, []

time: 63.2 us -> 60.7 us (0.960)
  Pallas kernels: 34.7 us -> 32.2 us
    pallas_call x2, Pallas kernels: 15.5 us -> 13 us  [on_device(): call(functools.partial(scan_kernel, lowest), (SMEM, SMEM) + (VMEM,) * 7,...]
  transfers between devices with their start and end apart: 17 -> 17, of which waited for: 6 -> 6; matrix products, arithmetic and copies ran while one was open for 0% -> 0% of each run, Pallas kernels for 44% -> 41%
where the time goes in v4:
time: 60.7 us; the launch traced here: 60.4 us
  Pallas kernels  32.2 us (53%)
  starting transfers between devices  21.4 us (35%)
  waiting for transfers between devices  5.86 us (10%)
  local copies, waits for them, and re-layouts  0.71 us (1%)
    pallas_call x2, Pallas kernels, on_device(): call(functools.partial(scan_kernel, lowest), (SMEM, SMEM) + (VMEM,) * 7,...  13 us
    ppermute x8, starting transfers between devices, moved(): lax.ppermute(value, axis, [(i, (i + distance) % count) for i in range(cou...  11 us
    ppermute x7, starting transfers between devices, on_device(): arrived[turn] = lax.ppermute(tiles, RING, route) if turn else tiles  7.83 us
    pallas_call x2, Pallas kernels, on_device(): call(functools.partial(combine_kernel, lowest, len(begun)), (VMEM,) * 6 +...  4.81 us
    pallas_call x1, Pallas kernels, on_device(): call(growth_kernel, (SMEM, HBM, HBM), (VMEM,) * 5, [hold(state), hold(spe...  4.68 us
    pallas_call x2, Pallas kernels, on_device(): call(functools.partial(gather_kernel, turns), (SMEM, HBM), (VMEM,) * len(...  4.6 us
    ppermute x8, waiting for transfers between devices, moved(): lax.ppermute(value, axis, [(i, (i + distance) % count) for i in range(cou...  3.8 us
    pallas_call x1, Pallas kernels, on_device(): call(functools.partial(last_fill_kernel, late), (VMEM,) + (SMEM,) * 3 + (...  2.92 us
  transfers between devices with their start and end apart: 17, of which 6 were waited for; matrix products, arithmetic and copies ran while one was open for 0% of the time, Pallas kernels for 41%

profile of v4, /device:TPU:0, one launch (start us, length us, event | category | flops | bytes accessed | tf_op | source)
XLA Modules:
  0.0 60.4 jit_solution(16453121258956736895)
XLA Ops:
  0.0 0.7 %copy-done.1 = s32[1,1,1,8,16]{4,3,2,1,0:T(8,128)S(1)} copy-done((s32[1,1,1,8,16]{4,3,2,1,0:T(8,128)S(1)}, s32[1,1,1,8,16]{4,3,2,1,0:T(8,128)}, u32[]{:S(2)}) %copy-start.1) | copy-done | bytes 536
  0.7 2.1 %shard_map.83 = (f32[5,16,512]{2,1,0:T(8,128)S(1)}, f32[5,16,512]{2,1,0:T(8,128)S(1)}, f32[5,16,512]{2,1,0:T(8,128)S(1)}) custom-call(s32[8,16]{1,0:T(8,128)S(1)} %bitcast.12, f32[64,5,16,512]{3,2,1,0:T(8,128)} %bitcast.20), custom_call_target="tpu_custom_call" | custom-call | bytes 3000000 | tf_op jit(solution)/shard_map/pallas_call | solution.py:336
  2.8 3.0 %collective-permute-start = (f32[5,16,512]{2,1,0:T(8,128)S(1)}, f32[5,16,512]{2,1,0:T(8,128)S(1)}, u32[]{:S(2)}, u32[]{:S(2)}) collective-permute-start(f32[5,16,512]{2,1,0:T(8,128)S(1)} %get-tuple-element.38), channel_id=1, source_target_pairs={{0,8},{4,12},{8,0},{12,4},{16,24},{20,28},{24,16},{28,20},{1,9},{5... | collective-permute-start | bytes 491528 | tf_op jit(solution)/shard_map/ppermute | solution.py:345
  5.8 1.5 %collective-permute-start.1 = (f32[5,16,512]{2,1,0:T(8,128)S(1)}, f32[5,16,512]{2,1,0:T(8,128)S(1)}, u32[]{:S(2)}, u32[]{:S(2)}) collective-permute-start(f32[5,16,512]{2,1,0:T(8,128)S(1)} %get-tuple-element.39), channel_id=1, source_target_pairs={{0,16},{4,20},{8,24},{12,28},{16,0},{20,4},{24,8},{28,12},{1,17},{... | collective-permute-start | bytes 491528 | tf_op jit(solution)/shard_map/ppermute | solution.py:345
  7.4 2.5 %shard_map.84 = (f32[5,16,512]{2,1,0:T(8,128)S(1)}, f32[5,16,512]{2,1,0:T(8,128)S(1)}, f32[5,16,512]{2,1,0:T(8,128)S(1)}, f32[5,16,512]{2,1,0:T(8,128)S(1)}, f32[5,16,512]{2,1,0:T(8,128)S(1)}) custom-call(s32[8,16]{1,0:T(8,128)S(1)} %bitcast.13, f32[64,5,16,512]{3,2,1,0:T(8,128)} %bitcast.21), custom_call_target="tpu_custom_call" | custom-call | bytes 3000000 | tf_op jit(solution)/shard_map/pallas_call | solution.py:336
  10.5 1.5 %collective-permute-start.4 = (f32[5,16,512]{2,1,0:T(8,128)S(1)}, f32[5,16,512]{2,1,0:T(8,128)S(1)}, u32[]{:S(2)}, u32[]{:S(2)}) collective-permute-start(f32[5,16,512]{2,1,0:T(8,128)S(1)} %get-tuple-element.42), channel_id=1, source_target_pairs={{0,4},{4,0},{8,12},{12,8},{16,20},{20,16},{24,28},{28,24},{1,5},{5... | collective-permute-start | bytes 491528 | tf_op jit(solution)/shard_map/ppermute | solution.py:345
  12.0 1.1 %collective-permute-start.5 = (f32[5,16,512]{2,1,0:T(8,128)S(1)}, f32[5,16,512]{2,1,0:T(8,128)S(1)}, u32[]{:S(2)}, u32[]{:S(2)}) collective-permute-start(f32[5,16,512]{2,1,0:T(8,128)S(1)} %get-tuple-element.44), channel_id=1, source_target_pairs={{0,20},{4,16},{8,28},{12,24},{16,4},{20,0},{24,12},{28,8},{1,21},{... | collective-permute-start | bytes 491528 | tf_op jit(solution)/shard_map/ppermute | solution.py:345
  13.1 1.6 %collective-permute-done.1.refs_1_ = f32[5,16,512]{2,1,0:T(8,128)S(1)} collective-permute-done((f32[5,16,512]{2,1,0:T(8,128)S(1)}, f32[5,16,512]{2,1,0:T(8,128)S(1)}, u32[]{:S(2)}, u32[]{:S(2)}) %collective-permute-start.1) | collective-permute-done | bytes 163872 | tf_op jit(solution)/shard_map/ppermute | solution.py:345
  14.8 4.7 %shard_map.82 = (f32[64,5,16,512]{3,2,1,0:T(8,128)S(1)}, f32[64,16,512]{2,1,0:T(8,128)S(1)}, f32[64,5,16,512]{3,2,1,0:T(8,128)S(1)}, f32[5,16,512]{2,1,0:T(8,128)S(1)}, f32[5,16,512]{2,1,0:T(8,128)S(1)}) custom-call(f32[5]{0:T(128)S(1)} %copy-done.5, f32[64,5,16,512]{3,2,1,0:T(8,128)} %bitcast.22, f32[64,16,512]{2,1,0:T(8,128)S(1)} %bitcast.11), custom_call_target="tpu_custom_call" | custom-call | bytes 15000000 | tf_op jit(solution)/shard_map/pallas_call | solution.py:348
  19.5 2.0 %shard_map.85.refs_3_ = f32[64,5,16,512]{3,2,1,0:T(8,128)S(1)} custom-call(s32[8,16]{1,0:T(8,128)S(1)} %bitcast.14, s32[8,16]{1,0:T(8,128)S(1)} %bitcast.16, f32[8,16]{1,0:T(8,128)S(1)} %bitcast.18, f32[64,5,16,512]{3,2,1,0:T(8,128)S(1)} %get-tuple-element.37.flow_ref, ...), custom_call_target="tpu_custom_call", output_to_operand_aliasing={{}: (3, {})} | custom-call | bytes 6000000 | tf_op jit(solution)/shard_map/pallas_call | solution.py:355
  22.0 2.9 %shard_map.86 = (f32[64,5,16,512]{3,2,1,0:T(8,128)S(1)}, f32[4,5,16,512]{3,2,1,0:T(8,128)S(1)}, f32[2,5,16,512]{3,2,1,0:T(8,128)S(1)}, f32[2,5,16,512]{3,2,1,0:T...) custom-call(f32[5,16,512]{2,1,0:T(8,128)S(1)} %get-tuple-element.36.total_ref, ...), custom_call_target="tpu_custom_call", output_to_operand_aliasing={{0}: (4, {})} | custom-call | bytes 12000000 | tf_op jit(solution)/shard_map/pallas_call | solution.py:362
  24.9 1.9 %collective-permute-start.9 = (f32[2,5,16,512]{3,2,1,0:T(8,128)S(1)}, f32[2,5,16,512]{3,2,1,0:T(8,128)S(1)}, u32[]{:S(2)}, u32[]{:S(2)}) collective-permute-start(f32[2,5,16,512]{3,2,1,0:T(8,128)S(1)} %get-tuple-element.56), channel_id=1, source_target_pairs={{0,1},{1,0},{2,3},{3,2},{4,5},{5,4},{6,7},{7,6},{8,9},{9,8},{10,11... | collective-permute-start | bytes 983048 | tf_op jit(solution)/shard_map/ppermute | solution.py:375
  27.5 0.9 %collective-permute-start.7 = (f32[5,16,128]{2,1,0:T(8,128)S(1)}, f32[5,16,128]{2,1,0:T(8,128)S(1)}, u32[]{:S(2)}, u32[]{:S(2)}) collective-permute-start(f32[5,16,128]{2,1,0:T(8,128)S(1)} %get-tuple-element.49.tail_ref), channel_id=1, source_target_pairs={{0,4},{4,0},{1,5},{5,1},{2,6},{6,2},{3,7},{7,3},{8,12},{12,8},{9,1... | collective-permute-start | bytes 122888 | tf_op jit(solution)/shard_map/ppermute | solution.py:311
  28.5 0.8 %collective-permute-done.7.before_ref = f32[5,16,128]{2,1,0:T(8,128)S(1)} collective-permute-done((f32[5,16,128]{2,1,0:T(8,128)S(1)}, f32[5,16,128]{2,1,0:T(8,128)S(1)}, u32[]{:S(2)}, u32[]{:S(2)}) %collective-permute-start.7) | collective-permute-done | bytes 40992 | tf_op jit(solution)/shard_map/ppermute | solution.py:311
  29.7 7.7 %shard_map.87 = (f32[64,5,16,512]{3,2,1,0:T(8,128)S(1)}, f32[3,16,512]{2,1,0:T(8,128)S(1)}) custom-call(f32[5]{0:T(128)S(1)} %copy-done.5, f32[5]{0:T(128)S(1)} %copy-done.6, f32[64,5,16,512]{3,2,1,0:T(8,128)S(1)} %get-tuple-element.46.filled_ref, f32[64,5,16,512]{3,2,1,0:T(8,128)S(1)} %get-tuple-element.47.ratio_ref, ...), custom_call_target="tpu_custom_call", output_to_operand_aliasing={{0}: (2, {})} | custom-call | bytes 27000000 | tf_op jit(solution)/shard_map/pallas_call | solution.py:382
  37.5 2.6 %collective-permute-start.13 = (f32[3,16,512]{2,1,0:T(8,128)S(1)}, f32[3,16,512]{2,1,0:T(8,128)S(1)}, u32[]{:S(2)}, u32[]{:S(2)}) collective-permute-start(f32[3,16,512]{2,1,0:T(8,128)S(1)} %get-tuple-element.64), channel_id=1, source_target_pairs={{0,3},{1,0},{2,1},{3,2},{4,7},{5,4},{6,5},{7,6},{8,11},{9,8},{10,9... | collective-permute-start | bytes 294920 | tf_op jit(solution)/shard_map/ppermute | solution.py:311
  40.1 2.8 %collective-permute-start.12 = (f32[3,16,512]{2,1,0:T(8,128)S(1)}, f32[3,16,512]{2,1,0:T(8,128)S(1)}, u32[]{:S(2)}, u32[]{:S(2)}) collective-permute-start(f32[3,16,512]{2,1,0:T(8,128)S(1)} %get-tuple-element.63), channel_id=1, source_target_pairs={{0,2},{1,3},{2,0},{3,1},{4,6},{5,7},{6,4},{7,5},{8,10},{9,11},{10,... | collective-permute-start | bytes 294920 | tf_op jit(solution)/shard_map/ppermute | solution.py:311
  43.0 0.9 %collective-permute-start.11 = (f32[3,16,512]{2,1,0:T(8,128)S(1)}, f32[3,16,512]{2,1,0:T(8,128)S(1)}, u32[]{:S(2)}, u32[]{:S(2)}) collective-permute-start(f32[3,16,512]{2,1,0:T(8,128)S(1)} %get-tuple-element.63), channel_id=1, source_target_pairs={{0,1},{1,2},{2,3},{3,0},{4,5},{5,6},{6,7},{7,4},{8,9},{9,10},{10,1... | collective-permute-start | bytes 294920 | tf_op jit(solution)/shard_map/ppermute | solution.py:311
  43.8 5.3 %shard_map.88 = (f32[64,5,16,512]{3,2,1,0:T(8,128)S(1)}, f32[2,16,512]{2,1,0:T(8,128)S(1)}) custom-call(f32[5]{0:T(128)S(1)} %copy-done.5, f32[5]{0:T(128)S(1)} %copy-done.6, f32[64,5,16,512]{3,2,1,0:T(8,128)S(1)} %get-tuple-element.51.filled_ref, f32[64,5,16,512]{3,2,1,0:T(8,128)S(1)} %get-tuple-element.47.ratio_ref, ...), custom_call_target="tpu_custom_call", output_to_operand_aliasing={{0}: (2, {})} | custom-call | bytes 18000000 | tf_op jit(solution)/shard_map/pallas_call | solution.py:382
  49.2 3.0 %collective-permute-start.16 = (f32[2,16,512]{2,1,0:T(8,128)S(1)}, f32[2,16,512]{2,1,0:T(8,128)S(1)}, u32[]{:S(2)}, u32[]{:S(2)}) collective-permute-start(f32[2,16,512]{2,1,0:T(8,128)S(1)} %get-tuple-element.66), channel_id=1, source_target_pairs={{0,3},{1,0},{2,1},{3,2},{4,7},{5,4},{6,5},{7,6},{8,11},{9,8},{10,9... | collective-permute-start | bytes 196616 | tf_op jit(solution)/shard_map/ppermute | solution.py:311
  52.9 2.7 %shard_map.91.refs_0_ = f32[64,5,16,512]{3,2,1,0:T(8,128)} custom-call(f32[64,5,16,512]{3,2,1,0:T(8,128)S(1)} %get-tuple-element.52.local_ref, f32[64,5,16,512]{3,2,1,0:T(8,128)S(1)} %get-tuple-element.47.ratio_ref, f32[3,16,512]{2,1,0:T(8,128)S(1)} %get-tuple-element.61.first_ref, f32[3,16,512]{2,1,0:T(8,128)S(1)} %get-tuple-element.62.last_ref, ...), custom_call_target="tpu_custom_call" | custom-call | bytes 9000000 | tf_op jit(solution)/shard_map/pallas_call | solution.py:399
  55.7 1.9 %collective-permute-done.15.refs_2_ = f32[2,16,512]{2,1,0:T(8,128)S(1)} collective-permute-done((f32[2,16,512]{2,1,0:T(8,128)S(1)}, f32[2,16,512]{2,1,0:T(8,128)S(1)}, u32[]{:S(2)}, u32[]{:S(2)}) %collective-permute-start.15) | collective-permute-done | bytes 65568 | tf_op jit(solution)/shard_map/ppermute | solution.py:311
  57.6 0.7 %collective-permute-done.14.refs_1_ = f32[2,16,512]{2,1,0:T(8,128)S(1)} collective-permute-done((f32[2,16,512]{2,1,0:T(8,128)S(1)}, f32[2,16,512]{2,1,0:T(8,128)S(1)}, u32[]{:S(2)}, u32[]{:S(2)}) %collective-permute-start.14) | collective-permute-done | bytes 65568 | tf_op jit(solution)/shard_map/ppermute | solution.py:311
  58.3 2.1 %shard_map.92 = f32[64,5,16,512]{3,2,1,0:T(8,128)} custom-call(f32[64,5,16,512]{3,2,1,0:T(8,128)S(1)} %get-tuple-element.52.local_ref, f32[64,5,16,512]{3,2,1,0:T(8,128)S(1)} %get-tuple-element.47.ratio_ref, f32[2,16,512]{2,1,0:T(8,128)S(1)} %get-tuple-element.58.first_ref, ...), custom_call_target="tpu_custom_call", output_to_operand_aliasing={{}: (6, {})} | custom-call | bytes 6000000 | tf_op jit(solution)/shard_map/pallas_call | solution.py:399
  (35 shorter events, 3.0 us)
Async XLA Ops:
  0.0 0.7 %copy-start.1 = (s32[1,1,1,8,16]{4,3,2,1,0:T(8,128)S(1)}, s32[1,1,1,8,16]{4,3,2,1,0:T(8,128)}, u32[]{:S(2)}) copy-start(s32[1,1,1,8,16]{4,3,2,1,0:T(8,128)} %param.12) | copy-start | bytes 1540
  0.7 14.1 %copy-start = (f32[1,64,16,512]{3,2,1,0:T(8,128)S(1)}, f32[1,64,16,512]{3,2,1,0:T(8,128)}, u32[]{:S(2)}) copy-start(f32[1,64,16,512]{3,2,1,0:T(8,128)} %param.9) | copy-start | bytes 6291460
  0.7 14.1 %copy-start.5 = (f32[5]{0:T(128)S(1)}, f32[5]{0:T(128)}, u32[]{:S(2)}) copy-start(f32[5]{0:T(128)} %scale_ref.5) | copy-start | bytes 64
  2.8 9.3 %collective-permute-start = (f32[5,16,512]{2,1,0:T(8,128)S(1)}, f32[5,16,512]{2,1,0:T(8,128)S(1)}, u32[]{:S(2)}, u32[]{:S(2)}) collective-permute-start(f32[5,16,512]{2,1,0:T(8,128)S(1)} %get-tuple-element.38), channel_id=1, source_target_pairs={{0,8},{4,12},{8,0},{12,4},{16,24},{20,28},{24,16},{28,20},{1,9},{5... | collective-permute-start | bytes 491528 | tf_op jit(solution)/shard_map/ppermute | solution.py:345
  5.8 9.0 %collective-permute-start.1 = (f32[5,16,512]{2,1,0:T(8,128)S(1)}, f32[5,16,512]{2,1,0:T(8,128)S(1)}, u32[]{:S(2)}, u32[]{:S(2)}) collective-permute-start(f32[5,16,512]{2,1,0:T(8,128)S(1)} %get-tuple-element.39), channel_id=1, source_target_pairs={{0,16},{4,20},{8,24},{12,28},{16,0},{20,4},{24,8},{28,12},{1,17},{... | collective-permute-start | bytes 491528 | tf_op jit(solution)/shard_map/ppermute | solution.py:345
  7.3 12.2 %copy-start.2 = (s32[1,1,1,8,16]{4,3,2,1,0:T(8,128)S(1)}, s32[1,1,1,8,16]{4,3,2,1,0:T(8,128)}, u32[]{:S(2)}) copy-start(s32[1,1,1,8,16]{4,3,2,1,0:T(8,128)} %param.13) | copy-start | bytes 1540
  7.3 12.2 %copy-start.3 = (s32[1,1,1,8,16]{4,3,2,1,0:T(8,128)S(1)}, s32[1,1,1,8,16]{4,3,2,1,0:T(8,128)}, u32[]{:S(2)}) copy-start(s32[1,1,1,8,16]{4,3,2,1,0:T(8,128)} %param.14) | copy-start | bytes 1540
  7.3 12.2 %copy-start.4 = (f32[1,1,1,8,16]{4,3,2,1,0:T(8,128)S(1)}, f32[1,1,1,8,16]{4,3,2,1,0:T(8,128)}, u32[]{:S(2)}) copy-start(f32[1,1,1,8,16]{4,3,2,1,0:T(8,128)} %param.15) | copy-start | bytes 1540
  7.3 12.2 %collective-permute-start.2 = (f32[5,16,512]{2,1,0:T(8,128)S(1)}, f32[5,16,512]{2,1,0:T(8,128)S(1)}, u32[]{:S(2)}, u32[]{:S(2)}) collective-permute-start(f32[5,16,512]{2,1,0:T(8,128)S(1)} %get-tuple-element.40), channel_id=1, source_target_pairs={{0,24},{4,28},{8,16},{12,20},{16,8},{20,12},{24,0},{28,4},{1,25},{... | collective-permute-start | bytes 491528 | tf_op jit(solution)/shard_map/ppermute | solution.py:345
  9.9 9.6 %collective-permute-start.3 = (f32[5,16,512]{2,1,0:T(8,128)S(1)}, f32[5,16,512]{2,1,0:T(8,128)S(1)}, u32[]{:S(2)}, u32[]{:S(2)}) collective-permute-start(f32[5,16,512]{2,1,0:T(8,128)S(1)} %get-tuple-element.41), channel_id=1, source_target_pairs={{0,12},{4,8},{8,4},{12,0},{16,28},{20,24},{24,20},{28,16},{1,13},{... | collective-permute-start | bytes 491528 | tf_op jit(solution)/shard_map/ppermute | solution.py:345
  10.5 9.0 %collective-permute-start.4 = (f32[5,16,512]{2,1,0:T(8,128)S(1)}, f32[5,16,512]{2,1,0:T(8,128)S(1)}, u32[]{:S(2)}, u32[]{:S(2)}) collective-permute-start(f32[5,16,512]{2,1,0:T(8,128)S(1)} %get-tuple-element.42), channel_id=1, source_target_pairs={{0,4},{4,0},{8,12},{12,8},{16,20},{20,16},{24,28},{28,24},{1,5},{5... | collective-permute-start | bytes 491528 | tf_op jit(solution)/shard_map/ppermute | solution.py:345
  12.0 10.0 %collective-permute-start.5 = (f32[5,16,512]{2,1,0:T(8,128)S(1)}, f32[5,16,512]{2,1,0:T(8,128)S(1)}, u32[]{:S(2)}, u32[]{:S(2)}) collective-permute-start(f32[5,16,512]{2,1,0:T(8,128)S(1)} %get-tuple-element.44), channel_id=1, source_target_pairs={{0,20},{4,16},{8,28},{12,24},{16,4},{20,0},{24,12},{28,8},{1,21},{... | collective-permute-start | bytes 491528 | tf_op jit(solution)/shard_map/ppermute | solution.py:345
  14.8 7.2 %collective-permute-start.6 = (f32[5,16,512]{2,1,0:T(8,128)S(1)}, f32[5,16,512]{2,1,0:T(8,128)S(1)}, u32[]{:S(2)}, u32[]{:S(2)}) collective-permute-start(f32[5,16,512]{2,1,0:T(8,128)S(1)} %get-tuple-element.45), channel_id=1, source_target_pairs={{0,28},{4,24},{8,20},{12,16},{16,12},{20,8},{24,4},{28,0},{1,29},{... | collective-permute-start | bytes 491528 | tf_op jit(solution)/shard_map/ppermute | solution.py:345
  21.6 8.1 %copy-start.6 = (f32[5]{0:T(128)S(1)}, f32[5]{0:T(128)}, u32[]{:S(2)}) copy-start(f32[5]{0:T(128)} %span_ref.3) | copy-start | bytes 64
  24.9 12.4 %collective-permute-start.9 = (f32[2,5,16,512]{3,2,1,0:T(8,128)S(1)}, f32[2,5,16,512]{3,2,1,0:T(8,128)S(1)}, u32[]{:S(2)}, u32[]{:S(2)}) collective-permute-start(f32[2,5,16,512]{3,2,1,0:T(8,128)S(1)} %get-tuple-element.56), channel_id=1, source_target_pairs={{0,1},{1,0},{2,3},{3,2},{4,5},{5,4},{6,7},{7,6},{8,9},{9,8},{10,11... | collective-permute-start | bytes 983048 | tf_op jit(solution)/shard_map/ppermute | solution.py:375
  26.8 10.5 %collective-permute-start.10 = (f32[2,5,16,512]{3,2,1,0:T(8,128)S(1)}, f32[2,5,16,512]{3,2,1,0:T(8,128)S(1)}, u32[]{:S(2)}, u32[]{:S(2)}) collective-permute-start(f32[2,5,16,512]{3,2,1,0:T(8,128)S(1)} %get-tuple-element.57), channel_id=1, source_target_pairs={{0,0},{1,2},{2,1},{3,3},{4,4},{5,6},{6,5},{7,7},{8,8},{9,10},{10,9... | collective-permute-start | bytes 983048 | tf_op jit(solution)/shard_map/ppermute | solution.py:375
  27.5 1.8 %collective-permute-start.7 = (f32[5,16,128]{2,1,0:T(8,128)S(1)}, f32[5,16,128]{2,1,0:T(8,128)S(1)}, u32[]{:S(2)}, u32[]{:S(2)}) collective-permute-start(f32[5,16,128]{2,1,0:T(8,128)S(1)} %get-tuple-element.49.tail_ref), channel_id=1, source_target_pairs={{0,4},{4,0},{1,5},{5,1},{2,6},{6,2},{3,7},{7,3},{8,12},{12,8},{9,1... | collective-permute-start | bytes 122888 | tf_op jit(solution)/shard_map/ppermute | solution.py:311
  28.4 1.2 %collective-permute-start.8 = (f32[5,16,128]{2,1,0:T(8,128)S(1)}, f32[5,16,128]{2,1,0:T(8,128)S(1)}, u32[]{:S(2)}, u32[]{:S(2)}) collective-permute-start(f32[5,16,128]{2,1,0:T(8,128)S(1)} %get-tuple-element.50.head_ref), channel_id=1, source_target_pairs={{0,4},{4,0},{1,5},{5,1},{2,6},{6,2},{3,7},{7,3},{8,12},{12,8},{9,1... | collective-permute-start | bytes 122888 | tf_op jit(solution)/shard_map/ppermute | solution.py:311
  37.5 14.8 %collective-permute-start.13 = (f32[3,16,512]{2,1,0:T(8,128)S(1)}, f32[3,16,512]{2,1,0:T(8,128)S(1)}, u32[]{:S(2)}, u32[]{:S(2)}) collective-permute-start(f32[3,16,512]{2,1,0:T(8,128)S(1)} %get-tuple-element.64), channel_id=1, source_target_pairs={{0,3},{1,0},{2,1},{3,2},{4,7},{5,4},{6,5},{7,6},{8,11},{9,8},{10,9... | collective-permute-start | bytes 294920 | tf_op jit(solution)/shard_map/ppermute | solution.py:311
  40.1 12.8 %collective-permute-start.12 = (f32[3,16,512]{2,1,0:T(8,128)S(1)}, f32[3,16,512]{2,1,0:T(8,128)S(1)}, u32[]{:S(2)}, u32[]{:S(2)}) collective-permute-start(f32[3,16,512]{2,1,0:T(8,128)S(1)} %get-tuple-element.63), channel_id=1, source_target_pairs={{0,2},{1,3},{2,0},{3,1},{4,6},{5,7},{6,4},{7,5},{8,10},{9,11},{10,... | collective-permute-start | bytes 294920 | tf_op jit(solution)/shard_map/ppermute | solution.py:311
  43.0 9.9 %collective-permute-start.11 = (f32[3,16,512]{2,1,0:T(8,128)S(1)}, f32[3,16,512]{2,1,0:T(8,128)S(1)}, u32[]{:S(2)}, u32[]{:S(2)}) collective-permute-start(f32[3,16,512]{2,1,0:T(8,128)S(1)} %get-tuple-element.63), channel_id=1, source_target_pairs={{0,1},{1,2},{2,3},{3,0},{4,5},{5,6},{6,7},{7,4},{8,9},{9,10},{10,1... | collective-permute-start | bytes 294920 | tf_op jit(solution)/shard_map/ppermute | solution.py:311
  49.2 6.4 %collective-permute-start.16 = (f32[2,16,512]{2,1,0:T(8,128)S(1)}, f32[2,16,512]{2,1,0:T(8,128)S(1)}, u32[]{:S(2)}, u32[]{:S(2)}) collective-permute-start(f32[2,16,512]{2,1,0:T(8,128)S(1)} %get-tuple-element.66), channel_id=1, source_target_pairs={{0,3},{1,0},{2,1},{3,2},{4,7},{5,4},{6,5},{7,6},{8,11},{9,8},{10,9... | collective-permute-start | bytes 196616 | tf_op jit(solution)/shard_map/ppermute | solution.py:311
  52.2 5.3 %collective-permute-start.15 = (f32[2,16,512]{2,1,0:T(8,128)S(1)}, f32[2,16,512]{2,1,0:T(8,128)S(1)}, u32[]{:S(2)}, u32[]{:S(2)}) collective-permute-start(f32[2,16,512]{2,1,0:T(8,128)S(1)} %get-tuple-element.65), channel_id=1, source_target_pairs={{0,2},{1,3},{2,0},{3,1},{4,6},{5,7},{6,4},{7,5},{8,10},{9,11},{10,... | collective-permute-start | bytes 196616 | tf_op jit(solution)/shard_map/ppermute | solution.py:311
  52.3 6.1 %collective-permute-start.14 = (f32[2,16,512]{2,1,0:T(8,128)S(1)}, f32[2,16,512]{2,1,0:T(8,128)S(1)}, u32[]{:S(2)}, u32[]{:S(2)}) collective-permute-start(f32[2,16,512]{2,1,0:T(8,128)S(1)} %get-tuple-element.65), channel_id=1, source_target_pairs={{0,1},{1,2},{2,3},{3,0},{4,5},{5,6},{6,7},{7,4},{8,9},{9,10},{10,1... | collective-permute-start | bytes 196616 | tf_op jit(solution)/shard_map/ppermute | solution.py:311

commit v5 on v4

--- a/solution.py
+++ b/solution.py
@@ -10,7 +10,7 @@
 LANES = 128
 SUB = 8
 STEPS = 16
-LAG = 6
+LAG = 7
 F32 = jnp.float32
 
 
@@ -375,7 +375,7 @@
         met.append(lax.ppermute(message, "stream", route))
     odd, even = met
     assert sections <= 4
-    split = (components + 1) // 2
+    split = max(components - 1, 1)
     state_now, parts = filled, []
     for lowest, size in ((0, split), (split, components - split)):
         some = (size, rows_y, width_z)
@@ -406,7 +406,7 @@
                 pltpu.SemaphoreType.DMA,
             ],
             aliases={6: 0} if begun else None,
-            limit=10 << 20,
+            limit=12 << 20,
             micros=some[0],
         )(state_now, ratio, first_slope, last_slope, even, odd, *begun, *fluxes)
     (done,) = begun

time: 60.7 us -> 64.3 us (1.059)
  starting transfers between devices: 21.4 us -> 25.6 us
    ppermute x8, starting transfers between devices: 11 us -> 15.2 us  [moved(): lax.ppermute(value, axis, [(i, (i + distance) % count) for i in range(cou...]
  transfers between devices with their start and end apart: 17 -> 17, of which waited for: 6 -> 5; matrix products, arithmetic and copies ran while one was open for 0% -> 0% of each run, Pallas kernels for 41% -> 40%
where the time goes in v5:
time: 64.3 us; the launch traced here: 63.9 us
  Pallas kernels  31.8 us (49%)
  starting transfers between devices  25.6 us (40%)
  waiting for transfers between devices  5.7 us (9%)
  local copies, waits for them, and re-layouts  0.71 us (1%)
    ppermute x8, starting transfers between devices, moved(): lax.ppermute(value, axis, [(i, (i + distance) % count) for i in range(cou...  15.2 us
    pallas_call x2, Pallas kernels, on_device(): call(functools.partial(scan_kernel, lowest), (SMEM, SMEM) + (VMEM,) * 7,...  12.6 us
    ppermute x7, starting transfers between devices, on_device(): arrived[turn] = lax.ppermute(tiles, RING, route) if turn else tiles  7.83 us
    pallas_call x2, Pallas kernels, on_device(): call(functools.partial(combine_kernel, lowest, len(begun)), (VMEM,) * 6 +...  4.78 us
    pallas_call x1, Pallas kernels, on_device(): call(growth_kernel, (SMEM, HBM, HBM), (VMEM,) * 5, [hold(state), hold(spe...  4.68 us
    pallas_call x2, Pallas kernels, on_device(): call(functools.partial(gather_kernel, turns), (SMEM, HBM), (VMEM,) * len(...  4.6 us
    ppermute x8, waiting for transfers between devices, moved(): lax.ppermute(value, axis, [(i, (i + distance) % count) for i in range(cou...  3.64 us
    pallas_call x1, Pallas kernels, on_device(): call(functools.partial(last_fill_kernel, late), (VMEM,) + (SMEM,) * 3 + (...  2.92 us
  transfers between devices with their start and end apart: 17, of which 5 were waited for; matrix products, arithmetic and copies ran while one was open for 0% of the time, Pallas kernels for 40%

profile of v5, /device:TPU:0, one launch (start us, length us, event | category | flops | bytes accessed | tf_op | source)
XLA Modules:
  0.0 63.9 jit_solution(14993158193936661953)
XLA Ops:
  0.0 0.7 %copy-done.1 = s32[1,1,1,8,16]{4,3,2,1,0:T(8,128)S(1)} copy-done((s32[1,1,1,8,16]{4,3,2,1,0:T(8,128)S(1)}, s32[1,1,1,8,16]{4,3,2,1,0:T(8,128)}, u32[]{:S(2)}) %copy-start.1) | copy-done | bytes 536
  0.7 2.1 %shard_map.83 = (f32[5,16,512]{2,1,0:T(8,128)S(1)}, f32[5,16,512]{2,1,0:T(8,128)S(1)}, f32[5,16,512]{2,1,0:T(8,128)S(1)}) custom-call(s32[8,16]{1,0:T(8,128)S(1)} %bitcast.12, f32[64,5,16,512]{3,2,1,0:T(8,128)} %bitcast.20), custom_call_target="tpu_custom_call" | custom-call | bytes 3000000 | tf_op jit(solution)/shard_map/pallas_call | solution.py:336
  2.8 3.0 %collective-permute-start = (f32[5,16,512]{2,1,0:T(8,128)S(1)}, f32[5,16,512]{2,1,0:T(8,128)S(1)}, u32[]{:S(2)}, u32[]{:S(2)}) collective-permute-start(f32[5,16,512]{2,1,0:T(8,128)S(1)} %get-tuple-element.38), channel_id=1, source_target_pairs={{0,8},{4,12},{8,0},{12,4},{16,24},{20,28},{24,16},{28,20},{1,9},{5... | collective-permute-start | bytes 491528 | tf_op jit(solution)/shard_map/ppermute | solution.py:345
  5.8 1.5 %collective-permute-start.1 = (f32[5,16,512]{2,1,0:T(8,128)S(1)}, f32[5,16,512]{2,1,0:T(8,128)S(1)}, u32[]{:S(2)}, u32[]{:S(2)}) collective-permute-start(f32[5,16,512]{2,1,0:T(8,128)S(1)} %get-tuple-element.39), channel_id=1, source_target_pairs={{0,16},{4,20},{8,24},{12,28},{16,0},{20,4},{24,8},{28,12},{1,17},{... | collective-permute-start | bytes 491528 | tf_op jit(solution)/shard_map/ppermute | solution.py:345
  7.4 2.5 %shard_map.84 = (f32[5,16,512]{2,1,0:T(8,128)S(1)}, f32[5,16,512]{2,1,0:T(8,128)S(1)}, f32[5,16,512]{2,1,0:T(8,128)S(1)}, f32[5,16,512]{2,1,0:T(8,128)S(1)}, f32[5,16,512]{2,1,0:T(8,128)S(1)}) custom-call(s32[8,16]{1,0:T(8,128)S(1)} %bitcast.13, f32[64,5,16,512]{3,2,1,0:T(8,128)} %bitcast.21), custom_call_target="tpu_custom_call" | custom-call | bytes 3000000 | tf_op jit(solution)/shard_map/pallas_call | solution.py:336
  10.5 1.5 %collective-permute-start.4 = (f32[5,16,512]{2,1,0:T(8,128)S(1)}, f32[5,16,512]{2,1,0:T(8,128)S(1)}, u32[]{:S(2)}, u32[]{:S(2)}) collective-permute-start(f32[5,16,512]{2,1,0:T(8,128)S(1)} %get-tuple-element.42), channel_id=1, source_target_pairs={{0,4},{4,0},{8,12},{12,8},{16,20},{20,16},{24,28},{28,24},{1,5},{5... | collective-permute-start | bytes 491528 | tf_op jit(solution)/shard_map/ppermute | solution.py:345
  12.0 1.1 %collective-permute-start.5 = (f32[5,16,512]{2,1,0:T(8,128)S(1)}, f32[5,16,512]{2,1,0:T(8,128)S(1)}, u32[]{:S(2)}, u32[]{:S(2)}) collective-permute-start(f32[5,16,512]{2,1,0:T(8,128)S(1)} %get-tuple-element.44), channel_id=1, source_target_pairs={{0,20},{4,16},{8,28},{12,24},{16,4},{20,0},{24,12},{28,8},{1,21},{... | collective-permute-start | bytes 491528 | tf_op jit(solution)/shard_map/ppermute | solution.py:345
  13.1 1.6 %collective-permute-done.1.refs_1_ = f32[5,16,512]{2,1,0:T(8,128)S(1)} collective-permute-done((f32[5,16,512]{2,1,0:T(8,128)S(1)}, f32[5,16,512]{2,1,0:T(8,128)S(1)}, u32[]{:S(2)}, u32[]{:S(2)}) %collective-permute-start.1) | collective-permute-done | bytes 163872 | tf_op jit(solution)/shard_map/ppermute | solution.py:345
  14.8 4.7 %shard_map.82 = (f32[64,5,16,512]{3,2,1,0:T(8,128)S(1)}, f32[64,16,512]{2,1,0:T(8,128)S(1)}, f32[64,5,16,512]{3,2,1,0:T(8,128)S(1)}, f32[5,16,512]{2,1,0:T(8,128)S(1)}, f32[5,16,512]{2,1,0:T(8,128)S(1)}) custom-call(f32[5]{0:T(128)S(1)} %copy-done.5, f32[64,5,16,512]{3,2,1,0:T(8,128)} %bitcast.22, f32[64,16,512]{2,1,0:T(8,128)S(1)} %bitcast.11), custom_call_target="tpu_custom_call" | custom-call | bytes 15000000 | tf_op jit(solution)/shard_map/pallas_call | solution.py:348
  19.5 2.0 %shard_map.85.refs_3_ = f32[64,5,16,512]{3,2,1,0:T(8,128)S(1)} custom-call(s32[8,16]{1,0:T(8,128)S(1)} %bitcast.14, s32[8,16]{1,0:T(8,128)S(1)} %bitcast.16, f32[8,16]{1,0:T(8,128)S(1)} %bitcast.18, f32[64,5,16,512]{3,2,1,0:T(8,128)S(1)} %get-tuple-element.37.flow_ref, ...), custom_call_target="tpu_custom_call", output_to_operand_aliasing={{}: (3, {})} | custom-call | bytes 6000000 | tf_op jit(solution)/shard_map/pallas_call | solution.py:355
  22.0 2.9 %shard_map.86 = (f32[64,5,16,512]{3,2,1,0:T(8,128)S(1)}, f32[4,5,16,512]{3,2,1,0:T(8,128)S(1)}, f32[2,5,16,512]{3,2,1,0:T(8,128)S(1)}, f32[2,5,16,512]{3,2,1,0:T...) custom-call(f32[5,16,512]{2,1,0:T(8,128)S(1)} %get-tuple-element.36.total_ref, ...), custom_call_target="tpu_custom_call", output_to_operand_aliasing={{0}: (4, {})} | custom-call | bytes 12000000 | tf_op jit(solution)/shard_map/pallas_call | solution.py:362
  24.9 1.9 %collective-permute-start.9 = (f32[2,5,16,512]{3,2,1,0:T(8,128)S(1)}, f32[2,5,16,512]{3,2,1,0:T(8,128)S(1)}, u32[]{:S(2)}, u32[]{:S(2)}) collective-permute-start(f32[2,5,16,512]{3,2,1,0:T(8,128)S(1)} %get-tuple-element.56), channel_id=1, source_target_pairs={{0,1},{1,0},{2,3},{3,2},{4,5},{5,4},{6,7},{7,6},{8,9},{9,8},{10,11... | collective-permute-start | bytes 983048 | tf_op jit(solution)/shard_map/ppermute | solution.py:375
  26.8 0.7 %collective-permute-start.10 = (f32[2,5,16,512]{3,2,1,0:T(8,128)S(1)}, f32[2,5,16,512]{3,2,1,0:T(8,128)S(1)}, u32[]{:S(2)}, u32[]{:S(2)}) collective-permute-start(f32[2,5,16,512]{3,2,1,0:T(8,128)S(1)} %get-tuple-element.57), channel_id=1, source_target_pairs={{0,0},{1,2},{2,1},{3,3},{4,4},{5,6},{6,5},{7,7},{8,8},{9,10},{10,9... | collective-permute-start | bytes 983048 | tf_op jit(solution)/shard_map/ppermute | solution.py:375
  27.5 0.9 %collective-permute-start.7 = (f32[5,16,128]{2,1,0:T(8,128)S(1)}, f32[5,16,128]{2,1,0:T(8,128)S(1)}, u32[]{:S(2)}, u32[]{:S(2)}) collective-permute-start(f32[5,16,128]{2,1,0:T(8,128)S(1)} %get-tuple-element.49.tail_ref), channel_id=1, source_target_pairs={{0,4},{4,0},{1,5},{5,1},{2,6},{6,2},{3,7},{7,3},{8,12},{12,8},{9,1... | collective-permute-start | bytes 122888 | tf_op jit(solution)/shard_map/ppermute | solution.py:311
  28.5 0.8 %collective-permute-done.7.before_ref = f32[5,16,128]{2,1,0:T(8,128)S(1)} collective-permute-done((f32[5,16,128]{2,1,0:T(8,128)S(1)}, f32[5,16,128]{2,1,0:T(8,128)S(1)}, u32[]{:S(2)}, u32[]{:S(2)}) %collective-permute-start.7) | collective-permute-done | bytes 40992 | tf_op jit(solution)/shard_map/ppermute | solution.py:311
  29.7 9.7 %shard_map.87 = (f32[64,5,16,512]{3,2,1,0:T(8,128)S(1)}, f32[4,16,512]{2,1,0:T(8,128)S(1)}) custom-call(f32[5]{0:T(128)S(1)} %copy-done.5, f32[5]{0:T(128)S(1)} %copy-done.6, f32[64,5,16,512]{3,2,1,0:T(8,128)S(1)} %get-tuple-element.46.filled_ref, f32[64,5,16,512]{3,2,1,0:T(8,128)S(1)} %get-tuple-element.47.ratio_ref, ...), custom_call_target="tpu_custom_call", output_to_operand_aliasing={{0}: (2, {})} | custom-call | bytes 36000000 | tf_op jit(solution)/shard_map/pallas_call | solution.py:382
  39.5 2.6 %collective-permute-start.13 = (f32[4,16,512]{2,1,0:T(8,128)S(1)}, f32[4,16,512]{2,1,0:T(8,128)S(1)}, u32[]{:S(2)}, u32[]{:S(2)}) collective-permute-start(f32[4,16,512]{2,1,0:T(8,128)S(1)} %get-tuple-element.64), channel_id=1, source_target_pairs={{0,3},{1,0},{2,1},{3,2},{4,7},{5,4},{6,5},{7,6},{8,11},{9,8},{10,9... | collective-permute-start | bytes 393224 | tf_op jit(solution)/shard_map/ppermute | solution.py:311
  42.2 2.8 %collective-permute-start.12 = (f32[4,16,512]{2,1,0:T(8,128)S(1)}, f32[4,16,512]{2,1,0:T(8,128)S(1)}, u32[]{:S(2)}, u32[]{:S(2)}) collective-permute-start(f32[4,16,512]{2,1,0:T(8,128)S(1)} %get-tuple-element.63), channel_id=1, source_target_pairs={{0,2},{1,3},{2,0},{3,1},{4,6},{5,7},{6,4},{7,5},{8,10},{9,11},{10,... | collective-permute-start | bytes 393224 | tf_op jit(solution)/shard_map/ppermute | solution.py:311
  45.3 2.9 %shard_map.88 = (f32[64,5,16,512]{3,2,1,0:T(8,128)S(1)}, f32[1,16,512]{2,1,0:T(8,128)S(1)}) custom-call(f32[5]{0:T(128)S(1)} %copy-done.5, f32[5]{0:T(128)S(1)} %copy-done.6, f32[64,5,16,512]{3,2,1,0:T(8,128)S(1)} %get-tuple-element.51.filled_ref, f32[64,5,16,512]{3,2,1,0:T(8,128)S(1)} %get-tuple-element.47.ratio_ref, ...), custom_call_target="tpu_custom_call", output_to_operand_aliasing={{0}: (2, {})} | custom-call | bytes 9000000 | tf_op jit(solution)/shard_map/pallas_call | solution.py:382
  48.2 3.6 %collective-permute-start.16 = (f32[1,16,512]{2,1,0:T(8,128)S(1)}, f32[1,16,512]{2,1,0:T(8,128)S(1)}, u32[]{:S(2)}, u32[]{:S(2)}) collective-permute-start(f32[1,16,512]{2,1,0:T(8,128)S(1)} %get-tuple-element.66), channel_id=1, source_target_pairs={{0,3},{1,0},{2,1},{3,2},{4,7},{5,4},{6,5},{7,6},{8,11},{9,8},{10,9... | collective-permute-start | bytes 98312 | tf_op jit(solution)/shard_map/ppermute | solution.py:311
  51.8 4.8 %collective-permute-start.14 = (f32[1,16,512]{2,1,0:T(8,128)S(1)}, f32[1,16,512]{2,1,0:T(8,128)S(1)}, u32[]{:S(2)}, u32[]{:S(2)}) collective-permute-start(f32[1,16,512]{2,1,0:T(8,128)S(1)} %get-tuple-element.65), channel_id=1, source_target_pairs={{0,1},{1,2},{2,3},{3,0},{4,5},{5,6},{6,7},{7,4},{8,9},{9,10},{10,1... | collective-permute-start | bytes 98312 | tf_op jit(solution)/shard_map/ppermute | solution.py:311
  56.6 2.5 %collective-permute-done.12.refs_1_ = f32[4,16,512]{2,1,0:T(8,128)S(1)} collective-permute-done((f32[4,16,512]{2,1,0:T(8,128)S(1)}, f32[4,16,512]{2,1,0:T(8,128)S(1)}, u32[]{:S(2)}, u32[]{:S(2)}) %collective-permute-start.12) | collective-permute-done | bytes 131104 | tf_op jit(solution)/shard_map/ppermute | solution.py:311
  59.1 3.4 %shard_map.91.refs_0_ = f32[64,5,16,512]{3,2,1,0:T(8,128)} custom-call(f32[64,5,16,512]{3,2,1,0:T(8,128)S(1)} %get-tuple-element.52.local_ref, f32[64,5,16,512]{3,2,1,0:T(8,128)S(1)} %get-tuple-element.47.ratio_ref, f32[4,16,512]{2,1,0:T(8,128)S(1)} %get-tuple-element.61.first_ref, f32[4,16,512]{2,1,0:T(8,128)S(1)} %get-tuple-element.62.last_ref, ...), custom_call_target="tpu_custom_call" | custom-call | bytes 12000000 | tf_op jit(solution)/shard_map/pallas_call | solution.py:399
  62.6 1.4 %shard_map.92 = f32[64,5,16,512]{3,2,1,0:T(8,128)} custom-call(f32[64,5,16,512]{3,2,1,0:T(8,128)S(1)} %get-tuple-element.52.local_ref, f32[64,5,16,512]{3,2,1,0:T(8,128)S(1)} %get-tuple-element.47.ratio_ref, f32[1,16,512]{2,1,0:T(8,128)S(1)} %get-tuple-element.58.first_ref, ...), custom_call_target="tpu_custom_call", output_to_operand_aliasing={{}: (6, {})} | custom-call | bytes 3000000 | tf_op jit(solution)/shard_map/pallas_call | solution.py:399
  (35 shorter events, 2.0 us)
Async XLA Ops:
  0.0 0.7 %copy-start.1 = (s32[1,1,1,8,16]{4,3,2,1,0:T(8,128)S(1)}, s32[1,1,1,8,16]{4,3,2,1,0:T(8,128)}, u32[]{:S(2)}) copy-start(s32[1,1,1,8,16]{4,3,2,1,0:T(8,128)} %param.12) | copy-start | bytes 1540
  0.7 14.1 %copy-start = (f32[1,64,16,512]{3,2,1,0:T(8,128)S(1)}, f32[1,64,16,512]{3,2,1,0:T(8,128)}, u32[]{:S(2)}) copy-start(f32[1,64,16,512]{3,2,1,0:T(8,128)} %param.9) | copy-start | bytes 6291460
  0.7 14.1 %copy-start.5 = (f32[5]{0:T(128)S(1)}, f32[5]{0:T(128)}, u32[]{:S(2)}) copy-start(f32[5]{0:T(128)} %scale_ref.5) | copy-start | bytes 64
  2.8 9.3 %collective-permute-start = (f32[5,16,512]{2,1,0:T(8,128)S(1)}, f32[5,16,512]{2,1,0:T(8,128)S(1)}, u32[]{:S(2)}, u32[]{:S(2)}) collective-permute-start(f32[5,16,512]{2,1,0:T(8,128)S(1)} %get-tuple-element.38), channel_id=1, source_target_pairs={{0,8},{4,12},{8,0},{12,4},{16,24},{20,28},{24,16},{28,20},{1,9},{5... | collective-permute-start | bytes 491528 | tf_op jit(solution)/shard_map/ppermute | solution.py:345
  5.8 9.0 %collective-permute-start.1 = (f32[5,16,512]{2,1,0:T(8,128)S(1)}, f32[5,16,512]{2,1,0:T(8,128)S(1)}, u32[]{:S(2)}, u32[]{:S(2)}) collective-permute-start(f32[5,16,512]{2,1,0:T(8,128)S(1)} %get-tuple-element.39), channel_id=1, source_target_pairs={{0,16},{4,20},{8,24},{12,28},{16,0},{20,4},{24,8},{28,12},{1,17},{... | collective-permute-start | bytes 491528 | tf_op jit(solution)/shard_map/ppermute | solution.py:345
  7.3 12.2 %copy-start.2 = (s32[1,1,1,8,16]{4,3,2,1,0:T(8,128)S(1)}, s32[1,1,1,8,16]{4,3,2,1,0:T(8,128)}, u32[]{:S(2)}) copy-start(s32[1,1,1,8,16]{4,3,2,1,0:T(8,128)} %param.13) | copy-start | bytes 1540
  7.3 12.2 %copy-start.3 = (s32[1,1,1,8,16]{4,3,2,1,0:T(8,128)S(1)}, s32[1,1,1,8,16]{4,3,2,1,0:T(8,128)}, u32[]{:S(2)}) copy-start(s32[1,1,1,8,16]{4,3,2,1,0:T(8,128)} %param.14) | copy-start | bytes 1540
  7.3 12.2 %copy-start.4 = (f32[1,1,1,8,16]{4,3,2,1,0:T(8,128)S(1)}, f32[1,1,1,8,16]{4,3,2,1,0:T(8,128)}, u32[]{:S(2)}) copy-start(f32[1,1,1,8,16]{4,3,2,1,0:T(8,128)} %param.15) | copy-start | bytes 1540
  7.3 12.2 %collective-permute-start.2 = (f32[5,16,512]{2,1,0:T(8,128)S(1)}, f32[5,16,512]{2,1,0:T(8,128)S(1)}, u32[]{:S(2)}, u32[]{:S(2)}) collective-permute-start(f32[5,16,512]{2,1,0:T(8,128)S(1)} %get-tuple-element.40), channel_id=1, source_target_pairs={{0,24},{4,28},{8,16},{12,20},{16,8},{20,12},{24,0},{28,4},{1,25},{... | collective-permute-start | bytes 491528 | tf_op jit(solution)/shard_map/ppermute | solution.py:345
  9.9 9.6 %collective-permute-start.3 = (f32[5,16,512]{2,1,0:T(8,128)S(1)}, f32[5,16,512]{2,1,0:T(8,128)S(1)}, u32[]{:S(2)}, u32[]{:S(2)}) collective-permute-start(f32[5,16,512]{2,1,0:T(8,128)S(1)} %get-tuple-element.41), channel_id=1, source_target_pairs={{0,12},{4,8},{8,4},{12,0},{16,28},{20,24},{24,20},{28,16},{1,13},{... | collective-permute-start | bytes 491528 | tf_op jit(solution)/shard_map/ppermute | solution.py:345
  10.5 9.0 %collective-permute-start.4 = (f32[5,16,512]{2,1,0:T(8,128)S(1)}, f32[5,16,512]{2,1,0:T(8,128)S(1)}, u32[]{:S(2)}, u32[]{:S(2)}) collective-permute-start(f32[5,16,512]{2,1,0:T(8,128)S(1)} %get-tuple-element.42), channel_id=1, source_target_pairs={{0,4},{4,0},{8,12},{12,8},{16,20},{20,16},{24,28},{28,24},{1,5},{5... | collective-permute-start | bytes 491528 | tf_op jit(solution)/shard_map/ppermute | solution.py:345
  12.0 10.0 %collective-permute-start.5 = (f32[5,16,512]{2,1,0:T(8,128)S(1)}, f32[5,16,512]{2,1,0:T(8,128)S(1)}, u32[]{:S(2)}, u32[]{:S(2)}) collective-permute-start(f32[5,16,512]{2,1,0:T(8,128)S(1)} %get-tuple-element.44), channel_id=1, source_target_pairs={{0,20},{4,16},{8,28},{12,24},{16,4},{20,0},{24,12},{28,8},{1,21},{... | collective-permute-start | bytes 491528 | tf_op jit(solution)/shard_map/ppermute | solution.py:345
  14.8 7.2 %collective-permute-start.6 = (f32[5,16,512]{2,1,0:T(8,128)S(1)}, f32[5,16,512]{2,1,0:T(8,128)S(1)}, u32[]{:S(2)}, u32[]{:S(2)}) collective-permute-start(f32[5,16,512]{2,1,0:T(8,128)S(1)} %get-tuple-element.45), channel_id=1, source_target_pairs={{0,28},{4,24},{8,20},{12,16},{16,12},{20,8},{24,4},{28,0},{1,29},{... | collective-permute-start | bytes 491528 | tf_op jit(solution)/shard_map/ppermute | solution.py:345
  21.6 8.1 %copy-start.6 = (f32[5]{0:T(128)S(1)}, f32[5]{0:T(128)}, u32[]{:S(2)}) copy-start(f32[5]{0:T(128)} %span_ref.3) | copy-start | bytes 64
  24.9 14.4 %collective-permute-start.9 = (f32[2,5,16,512]{3,2,1,0:T(8,128)S(1)}, f32[2,5,16,512]{3,2,1,0:T(8,128)S(1)}, u32[]{:S(2)}, u32[]{:S(2)}) collective-permute-start(f32[2,5,16,512]{3,2,1,0:T(8,128)S(1)} %get-tuple-element.56), channel_id=1, source_target_pairs={{0,1},{1,0},{2,3},{3,2},{4,5},{5,4},{6,7},{7,6},{8,9},{9,8},{10,11... | collective-permute-start | bytes 983048 | tf_op jit(solution)/shard_map/ppermute | solution.py:375
  26.8 12.5 %collective-permute-start.10 = (f32[2,5,16,512]{3,2,1,0:T(8,128)S(1)}, f32[2,5,16,512]{3,2,1,0:T(8,128)S(1)}, u32[]{:S(2)}, u32[]{:S(2)}) collective-permute-start(f32[2,5,16,512]{3,2,1,0:T(8,128)S(1)} %get-tuple-element.57), channel_id=1, source_target_pairs={{0,0},{1,2},{2,1},{3,3},{4,4},{5,6},{6,5},{7,7},{8,8},{9,10},{10,9... | collective-permute-start | bytes 983048 | tf_op jit(solution)/shard_map/ppermute | solution.py:375
  27.5 1.8 %collective-permute-start.7 = (f32[5,16,128]{2,1,0:T(8,128)S(1)}, f32[5,16,128]{2,1,0:T(8,128)S(1)}, u32[]{:S(2)}, u32[]{:S(2)}) collective-permute-start(f32[5,16,128]{2,1,0:T(8,128)S(1)} %get-tuple-element.49.tail_ref), channel_id=1, source_target_pairs={{0,4},{4,0},{1,5},{5,1},{2,6},{6,2},{3,7},{7,3},{8,12},{12,8},{9,1... | collective-permute-start | bytes 122888 | tf_op jit(solution)/shard_map/ppermute | solution.py:311
  28.4 1.2 %collective-permute-start.8 = (f32[5,16,128]{2,1,0:T(8,128)S(1)}, f32[5,16,128]{2,1,0:T(8,128)S(1)}, u32[]{:S(2)}, u32[]{:S(2)}) collective-permute-start(f32[5,16,128]{2,1,0:T(8,128)S(1)} %get-tuple-element.50.head_ref), channel_id=1, source_target_pairs={{0,4},{4,0},{1,5},{5,1},{2,6},{6,2},{3,7},{7,3},{8,12},{12,8},{9,1... | collective-permute-start | bytes 122888 | tf_op jit(solution)/shard_map/ppermute | solution.py:311
  39.5 12.3 %collective-permute-start.13 = (f32[4,16,512]{2,1,0:T(8,128)S(1)}, f32[4,16,512]{2,1,0:T(8,128)S(1)}, u32[]{:S(2)}, u32[]{:S(2)}) collective-permute-start(f32[4,16,512]{2,1,0:T(8,128)S(1)} %get-tuple-element.64), channel_id=1, source_target_pairs={{0,3},{1,0},{2,1},{3,2},{4,7},{5,4},{6,5},{7,6},{8,11},{9,8},{10,9... | collective-permute-start | bytes 393224 | tf_op jit(solution)/shard_map/ppermute | solution.py:311
  42.2 17.0 %collective-permute-start.12 = (f32[4,16,512]{2,1,0:T(8,128)S(1)}, f32[4,16,512]{2,1,0:T(8,128)S(1)}, u32[]{:S(2)}, u32[]{:S(2)}) collective-permute-start(f32[4,16,512]{2,1,0:T(8,128)S(1)} %get-tuple-element.63), channel_id=1, source_target_pairs={{0,2},{1,3},{2,0},{3,1},{4,6},{5,7},{6,4},{7,5},{8,10},{9,11},{10,... | collective-permute-start | bytes 393224 | tf_op jit(solution)/shard_map/ppermute | solution.py:311
  45.0 14.1 %collective-permute-start.11 = (f32[4,16,512]{2,1,0:T(8,128)S(1)}, f32[4,16,512]{2,1,0:T(8,128)S(1)}, u32[]{:S(2)}, u32[]{:S(2)}) collective-permute-start(f32[4,16,512]{2,1,0:T(8,128)S(1)} %get-tuple-element.63), channel_id=1, source_target_pairs={{0,1},{1,2},{2,3},{3,0},{4,5},{5,6},{6,7},{7,4},{8,9},{9,10},{10,1... | collective-permute-start | bytes 393224 | tf_op jit(solution)/shard_map/ppermute | solution.py:311
  48.2 14.3 %collective-permute-start.16 = (f32[1,16,512]{2,1,0:T(8,128)S(1)}, f32[1,16,512]{2,1,0:T(8,128)S(1)}, u32[]{:S(2)}, u32[]{:S(2)}) collective-permute-start(f32[1,16,512]{2,1,0:T(8,128)S(1)} %get-tuple-element.66), channel_id=1, source_target_pairs={{0,3},{1,0},{2,1},{3,2},{4,7},{5,4},{6,5},{7,6},{8,11},{9,8},{10,9... | collective-permute-start | bytes 98312 | tf_op jit(solution)/shard_map/ppermute | solution.py:311
  51.8 10.7 %collective-permute-start.15 = (f32[1,16,512]{2,1,0:T(8,128)S(1)}, f32[1,16,512]{2,1,0:T(8,128)S(1)}, u32[]{:S(2)}, u32[]{:S(2)}) collective-permute-start(f32[1,16,512]{2,1,0:T(8,128)S(1)} %get-tuple-element.65), channel_id=1, source_target_pairs={{0,2},{1,3},{2,0},{3,1},{4,6},{5,7},{6,4},{7,5},{8,10},{9,11},{10,... | collective-permute-start | bytes 98312 | tf_op jit(solution)/shard_map/ppermute | solution.py:311
  51.8 10.7 %collective-permute-start.14 = (f32[1,16,512]{2,1,0:T(8,128)S(1)}, f32[1,16,512]{2,1,0:T(8,128)S(1)}, u32[]{:S(2)}, u32[]{:S(2)}) collective-permute-start(f32[1,16,512]{2,1,0:T(8,128)S(1)} %get-tuple-element.65), channel_id=1, source_target_pairs={{0,1},{1,2},{2,3},{3,0},{4,5},{5,6},{6,7},{7,4},{8,9},{9,10},{10,1... | collective-permute-start | bytes 98312 | tf_op jit(solution)/shard_map/ppermute | solution.py:311

commit v6 on v5

--- a/solution.py
+++ b/solution.py
@@ -328,7 +328,8 @@
     )
     assert peers & (peers - 1) == 0
 
-    order = sorted(range(1, peers), key=lambda turn: (turn == 1, turn & 1, turn))
+    far = lambda turn: bin(turn >> 1).count("1")
+    order = sorted(range(1, peers), key=lambda turn: (turn == 1, turn & 1, -far(turn), turn))
     near = peers // 2 - 1
     arrived = {}
     groups = [order[:near], order[near:] + [0]]
@@ -375,7 +376,7 @@
         met.append(lax.ppermute(message, "stream", route))
     odd, even = met
     assert sections <= 4
-    split = max(components - 1, 1)
+    split = (components + 1) // 2
     state_now, parts = filled, []
     for lowest, size in ((0, split), (split, components - split)):
         some = (size, rows_y, width_z)

time: 64.3 us -> 59.9 us (0.932)
  starting transfers between devices: 25.6 us -> 21.1 us
    ppermute x8, starting transfers between devices: 15.2 us -> 10.7 us  [moved(): lax.ppermute(value, axis, [(i, (i + distance) % count) for i in range(cou...]
  transfers between devices with their start and end apart: 17 -> 17, of which waited for: 5 -> 5; matrix products, arithmetic and copies ran while one was open for 0% -> 0% of each run, Pallas kernels for 40% -> 41%
where the time goes in v6:
time: 59.9 us; the launch traced here: 59.5 us
  Pallas kernels  31.8 us (53%)
  starting transfers between devices  21.1 us (35%)
  waiting for transfers between devices  5.73 us (10%)
  local copies, waits for them, and re-layouts  0.71 us (1%)
    pallas_call x2, Pallas kernels, on_device(): call(functools.partial(scan_kernel, lowest), (SMEM, SMEM) + (VMEM,) * 7,...  12.6 us
    ppermute x8, starting transfers between devices, moved(): lax.ppermute(value, axis, [(i, (i + distance) % count) for i in range(cou...  10.7 us
    ppermute x7, starting transfers between devices, on_device(): arrived[turn] = lax.ppermute(tiles, RING, route) if turn else tiles  7.8 us
    pallas_call x2, Pallas kernels, on_device(): call(functools.partial(combine_kernel, lowest, len(begun)), (VMEM,) * 6 +...  4.82 us
    pallas_call x1, Pallas kernels, on_device(): call(growth_kernel, (SMEM, HBM, HBM), (VMEM,) * 5, [hold(state), hold(spe...  4.68 us
    pallas_call x2, Pallas kernels, on_device(): call(functools.partial(gather_kernel, turns), (SMEM, HBM), (VMEM,) * len(...  4.6 us
    ppermute x8, waiting for transfers between devices, moved(): lax.ppermute(value, axis, [(i, (i + distance) % count) for i in range(cou...  3.7 us
    pallas_call x1, Pallas kernels, on_device(): call(functools.partial(last_fill_kernel, late), (VMEM,) + (SMEM,) * 3 + (...  3.03 us
  transfers between devices with their start and end apart: 17, of which 5 were waited for; matrix products, arithmetic and copies ran while one was open for 0% of the time, Pallas kernels for 41%

profile of v6, /device:TPU:0, one launch (start us, length us, event | category | flops | bytes accessed | tf_op | source)
XLA Modules:
  0.0 59.5 jit_solution(11155372570565118712)
XLA Ops:
  0.0 0.7 %copy-done.1 = s32[1,1,1,8,16]{4,3,2,1,0:T(8,128)S(1)} copy-done((s32[1,1,1,8,16]{4,3,2,1,0:T(8,128)S(1)}, s32[1,1,1,8,16]{4,3,2,1,0:T(8,128)}, u32[]{:S(2)}) %copy-start.1) | copy-done | bytes 536
  0.7 2.1 %shard_map.83 = (f32[5,16,512]{2,1,0:T(8,128)S(1)}, f32[5,16,512]{2,1,0:T(8,128)S(1)}, f32[5,16,512]{2,1,0:T(8,128)S(1)}) custom-call(s32[8,16]{1,0:T(8,128)S(1)} %bitcast.12, f32[64,5,16,512]{3,2,1,0:T(8,128)} %bitcast.20), custom_call_target="tpu_custom_call" | custom-call | bytes 3000000 | tf_op jit(solution)/shard_map/pallas_call | solution.py:337
  2.8 4.0 %collective-permute-start = (f32[5,16,512]{2,1,0:T(8,128)S(1)}, f32[5,16,512]{2,1,0:T(8,128)S(1)}, u32[]{:S(2)}, u32[]{:S(2)}) collective-permute-start(f32[5,16,512]{2,1,0:T(8,128)S(1)} %get-tuple-element.38), channel_id=1, source_target_pairs={{0,24},{4,28},{8,16},{12,20},{16,8},{20,12},{24,0},{28,4},{1,25},{... | collective-permute-start | bytes 491528 | tf_op jit(solution)/shard_map/ppermute | solution.py:346
  6.7 0.5 collective-permute-start.1
  7.4 2.5 %shard_map.84 = (f32[5,16,512]{2,1,0:T(8,128)S(1)}, f32[5,16,512]{2,1,0:T(8,128)S(1)}, f32[5,16,512]{2,1,0:T(8,128)S(1)}, f32[5,16,512]{2,1,0:T(8,128)S(1)}, f32[5,16,512]{2,1,0:T(8,128)S(1)}) custom-call(s32[8,16]{1,0:T(8,128)S(1)} %bitcast.13, f32[64,5,16,512]{3,2,1,0:T(8,128)} %bitcast.21), custom_call_target="tpu_custom_call" | custom-call | bytes 3000000 | tf_op jit(solution)/shard_map/pallas_call | solution.py:337
  9.9 1.5 %collective-permute-start.3 = (f32[5,16,512]{2,1,0:T(8,128)S(1)}, f32[5,16,512]{2,1,0:T(8,128)S(1)}, u32[]{:S(2)}, u32[]{:S(2)}) collective-permute-start(f32[5,16,512]{2,1,0:T(8,128)S(1)} %get-tuple-element.41), channel_id=1, source_target_pairs={{0,28},{4,24},{8,20},{12,16},{16,12},{20,8},{24,4},{28,0},{1,29},{... | collective-permute-start | bytes 491528 | tf_op jit(solution)/shard_map/ppermute | solution.py:346
  11.5 1.5 %collective-permute-start.4 = (f32[5,16,512]{2,1,0:T(8,128)S(1)}, f32[5,16,512]{2,1,0:T(8,128)S(1)}, u32[]{:S(2)}, u32[]{:S(2)}) collective-permute-start(f32[5,16,512]{2,1,0:T(8,128)S(1)} %get-tuple-element.42), channel_id=1, source_target_pairs={{0,4},{4,0},{8,12},{12,8},{16,20},{20,16},{24,28},{28,24},{1,5},{5... | collective-permute-start | bytes 491528 | tf_op jit(solution)/shard_map/ppermute | solution.py:346
  13.1 2.0 %collective-permute-done.1.refs_1_ = f32[5,16,512]{2,1,0:T(8,128)S(1)} collective-permute-done((f32[5,16,512]{2,1,0:T(8,128)S(1)}, f32[5,16,512]{2,1,0:T(8,128)S(1)}, u32[]{:S(2)}, u32[]{:S(2)}) %collective-permute-start.1) | collective-permute-done | bytes 163872 | tf_op jit(solution)/shard_map/ppermute | solution.py:346
  15.1 4.7 %shard_map.82 = (f32[64,5,16,512]{3,2,1,0:T(8,128)S(1)}, f32[64,16,512]{2,1,0:T(8,128)S(1)}, f32[64,5,16,512]{3,2,1,0:T(8,128)S(1)}, f32[5,16,512]{2,1,0:T(8,128)S(1)}, f32[5,16,512]{2,1,0:T(8,128)S(1)}) custom-call(f32[5]{0:T(128)S(1)} %copy-done.5, f32[64,5,16,512]{3,2,1,0:T(8,128)} %bitcast.22, f32[64,16,512]{2,1,0:T(8,128)S(1)} %bitcast.11), custom_call_target="tpu_custom_call" | custom-call | bytes 15000000 | tf_op jit(solution)/shard_map/pallas_call | solution.py:349
  19.9 1.9 %shard_map.85.refs_3_ = f32[64,5,16,512]{3,2,1,0:T(8,128)S(1)} custom-call(s32[8,16]{1,0:T(8,128)S(1)} %bitcast.14, s32[8,16]{1,0:T(8,128)S(1)} %bitcast.16, f32[8,16]{1,0:T(8,128)S(1)} %bitcast.18, f32[64,5,16,512]{3,2,1,0:T(8,128)S(1)} %get-tuple-element.37.flow_ref, ...), custom_call_target="tpu_custom_call", output_to_operand_aliasing={{}: (3, {})} | custom-call | bytes 6000000 | tf_op jit(solution)/shard_map/pallas_call | solution.py:356
  21.9 3.0 %shard_map.86 = (f32[64,5,16,512]{3,2,1,0:T(8,128)S(1)}, f32[4,5,16,512]{3,2,1,0:T(8,128)S(1)}, f32[2,5,16,512]{3,2,1,0:T(8,128)S(1)}, f32[2,5,16,512]{3,2,1,0:T...) custom-call(f32[5,16,512]{2,1,0:T(8,128)S(1)} %get-tuple-element.36.total_ref, ...), custom_call_target="tpu_custom_call", output_to_operand_aliasing={{0}: (4, {})} | custom-call | bytes 12000000 | tf_op jit(solution)/shard_map/pallas_call | solution.py:363
  24.9 1.9 %collective-permute-start.9 = (f32[2,5,16,512]{3,2,1,0:T(8,128)S(1)}, f32[2,5,16,512]{3,2,1,0:T(8,128)S(1)}, u32[]{:S(2)}, u32[]{:S(2)}) collective-permute-start(f32[2,5,16,512]{3,2,1,0:T(8,128)S(1)} %get-tuple-element.56), channel_id=1, source_target_pairs={{0,1},{1,0},{2,3},{3,2},{4,5},{5,4},{6,7},{7,6},{8,9},{9,8},{10,11... | collective-permute-start | bytes 983048 | tf_op jit(solution)/shard_map/ppermute | solution.py:376
  26.8 0.7 %collective-permute-start.10 = (f32[2,5,16,512]{3,2,1,0:T(8,128)S(1)}, f32[2,5,16,512]{3,2,1,0:T(8,128)S(1)}, u32[]{:S(2)}, u32[]{:S(2)}) collective-permute-start(f32[2,5,16,512]{3,2,1,0:T(8,128)S(1)} %get-tuple-element.57), channel_id=1, source_target_pairs={{0,0},{1,2},{2,1},{3,3},{4,4},{5,6},{6,5},{7,7},{8,8},{9,10},{10,9... | collective-permute-start | bytes 983048 | tf_op jit(solution)/shard_map/ppermute | solution.py:376
  28.1 0.7 %collective-permute-done.7.before_ref = f32[5,16,128]{2,1,0:T(8,128)S(1)} collective-permute-done((f32[5,16,128]{2,1,0:T(8,128)S(1)}, f32[5,16,128]{2,1,0:T(8,128)S(1)}, u32[]{:S(2)}, u32[]{:S(2)}) %collective-permute-start.7) | collective-permute-done | bytes 40992 | tf_op jit(solution)/shard_map/ppermute | solution.py:311
  29.0 7.4 %shard_map.87 = (f32[64,5,16,512]{3,2,1,0:T(8,128)S(1)}, f32[3,16,512]{2,1,0:T(8,128)S(1)}) custom-call(f32[5]{0:T(128)S(1)} %copy-done.5, f32[5]{0:T(128)S(1)} %copy-done.6, f32[64,5,16,512]{3,2,1,0:T(8,128)S(1)} %get-tuple-element.46.filled_ref, f32[64,5,16,512]{3,2,1,0:T(8,128)S(1)} %get-tuple-element.47.ratio_ref, ...), custom_call_target="tpu_custom_call", output_to_operand_aliasing={{0}: (2, {})} | custom-call | bytes 27000000 | tf_op jit(solution)/shard_map/pallas_call | solution.py:383
  36.5 2.6 %collective-permute-start.13 = (f32[3,16,512]{2,1,0:T(8,128)S(1)}, f32[3,16,512]{2,1,0:T(8,128)S(1)}, u32[]{:S(2)}, u32[]{:S(2)}) collective-permute-start(f32[3,16,512]{2,1,0:T(8,128)S(1)} %get-tuple-element.64), channel_id=1, source_target_pairs={{0,3},{1,0},{2,1},{3,2},{4,7},{5,4},{6,5},{7,6},{8,11},{9,8},{10,9... | collective-permute-start | bytes 294920 | tf_op jit(solution)/shard_map/ppermute | solution.py:311
  39.1 3.0 %collective-permute-start.12 = (f32[3,16,512]{2,1,0:T(8,128)S(1)}, f32[3,16,512]{2,1,0:T(8,128)S(1)}, u32[]{:S(2)}, u32[]{:S(2)}) collective-permute-start(f32[3,16,512]{2,1,0:T(8,128)S(1)} %get-tuple-element.63), channel_id=1, source_target_pairs={{0,2},{1,3},{2,0},{3,1},{4,6},{5,7},{6,4},{7,5},{8,10},{9,11},{10,... | collective-permute-start | bytes 294920 | tf_op jit(solution)/shard_map/ppermute | solution.py:311
  42.1 1.0 %collective-permute-start.11 = (f32[3,16,512]{2,1,0:T(8,128)S(1)}, f32[3,16,512]{2,1,0:T(8,128)S(1)}, u32[]{:S(2)}, u32[]{:S(2)}) collective-permute-start(f32[3,16,512]{2,1,0:T(8,128)S(1)} %get-tuple-element.63), channel_id=1, source_target_pairs={{0,1},{1,2},{2,3},{3,0},{4,5},{5,6},{6,7},{7,4},{8,9},{9,10},{10,1... | collective-permute-start | bytes 294920 | tf_op jit(solution)/shard_map/ppermute | solution.py:311
  43.1 5.2 %shard_map.88 = (f32[64,5,16,512]{3,2,1,0:T(8,128)S(1)}, f32[2,16,512]{2,1,0:T(8,128)S(1)}) custom-call(f32[5]{0:T(128)S(1)} %copy-done.5, f32[5]{0:T(128)S(1)} %copy-done.6, f32[64,5,16,512]{3,2,1,0:T(8,128)S(1)} %get-tuple-element.51.filled_ref, f32[64,5,16,512]{3,2,1,0:T(8,128)S(1)} %get-tuple-element.47.ratio_ref, ...), custom_call_target="tpu_custom_call", output_to_operand_aliasing={{0}: (2, {})} | custom-call | bytes 18000000 | tf_op jit(solution)/shard_map/pallas_call | solution.py:383
  48.3 2.9 %collective-permute-start.16 = (f32[2,16,512]{2,1,0:T(8,128)S(1)}, f32[2,16,512]{2,1,0:T(8,128)S(1)}, u32[]{:S(2)}, u32[]{:S(2)}) collective-permute-start(f32[2,16,512]{2,1,0:T(8,128)S(1)} %get-tuple-element.66), channel_id=1, source_target_pairs={{0,3},{1,0},{2,1},{3,2},{4,7},{5,4},{6,5},{7,6},{8,11},{9,8},{10,9... | collective-permute-start | bytes 196616 | tf_op jit(solution)/shard_map/ppermute | solution.py:311
  51.2 0.6 %collective-permute-start.14 = (f32[2,16,512]{2,1,0:T(8,128)S(1)}, f32[2,16,512]{2,1,0:T(8,128)S(1)}, u32[]{:S(2)}, u32[]{:S(2)}) collective-permute-start(f32[2,16,512]{2,1,0:T(8,128)S(1)} %get-tuple-element.65), channel_id=1, source_target_pairs={{0,1},{1,2},{2,3},{3,0},{4,5},{5,6},{6,7},{7,4},{8,9},{9,10},{10,1... | collective-permute-start | bytes 196616 | tf_op jit(solution)/shard_map/ppermute | solution.py:311
  52.1 2.7 %shard_map.91.refs_0_ = f32[64,5,16,512]{3,2,1,0:T(8,128)} custom-call(f32[64,5,16,512]{3,2,1,0:T(8,128)S(1)} %get-tuple-element.52.local_ref, f32[64,5,16,512]{3,2,1,0:T(8,128)S(1)} %get-tuple-element.47.ratio_ref, f32[3,16,512]{2,1,0:T(8,128)S(1)} %get-tuple-element.61.first_ref, f32[3,16,512]{2,1,0:T(8,128)S(1)} %get-tuple-element.62.last_ref, ...), custom_call_target="tpu_custom_call" | custom-call | bytes 9000000 | tf_op jit(solution)/shard_map/pallas_call | solution.py:400
  54.8 2.6 %collective-permute-done.15.refs_2_ = f32[2,16,512]{2,1,0:T(8,128)S(1)} collective-permute-done((f32[2,16,512]{2,1,0:T(8,128)S(1)}, f32[2,16,512]{2,1,0:T(8,128)S(1)}, u32[]{:S(2)}, u32[]{:S(2)}) %collective-permute-start.15) | collective-permute-done | bytes 65568 | tf_op jit(solution)/shard_map/ppermute | solution.py:311
  57.5 2.1 %shard_map.92 = f32[64,5,16,512]{3,2,1,0:T(8,128)} custom-call(f32[64,5,16,512]{3,2,1,0:T(8,128)S(1)} %get-tuple-element.52.local_ref, f32[64,5,16,512]{3,2,1,0:T(8,128)S(1)} %get-tuple-element.47.ratio_ref, f32[2,16,512]{2,1,0:T(8,128)S(1)} %get-tuple-element.58.first_ref, ...), custom_call_target="tpu_custom_call", output_to_operand_aliasing={{}: (6, {})} | custom-call | bytes 6000000 | tf_op jit(solution)/shard_map/pallas_call | solution.py:400
  (35 shorter events, 1.4 us)
Async XLA Ops:
  0.0 0.7 %copy-start.1 = (s32[1,1,1,8,16]{4,3,2,1,0:T(8,128)S(1)}, s32[1,1,1,8,16]{4,3,2,1,0:T(8,128)}, u32[]{:S(2)}) copy-start(s32[1,1,1,8,16]{4,3,2,1,0:T(8,128)} %param.12) | copy-start | bytes 1540
  0.7 14.5 %copy-start = (f32[1,64,16,512]{3,2,1,0:T(8,128)S(1)}, f32[1,64,16,512]{3,2,1,0:T(8,128)}, u32[]{:S(2)}) copy-start(f32[1,64,16,512]{3,2,1,0:T(8,128)} %param.9) | copy-start | bytes 6291460
  0.7 14.5 %copy-start.5 = (f32[5]{0:T(128)S(1)}, f32[5]{0:T(128)}, u32[]{:S(2)}) copy-start(f32[5]{0:T(128)} %scale_ref.5) | copy-start | bytes 64
  2.8 10.2 %collective-permute-start = (f32[5,16,512]{2,1,0:T(8,128)S(1)}, f32[5,16,512]{2,1,0:T(8,128)S(1)}, u32[]{:S(2)}, u32[]{:S(2)}) collective-permute-start(f32[5,16,512]{2,1,0:T(8,128)S(1)} %get-tuple-element.38), channel_id=1, source_target_pairs={{0,24},{4,28},{8,16},{12,20},{16,8},{20,12},{24,0},{28,4},{1,25},{... | collective-permute-start | bytes 491528 | tf_op jit(solution)/shard_map/ppermute | solution.py:346
  6.7 8.4 %collective-permute-start.1 = (f32[5,16,512]{2,1,0:T(8,128)S(1)}, f32[5,16,512]{2,1,0:T(8,128)S(1)}, u32[]{:S(2)}, u32[]{:S(2)}) collective-permute-start(f32[5,16,512]{2,1,0:T(8,128)S(1)} %get-tuple-element.39), channel_id=1, source_target_pairs={{0,8},{4,12},{8,0},{12,4},{16,24},{20,28},{24,16},{28,20},{1,9},{5... | collective-permute-start | bytes 491528 | tf_op jit(solution)/shard_map/ppermute | solution.py:346
  7.3 12.6 %copy-start.2 = (s32[1,1,1,8,16]{4,3,2,1,0:T(8,128)S(1)}, s32[1,1,1,8,16]{4,3,2,1,0:T(8,128)}, u32[]{:S(2)}) copy-start(s32[1,1,1,8,16]{4,3,2,1,0:T(8,128)} %param.13) | copy-start | bytes 1540
  7.3 12.6 %copy-start.3 = (s32[1,1,1,8,16]{4,3,2,1,0:T(8,128)S(1)}, s32[1,1,1,8,16]{4,3,2,1,0:T(8,128)}, u32[]{:S(2)}) copy-start(s32[1,1,1,8,16]{4,3,2,1,0:T(8,128)} %param.14) | copy-start | bytes 1540
  7.3 12.6 %copy-start.4 = (f32[1,1,1,8,16]{4,3,2,1,0:T(8,128)S(1)}, f32[1,1,1,8,16]{4,3,2,1,0:T(8,128)}, u32[]{:S(2)}) copy-start(f32[1,1,1,8,16]{4,3,2,1,0:T(8,128)} %param.15) | copy-start | bytes 1540
  7.3 12.6 %collective-permute-start.2 = (f32[5,16,512]{2,1,0:T(8,128)S(1)}, f32[5,16,512]{2,1,0:T(8,128)S(1)}, u32[]{:S(2)}, u32[]{:S(2)}) collective-permute-start(f32[5,16,512]{2,1,0:T(8,128)S(1)} %get-tuple-element.40), channel_id=1, source_target_pairs={{0,16},{4,20},{8,24},{12,28},{16,0},{20,4},{24,8},{28,12},{1,17},{... | collective-permute-start | bytes 491528 | tf_op jit(solution)/shard_map/ppermute | solution.py:346
  9.9 9.9 %collective-permute-start.3 = (f32[5,16,512]{2,1,0:T(8,128)S(1)}, f32[5,16,512]{2,1,0:T(8,128)S(1)}, u32[]{:S(2)}, u32[]{:S(2)}) collective-permute-start(f32[5,16,512]{2,1,0:T(8,128)S(1)} %get-tuple-element.41), channel_id=1, source_target_pairs={{0,28},{4,24},{8,20},{12,16},{16,12},{20,8},{24,4},{28,0},{1,29},{... | collective-permute-start | bytes 491528 | tf_op jit(solution)/shard_map/ppermute | solution.py:346
  11.5 8.4 %collective-permute-start.4 = (f32[5,16,512]{2,1,0:T(8,128)S(1)}, f32[5,16,512]{2,1,0:T(8,128)S(1)}, u32[]{:S(2)}, u32[]{:S(2)}) collective-permute-start(f32[5,16,512]{2,1,0:T(8,128)S(1)} %get-tuple-element.42), channel_id=1, source_target_pairs={{0,4},{4,0},{8,12},{12,8},{16,20},{20,16},{24,28},{28,24},{1,5},{5... | collective-permute-start | bytes 491528 | tf_op jit(solution)/shard_map/ppermute | solution.py:346
  13.0 8.9 %collective-permute-start.5 = (f32[5,16,512]{2,1,0:T(8,128)S(1)}, f32[5,16,512]{2,1,0:T(8,128)S(1)}, u32[]{:S(2)}, u32[]{:S(2)}) collective-permute-start(f32[5,16,512]{2,1,0:T(8,128)S(1)} %get-tuple-element.44), channel_id=1, source_target_pairs={{0,12},{4,8},{8,4},{12,0},{16,28},{20,24},{24,20},{28,16},{1,13},{... | collective-permute-start | bytes 491528 | tf_op jit(solution)/shard_map/ppermute | solution.py:346
  15.1 6.7 %collective-permute-start.6 = (f32[5,16,512]{2,1,0:T(8,128)S(1)}, f32[5,16,512]{2,1,0:T(8,128)S(1)}, u32[]{:S(2)}, u32[]{:S(2)}) collective-permute-start(f32[5,16,512]{2,1,0:T(8,128)S(1)} %get-tuple-element.45), channel_id=1, source_target_pairs={{0,20},{4,16},{8,28},{12,24},{16,4},{20,0},{24,12},{28,8},{1,21},{... | collective-permute-start | bytes 491528 | tf_op jit(solution)/shard_map/ppermute | solution.py:346
  21.8 7.1 %copy-start.6 = (f32[5]{0:T(128)S(1)}, f32[5]{0:T(128)}, u32[]{:S(2)}) copy-start(f32[5]{0:T(128)} %span_ref.3) | copy-start | bytes 64
  24.9 11.5 %collective-permute-start.9 = (f32[2,5,16,512]{3,2,1,0:T(8,128)S(1)}, f32[2,5,16,512]{3,2,1,0:T(8,128)S(1)}, u32[]{:S(2)}, u32[]{:S(2)}) collective-permute-start(f32[2,5,16,512]{3,2,1,0:T(8,128)S(1)} %get-tuple-element.56), channel_id=1, source_target_pairs={{0,1},{1,0},{2,3},{3,2},{4,5},{5,4},{6,7},{7,6},{8,9},{9,8},{10,11... | collective-permute-start | bytes 983048 | tf_op jit(solution)/shard_map/ppermute | solution.py:376
  26.8 9.6 %collective-permute-start.10 = (f32[2,5,16,512]{3,2,1,0:T(8,128)S(1)}, f32[2,5,16,512]{3,2,1,0:T(8,128)S(1)}, u32[]{:S(2)}, u32[]{:S(2)}) collective-permute-start(f32[2,5,16,512]{3,2,1,0:T(8,128)S(1)} %get-tuple-element.57), channel_id=1, source_target_pairs={{0,0},{1,2},{2,1},{3,3},{4,4},{5,6},{6,5},{7,7},{8,8},{9,10},{10,9... | collective-permute-start | bytes 983048 | tf_op jit(solution)/shard_map/ppermute | solution.py:376
  27.5 1.3 %collective-permute-start.7 = (f32[5,16,128]{2,1,0:T(8,128)S(1)}, f32[5,16,128]{2,1,0:T(8,128)S(1)}, u32[]{:S(2)}, u32[]{:S(2)}) collective-permute-start(f32[5,16,128]{2,1,0:T(8,128)S(1)} %get-tuple-element.49.tail_ref), channel_id=1, source_target_pairs={{0,4},{4,0},{1,5},{5,1},{2,6},{6,2},{3,7},{7,3},{8,12},{12,8},{9,1... | collective-permute-start | bytes 122888 | tf_op jit(solution)/shard_map/ppermute | solution.py:311
  27.7 1.3 %collective-permute-start.8 = (f32[5,16,128]{2,1,0:T(8,128)S(1)}, f32[5,16,128]{2,1,0:T(8,128)S(1)}, u32[]{:S(2)}, u32[]{:S(2)}) collective-permute-start(f32[5,16,128]{2,1,0:T(8,128)S(1)} %get-tuple-element.50.head_ref), channel_id=1, source_target_pairs={{0,4},{4,0},{1,5},{5,1},{2,6},{6,2},{3,7},{7,3},{8,12},{12,8},{9,1... | collective-permute-start | bytes 122888 | tf_op jit(solution)/shard_map/ppermute | solution.py:311
  36.5 14.7 %collective-permute-start.13 = (f32[3,16,512]{2,1,0:T(8,128)S(1)}, f32[3,16,512]{2,1,0:T(8,128)S(1)}, u32[]{:S(2)}, u32[]{:S(2)}) collective-permute-start(f32[3,16,512]{2,1,0:T(8,128)S(1)} %get-tuple-element.64), channel_id=1, source_target_pairs={{0,3},{1,0},{2,1},{3,2},{4,7},{5,4},{6,5},{7,6},{8,11},{9,8},{10,9... | collective-permute-start | bytes 294920 | tf_op jit(solution)/shard_map/ppermute | solution.py:311
  39.1 13.0 %collective-permute-start.12 = (f32[3,16,512]{2,1,0:T(8,128)S(1)}, f32[3,16,512]{2,1,0:T(8,128)S(1)}, u32[]{:S(2)}, u32[]{:S(2)}) collective-permute-start(f32[3,16,512]{2,1,0:T(8,128)S(1)} %get-tuple-element.63), channel_id=1, source_target_pairs={{0,2},{1,3},{2,0},{3,1},{4,6},{5,7},{6,4},{7,5},{8,10},{9,11},{10,... | collective-permute-start | bytes 294920 | tf_op jit(solution)/shard_map/ppermute | solution.py:311
  42.1 10.0 %collective-permute-start.11 = (f32[3,16,512]{2,1,0:T(8,128)S(1)}, f32[3,16,512]{2,1,0:T(8,128)S(1)}, u32[]{:S(2)}, u32[]{:S(2)}) collective-permute-start(f32[3,16,512]{2,1,0:T(8,128)S(1)} %get-tuple-element.63), channel_id=1, source_target_pairs={{0,1},{1,2},{2,3},{3,0},{4,5},{5,6},{6,7},{7,4},{8,9},{9,10},{10,1... | collective-permute-start | bytes 294920 | tf_op jit(solution)/shard_map/ppermute | solution.py:311
  48.3 6.5 %collective-permute-start.16 = (f32[2,16,512]{2,1,0:T(8,128)S(1)}, f32[2,16,512]{2,1,0:T(8,128)S(1)}, u32[]{:S(2)}, u32[]{:S(2)}) collective-permute-start(f32[2,16,512]{2,1,0:T(8,128)S(1)} %get-tuple-element.66), channel_id=1, source_target_pairs={{0,3},{1,0},{2,1},{3,2},{4,7},{5,4},{6,5},{7,6},{8,11},{9,8},{10,9... | collective-permute-start | bytes 196616 | tf_op jit(solution)/shard_map/ppermute | solution.py:311
  51.2 6.2 %collective-permute-start.15 = (f32[2,16,512]{2,1,0:T(8,128)S(1)}, f32[2,16,512]{2,1,0:T(8,128)S(1)}, u32[]{:S(2)}, u32[]{:S(2)}) collective-permute-start(f32[2,16,512]{2,1,0:T(8,128)S(1)} %get-tuple-element.65), channel_id=1, source_target_pairs={{0,2},{1,3},{2,0},{3,1},{4,6},{5,7},{6,4},{7,5},{8,10},{9,11},{10,... | collective-permute-start | bytes 196616 | tf_op jit(solution)/shard_map/ppermute | solution.py:311
  51.2 6.2 %collective-permute-start.14 = (f32[2,16,512]{2,1,0:T(8,128)S(1)}, f32[2,16,512]{2,1,0:T(8,128)S(1)}, u32[]{:S(2)}, u32[]{:S(2)}) collective-permute-start(f32[2,16,512]{2,1,0:T(8,128)S(1)} %get-tuple-element.65), channel_id=1, source_target_pairs={{0,1},{1,2},{2,3},{3,0},{4,5},{5,6},{6,7},{7,4},{8,9},{9,10},{10,1... | collective-permute-start | bytes 196616 | tf_op jit(solution)/shard_map/ppermute | solution.py:311

commit v7 on v6

--- a/solution.py
+++ b/solution.py
@@ -245,17 +245,18 @@
 
 
 def edge_kernel(
-    lowest, flux_ref, total_ref, last_ref, rows_ref, even_ref, odd_ref,
-    flux_out, beyond_out, first_out, last_out,
+    lowest, total_ref, last_ref, rows_ref, even_ref, odd_ref, *refs
 ):
-    part = pl.ds(lowest, flux_ref.shape[0])
+    *flux_refs, flux_out, beyond_out, first_out, last_out = refs
+    part = pl.ds(lowest, flux_out.shape[0])
     behind = beside("behind", even_ref.at[0, part], odd_ref.at[0, part]) * inside("stream", 1)
     ahead = beside("ahead", even_ref.at[0, part], odd_ref.at[0, part]) * inside("stream", -1)
     row = [rows_ref[k, part] for k in range(4)]
     slope_first = limited(0.5 * (row[0] - behind), 0.5 * (row[1] - row[0]))
     slope_last = limited(0.5 * (row[3] - row[2]), 0.5 * (ahead - row[3]))
     kept = last_ref[part] * slope_last
-    flux = flux_ref[...] + total_ref[part] * slope_first + kept
+    flux = jnp.concatenate([ref[...] for ref in flux_refs], axis=0)
+    flux = flux + total_ref[part] * slope_first + kept
     flux_out[...] = flux
     beyond_out[...] = beside("ahead", even_ref.at[1, part], odd_ref.at[1, part]) * flux
     first_out[...] = slope_first
@@ -331,6 +332,7 @@
     far = lambda turn: bin(turn >> 1).count("1")
     order = sorted(range(1, peers), key=lambda turn: (turn == 1, turn & 1, -far(turn), turn))
     near = peers // 2 - 1
+    send_hbm = pltpu.with_memory_space_constraint(send, HBM)
     arrived = {}
     groups = [order[:near], order[near:] + [0]]
     for turns in groups:
@@ -340,7 +342,7 @@
             [jax.ShapeDtypeStruct((components, capacity, width_z), F32)] * len(turns),
             [pltpu.SemaphoreType.DMA((len(turns),))],
             micros=1,
-        )(send, flow)
+        )(send_hbm, flow)
         for turn, tiles in zip(turns, outgoing):
             route = [(i, i ^ turn) for i in range(peers)]
             arrived[turn] = lax.ppermute(tiles, RING, route) if turn else tiles
@@ -377,24 +379,28 @@
     odd, even = met
     assert sections <= 4
     split = (components + 1) // 2
-    state_now, parts = filled, []
-    for lowest, size in ((0, split), (split, components - split)):
-        some = (size, rows_y, width_z)
+    state_now, fluxes = filled, []
+    pieces = [(0, split)] + [(v, 1) for v in range(split, components)]
+    for lowest, size in pieces:
         state_now, flux = call(
             functools.partial(scan_kernel, lowest),
             (SMEM, SMEM) + (VMEM,) * 7, (VMEM,) * 2,
-            [hold(state), hold(some)],
+            [hold(state), hold((size, rows_y, width_z))],
             [pltpu.VMEM(edge, F32)] * 3,
             aliases={2: 0},
             micros=3 * size,
         )(char_scale, span_ratio, state_now, ratio, speed_in, tail, head, before, after)
+        fluxes.append(flux)
+    parts = []
+    for lowest, size, local in ((0, split, fluxes[:1]), (split, components - split, fluxes[1:])):
+        some = (size, rows_y, width_z)
         flux, beyond, first_slope, last_slope = call(
             functools.partial(edge_kernel, lowest),
-            (VMEM,) * 6, (VMEM,) * 4,
+            (VMEM,) * (5 + len(local)), (VMEM,) * 4,
             [jax.ShapeDtypeStruct(some, F32)] * 4,
-        )(flux, total, last, rows, even, odd)
-        fluxes = [moved(flux if d < 3 else beyond, "stream", d) for d in range(1, sections)]
-        parts.append((lowest, some, first_slope, last_slope, fluxes))
+        )(total, last, rows, even, odd, *local)
+        sent = [moved(flux if d < 3 else beyond, "stream", d) for d in range(1, sections)]
+        parts.append((lowest, some, first_slope, last_slope, sent))
     begun = ()
     for lowest, some, first_slope, last_slope, fluxes in parts:
         begun = call(

time: 59.9 us -> 60.1 us (level)
  Pallas kernels: 31.8 us -> 32.9 us
  local copies, waits for them, and re-layouts: 0.71 us -> 0.02 us
    unnamed x14 -> x12, local copies, waits for them, and re-layouts: 0.71 us -> 0.02 us
    pallas_call x2 -> x3, Pallas kernels: 12.6 us -> 13.2 us  [on_device(): call(functools.partial(scan_kernel, lowest), (SMEM, SMEM) + (VMEM,) * 7,...]
  transfers between devices with their start and end apart: 17 -> 17, of which waited for: 5 -> 4; matrix products, arithmetic and copies ran while one was open for 0% -> 0% of each run, Pallas kernels for 41% -> 42%
where the time goes in v7:
time: 60.1 us; the launch traced here: 59.8 us
  Pallas kernels  32.9 us (55%)
  starting transfers between devices  21.2 us (35%)
  waiting for transfers between devices  5.49 us (9%)
    pallas_call x3, Pallas kernels, on_device(): call(functools.partial(scan_kernel, lowest), (SMEM, SMEM) + (VMEM,) * 7,...  13.2 us
    ppermute x8, starting transfers between devices, moved(): lax.ppermute(value, axis, [(i, (i + distance) % count) for i in range(cou...  10.7 us
    ppermute x7, starting transfers between devices, on_device(): arrived[turn] = lax.ppermute(tiles, RING, route) if turn else tiles  7.83 us
    pallas_call x2, Pallas kernels, on_device(): call(functools.partial(gather_kernel, turns), (SMEM, HBM), (VMEM,) * len(...  5.04 us
    pallas_call x2, Pallas kernels, on_device(): call(functools.partial(combine_kernel, lowest, len(begun)), (VMEM,) * 6 +...  4.82 us
    pallas_call x1, Pallas kernels, on_device(): call(growth_kernel, (SMEM, HBM, HBM), (VMEM,) * 5, [hold(state), hold(spe...  4.68 us
    ppermute x8, waiting for transfers between devices, moved(): lax.ppermute(value, axis, [(i, (i + distance) % count) for i in range(cou...  3.69 us
    pallas_call x1, Pallas kernels, on_device(): call(functools.partial(last_fill_kernel, late), (VMEM,) + (SMEM,) * 3 + (...  3.03 us
  transfers between devices with their start and end apart: 17, of which 4 were waited for; matrix products, arithmetic and copies ran while one was open for 0% of the time, Pallas kernels for 42%

profile of v7, /device:TPU:0, one launch (start us, length us, event | category | flops | bytes accessed | tf_op | source)
XLA Modules:
  0.0 59.8 jit_solution(15136236252825178992)
XLA Ops:
  0.0 2.4 %shard_map.83 = (f32[5,16,512]{2,1,0:T(8,128)S(1)}, f32[5,16,512]{2,1,0:T(8,128)S(1)}, f32[5,16,512]{2,1,0:T(8,128)S(1)}) custom-call(s32[8,16]{1,0:T(8,128)} %bitcast.21, f32[64,5,16,512]{3,2,1,0:T(8,128)} %bitcast.18), custom_call_target="tpu_custom_call" | custom-call | bytes 3000000 | tf_op jit(solution)/shard_map/pallas_call | solution.py:339
  2.4 4.0 %collective-permute-start = (f32[5,16,512]{2,1,0:T(8,128)S(1)}, f32[5,16,512]{2,1,0:T(8,128)S(1)}, u32[]{:S(2)}, u32[]{:S(2)}) collective-permute-start(f32[5,16,512]{2,1,0:T(8,128)S(1)} %get-tuple-element.40), channel_id=1, source_target_pairs={{0,24},{4,28},{8,16},{12,20},{16,8},{20,12},{24,0},{28,4},{1,25},{... | collective-permute-start | bytes 491528 | tf_op jit(solution)/shard_map/ppermute | solution.py:348
  6.4 0.5 collective-permute-start.1
  7.0 2.7 %shard_map.84 = (f32[5,16,512]{2,1,0:T(8,128)S(1)}, f32[5,16,512]{2,1,0:T(8,128)S(1)}, f32[5,16,512]{2,1,0:T(8,128)S(1)}, f32[5,16,512]{2,1,0:T(8,128)S(1)}, f32[5,16,512]{2,1,0:T(8,128)S(1)}) custom-call(s32[8,16]{1,0:T(8,128)} %bitcast.22, f32[64,5,16,512]{3,2,1,0:T(8,128)} %bitcast.19), custom_call_target="tpu_custom_call" | custom-call | bytes 3000000 | tf_op jit(solution)/shard_map/pallas_call | solution.py:339
  9.7 1.5 %collective-permute-start.3 = (f32[5,16,512]{2,1,0:T(8,128)S(1)}, f32[5,16,512]{2,1,0:T(8,128)S(1)}, u32[]{:S(2)}, u32[]{:S(2)}) collective-permute-start(f32[5,16,512]{2,1,0:T(8,128)S(1)} %get-tuple-element.43), channel_id=1, source_target_pairs={{0,28},{4,24},{8,20},{12,16},{16,12},{20,8},{24,4},{28,0},{1,29},{... | collective-permute-start | bytes 491528 | tf_op jit(solution)/shard_map/ppermute | solution.py:348
  11.2 1.5 %collective-permute-start.4 = (f32[5,16,512]{2,1,0:T(8,128)S(1)}, f32[5,16,512]{2,1,0:T(8,128)S(1)}, u32[]{:S(2)}, u32[]{:S(2)}) collective-permute-start(f32[5,16,512]{2,1,0:T(8,128)S(1)} %get-tuple-element.44), channel_id=1, source_target_pairs={{0,4},{4,0},{8,12},{12,8},{16,20},{20,16},{24,28},{28,24},{1,5},{5... | collective-permute-start | bytes 491528 | tf_op jit(solution)/shard_map/ppermute | solution.py:348
  12.9 1.8 %collective-permute-done.1.refs_1_ = f32[5,16,512]{2,1,0:T(8,128)S(1)} collective-permute-done((f32[5,16,512]{2,1,0:T(8,128)S(1)}, f32[5,16,512]{2,1,0:T(8,128)S(1)}, u32[]{:S(2)}, u32[]{:S(2)}) %collective-permute-start.1) | collective-permute-done | bytes 163872 | tf_op jit(solution)/shard_map/ppermute | solution.py:348
  14.7 4.7 %shard_map.82 = (f32[64,5,16,512]{3,2,1,0:T(8,128)S(1)}, f32[64,16,512]{2,1,0:T(8,128)S(1)}, f32[64,5,16,512]{3,2,1,0:T(8,128)S(1)}, f32[5,16,512]{2,1,0:T(8,128)S(1)}, f32[5,16,512]{2,1,0:T(8,128)S(1)}) custom-call(f32[5]{0:T(128)S(1)} %copy-done.4, f32[64,5,16,512]{3,2,1,0:T(8,128)} %bitcast.20, f32[64,16,512]{2,1,0:T(8,128)S(1)} %bitcast.11), custom_call_target="tpu_custom_call" | custom-call | bytes 15000000 | tf_op jit(solution)/shard_map/pallas_call | solution.py:351
  19.4 1.9 %shard_map.85.refs_3_ = f32[64,5,16,512]{3,2,1,0:T(8,128)S(1)} custom-call(s32[8,16]{1,0:T(8,128)S(1)} %bitcast.12, s32[8,16]{1,0:T(8,128)S(1)} %bitcast.14, f32[8,16]{1,0:T(8,128)S(1)} %bitcast.16, f32[64,5,16,512]{3,2,1,0:T(8,128)S(1)} %get-tuple-element.39.flow_ref, ...), custom_call_target="tpu_custom_call", output_to_operand_aliasing={{}: (3, {})} | custom-call | bytes 6000000 | tf_op jit(solution)/shard_map/pallas_call | solution.py:358
  21.4 3.0 %shard_map.86 = (f32[64,5,16,512]{3,2,1,0:T(8,128)S(1)}, f32[4,5,16,512]{3,2,1,0:T(8,128)S(1)}, f32[2,5,16,512]{3,2,1,0:T(8,128)S(1)}, f32[2,5,16,512]{3,2,1,0:T...) custom-call(f32[5,16,512]{2,1,0:T(8,128)S(1)} %get-tuple-element.38.total_ref, ...), custom_call_target="tpu_custom_call", output_to_operand_aliasing={{0}: (4, {})} | custom-call | bytes 12000000 | tf_op jit(solution)/shard_map/pallas_call | solution.py:365
  24.4 1.9 %collective-permute-start.9 = (f32[2,5,16,512]{3,2,1,0:T(8,128)S(1)}, f32[2,5,16,512]{3,2,1,0:T(8,128)S(1)}, u32[]{:S(2)}, u32[]{:S(2)}) collective-permute-start(f32[2,5,16,512]{3,2,1,0:T(8,128)S(1)} %get-tuple-element.58), channel_id=1, source_target_pairs={{0,1},{1,0},{2,3},{3,2},{4,5},{5,4},{6,7},{7,6},{8,9},{9,8},{10,11... | collective-permute-start | bytes 983048 | tf_op jit(solution)/shard_map/ppermute | solution.py:378
  26.4 0.7 %collective-permute-start.10 = (f32[2,5,16,512]{3,2,1,0:T(8,128)S(1)}, f32[2,5,16,512]{3,2,1,0:T(8,128)S(1)}, u32[]{:S(2)}, u32[]{:S(2)}) collective-permute-start(f32[2,5,16,512]{3,2,1,0:T(8,128)S(1)} %get-tuple-element.59), channel_id=1, source_target_pairs={{0,0},{1,2},{2,1},{3,3},{4,4},{5,6},{6,5},{7,7},{8,8},{9,10},{10,9... | collective-permute-start | bytes 983048 | tf_op jit(solution)/shard_map/ppermute | solution.py:378
  27.6 0.7 %collective-permute-done.7.before_ref = f32[5,16,128]{2,1,0:T(8,128)S(1)} collective-permute-done((f32[5,16,128]{2,1,0:T(8,128)S(1)}, f32[5,16,128]{2,1,0:T(8,128)S(1)}, u32[]{:S(2)}, u32[]{:S(2)}) %collective-permute-start.7) | collective-permute-done | bytes 40992 | tf_op jit(solution)/shard_map/ppermute | solution.py:312
  28.5 7.4 %shard_map.87 = (f32[64,5,16,512]{3,2,1,0:T(8,128)S(1)}, f32[3,16,512]{2,1,0:T(8,128)S(1)}) custom-call(f32[5]{0:T(128)S(1)} %copy-done.4, f32[5]{0:T(128)S(1)} %copy-done.5, f32[64,5,16,512]{3,2,1,0:T(8,128)S(1)} %get-tuple-element.48.filled_ref, f32[64,5,16,512]{3,2,1,0:T(8,128)S(1)} %get-tuple-element.49.ratio_ref, ...), custom_call_target="tpu_custom_call", output_to_operand_aliasing={{0}: (2, {})} | custom-call | bytes 27000000 | tf_op jit(solution)/shard_map/pallas_call | solution.py:385
  36.1 2.6 %collective-permute-start.13 = (f32[3,16,512]{2,1,0:T(8,128)S(1)}, f32[3,16,512]{2,1,0:T(8,128)S(1)}, u32[]{:S(2)}, u32[]{:S(2)}) collective-permute-start(f32[3,16,512]{2,1,0:T(8,128)S(1)} %get-tuple-element.68), channel_id=1, source_target_pairs={{0,3},{1,0},{2,1},{3,2},{4,7},{5,4},{6,5},{7,6},{8,11},{9,8},{10,9... | collective-permute-start | bytes 294920 | tf_op jit(solution)/shard_map/ppermute | solution.py:312
  38.6 3.1 %collective-permute-start.12 = (f32[3,16,512]{2,1,0:T(8,128)S(1)}, f32[3,16,512]{2,1,0:T(8,128)S(1)}, u32[]{:S(2)}, u32[]{:S(2)}) collective-permute-start(f32[3,16,512]{2,1,0:T(8,128)S(1)} %get-tuple-element.67), channel_id=1, source_target_pairs={{0,2},{1,3},{2,0},{3,1},{4,6},{5,7},{6,4},{7,5},{8,10},{9,11},{10,... | collective-permute-start | bytes 294920 | tf_op jit(solution)/shard_map/ppermute | solution.py:312
  41.7 0.9 %collective-permute-start.11 = (f32[3,16,512]{2,1,0:T(8,128)S(1)}, f32[3,16,512]{2,1,0:T(8,128)S(1)}, u32[]{:S(2)}, u32[]{:S(2)}) collective-permute-start(f32[3,16,512]{2,1,0:T(8,128)S(1)} %get-tuple-element.67), channel_id=1, source_target_pairs={{0,1},{1,2},{2,3},{3,0},{4,5},{5,6},{6,7},{7,4},{8,9},{9,10},{10,1... | collective-permute-start | bytes 294920 | tf_op jit(solution)/shard_map/ppermute | solution.py:312
  42.6 2.9 %shard_map.88 = (f32[64,5,16,512]{3,2,1,0:T(8,128)S(1)}, f32[1,16,512]{2,1,0:T(8,128)S(1)}) custom-call(f32[5]{0:T(128)S(1)} %copy-done.4, f32[5]{0:T(128)S(1)} %copy-done.5, f32[64,5,16,512]{3,2,1,0:T(8,128)S(1)} %get-tuple-element.53.filled_ref, f32[64,5,16,512]{3,2,1,0:T(8,128)S(1)} %get-tuple-element.49.ratio_ref, ...), custom_call_target="tpu_custom_call", output_to_operand_aliasing={{0}: (2, {})} | custom-call | bytes 9000000 | tf_op jit(solution)/shard_map/pallas_call | solution.py:385
  45.5 2.9 %shard_map.89 = (f32[64,5,16,512]{3,2,1,0:T(8,128)S(1)}, f32[1,16,512]{2,1,0:T(8,128)S(1)}) custom-call(f32[5]{0:T(128)S(1)} %copy-done.4, f32[5]{0:T(128)S(1)} %copy-done.5, f32[64,5,16,512]{3,2,1,0:T(8,128)S(1)} %get-tuple-element.54.filled_ref, f32[64,5,16,512]{3,2,1,0:T(8,128)S(1)} %get-tuple-element.49.ratio_ref, ...), custom_call_target="tpu_custom_call", output_to_operand_aliasing={{0}: (2, {})} | custom-call | bytes 9000000 | tf_op jit(solution)/shard_map/pallas_call | solution.py:385
  48.5 3.0 %collective-permute-start.16 = (f32[2,16,512]{2,1,0:T(8,128)S(1)}, f32[2,16,512]{2,1,0:T(8,128)S(1)}, u32[]{:S(2)}, u32[]{:S(2)}) collective-permute-start(f32[2,16,512]{2,1,0:T(8,128)S(1)} %get-tuple-element.70), channel_id=1, source_target_pairs={{0,3},{1,0},{2,1},{3,2},{4,7},{5,4},{6,5},{7,6},{8,11},{9,8},{10,9... | collective-permute-start | bytes 196616 | tf_op jit(solution)/shard_map/ppermute | solution.py:312
  51.5 0.6 %collective-permute-start.14 = (f32[2,16,512]{2,1,0:T(8,128)S(1)}, f32[2,16,512]{2,1,0:T(8,128)S(1)}, u32[]{:S(2)}, u32[]{:S(2)}) collective-permute-start(f32[2,16,512]{2,1,0:T(8,128)S(1)} %get-tuple-element.69), channel_id=1, source_target_pairs={{0,1},{1,2},{2,3},{3,0},{4,5},{5,6},{6,7},{7,4},{8,9},{9,10},{10,1... | collective-permute-start | bytes 196616 | tf_op jit(solution)/shard_map/ppermute | solution.py:312
  52.1 2.7 %shard_map.92.refs_0_ = f32[64,5,16,512]{3,2,1,0:T(8,128)} custom-call(f32[64,5,16,512]{3,2,1,0:T(8,128)S(1)} %get-tuple-element.55.local_ref, f32[64,5,16,512]{3,2,1,0:T(8,128)S(1)} %get-tuple-element.49.ratio_ref, f32[3,16,512]{2,1,0:T(8,128)S(1)} %get-tuple-element.65.first_ref, f32[3,16,512]{2,1,0:T(8,128)S(1)} %get-tuple-element.66.last_ref, ...), custom_call_target="tpu_custom_call" | custom-call | bytes 9000000 | tf_op jit(solution)/shard_map/pallas_call | solution.py:406
  54.9 2.8 %collective-permute-done.15.refs_2_ = f32[2,16,512]{2,1,0:T(8,128)S(1)} collective-permute-done((f32[2,16,512]{2,1,0:T(8,128)S(1)}, f32[2,16,512]{2,1,0:T(8,128)S(1)}, u32[]{:S(2)}, u32[]{:S(2)}) %collective-permute-start.15) | collective-permute-done | bytes 65568 | tf_op jit(solution)/shard_map/ppermute | solution.py:312
  57.7 2.1 %shard_map.93 = f32[64,5,16,512]{3,2,1,0:T(8,128)} custom-call(f32[64,5,16,512]{3,2,1,0:T(8,128)S(1)} %get-tuple-element.55.local_ref, f32[64,5,16,512]{3,2,1,0:T(8,128)S(1)} %get-tuple-element.49.ratio_ref, f32[2,16,512]{2,1,0:T(8,128)S(1)} %get-tuple-element.62.first_ref, ...), custom_call_target="tpu_custom_call", output_to_operand_aliasing={{}: (6, {})} | custom-call | bytes 6000000 | tf_op jit(solution)/shard_map/pallas_call | solution.py:406
  (34 shorter events, 1.3 us)
Async XLA Ops:
  0.0 14.7 %copy-start = (f32[1,64,16,512]{3,2,1,0:T(8,128)S(1)}, f32[1,64,16,512]{3,2,1,0:T(8,128)}, u32[]{:S(2)}) copy-start(f32[1,64,16,512]{3,2,1,0:T(8,128)} %param.9) | copy-start | bytes 6291460
  0.0 14.7 %copy-start.4 = (f32[5]{0:T(128)S(1)}, f32[5]{0:T(128)}, u32[]{:S(2)}) copy-start(f32[5]{0:T(128)} %scale_ref.7) | copy-start | bytes 64
  2.4 10.3 %collective-permute-start = (f32[5,16,512]{2,1,0:T(8,128)S(1)}, f32[5,16,512]{2,1,0:T(8,128)S(1)}, u32[]{:S(2)}, u32[]{:S(2)}) collective-permute-start(f32[5,16,512]{2,1,0:T(8,128)S(1)} %get-tuple-element.40), channel_id=1, source_target_pairs={{0,24},{4,28},{8,16},{12,20},{16,8},{20,12},{24,0},{28,4},{1,25},{... | collective-permute-start | bytes 491528 | tf_op jit(solution)/shard_map/ppermute | solution.py:348
  6.4 8.3 %collective-permute-start.1 = (f32[5,16,512]{2,1,0:T(8,128)S(1)}, f32[5,16,512]{2,1,0:T(8,128)S(1)}, u32[]{:S(2)}, u32[]{:S(2)}) collective-permute-start(f32[5,16,512]{2,1,0:T(8,128)S(1)} %get-tuple-element.41), channel_id=1, source_target_pairs={{0,8},{4,12},{8,0},{12,4},{16,24},{20,28},{24,16},{28,20},{1,9},{5... | collective-permute-start | bytes 491528 | tf_op jit(solution)/shard_map/ppermute | solution.py:348
  6.9 12.5 %copy-start.1 = (s32[1,1,1,8,16]{4,3,2,1,0:T(8,128)S(1)}, s32[1,1,1,8,16]{4,3,2,1,0:T(8,128)}, u32[]{:S(2)}) copy-start(s32[1,1,1,8,16]{4,3,2,1,0:T(8,128)} %param.13) | copy-start | bytes 1540
  6.9 12.5 %copy-start.2 = (s32[1,1,1,8,16]{4,3,2,1,0:T(8,128)S(1)}, s32[1,1,1,8,16]{4,3,2,1,0:T(8,128)}, u32[]{:S(2)}) copy-start(s32[1,1,1,8,16]{4,3,2,1,0:T(8,128)} %param.14) | copy-start | bytes 1540
  6.9 12.5 %copy-start.3 = (f32[1,1,1,8,16]{4,3,2,1,0:T(8,128)S(1)}, f32[1,1,1,8,16]{4,3,2,1,0:T(8,128)}, u32[]{:S(2)}) copy-start(f32[1,1,1,8,16]{4,3,2,1,0:T(8,128)} %param.15) | copy-start | bytes 1540
  6.9 12.4 %collective-permute-start.2 = (f32[5,16,512]{2,1,0:T(8,128)S(1)}, f32[5,16,512]{2,1,0:T(8,128)S(1)}, u32[]{:S(2)}, u32[]{:S(2)}) collective-permute-start(f32[5,16,512]{2,1,0:T(8,128)S(1)} %get-tuple-element.42), channel_id=1, source_target_pairs={{0,16},{4,20},{8,24},{12,28},{16,0},{20,4},{24,8},{28,12},{1,17},{... | collective-permute-start | bytes 491528 | tf_op jit(solution)/shard_map/ppermute | solution.py:348
  9.7 9.7 %collective-permute-start.3 = (f32[5,16,512]{2,1,0:T(8,128)S(1)}, f32[5,16,512]{2,1,0:T(8,128)S(1)}, u32[]{:S(2)}, u32[]{:S(2)}) collective-permute-start(f32[5,16,512]{2,1,0:T(8,128)S(1)} %get-tuple-element.43), channel_id=1, source_target_pairs={{0,28},{4,24},{8,20},{12,16},{16,12},{20,8},{24,4},{28,0},{1,29},{... | collective-permute-start | bytes 491528 | tf_op jit(solution)/shard_map/ppermute | solution.py:348
  11.2 8.2 %collective-permute-start.4 = (f32[5,16,512]{2,1,0:T(8,128)S(1)}, f32[5,16,512]{2,1,0:T(8,128)S(1)}, u32[]{:S(2)}, u32[]{:S(2)}) collective-permute-start(f32[5,16,512]{2,1,0:T(8,128)S(1)} %get-tuple-element.44), channel_id=1, source_target_pairs={{0,4},{4,0},{8,12},{12,8},{16,20},{20,16},{24,28},{28,24},{1,5},{5... | collective-permute-start | bytes 491528 | tf_op jit(solution)/shard_map/ppermute | solution.py:348
  12.7 8.6 %collective-permute-start.5 = (f32[5,16,512]{2,1,0:T(8,128)S(1)}, f32[5,16,512]{2,1,0:T(8,128)S(1)}, u32[]{:S(2)}, u32[]{:S(2)}) collective-permute-start(f32[5,16,512]{2,1,0:T(8,128)S(1)} %get-tuple-element.46), channel_id=1, source_target_pairs={{0,12},{4,8},{8,4},{12,0},{16,28},{20,24},{24,20},{28,16},{1,13},{... | collective-permute-start | bytes 491528 | tf_op jit(solution)/shard_map/ppermute | solution.py:348
  14.6 6.7 %collective-permute-start.6 = (f32[5,16,512]{2,1,0:T(8,128)S(1)}, f32[5,16,512]{2,1,0:T(8,128)S(1)}, u32[]{:S(2)}, u32[]{:S(2)}) collective-permute-start(f32[5,16,512]{2,1,0:T(8,128)S(1)} %get-tuple-element.47), channel_id=1, source_target_pairs={{0,20},{4,16},{8,28},{12,24},{16,4},{20,0},{24,12},{28,8},{1,21},{... | collective-permute-start | bytes 491528 | tf_op jit(solution)/shard_map/ppermute | solution.py:348
  21.4 7.1 %copy-start.5 = (f32[5]{0:T(128)S(1)}, f32[5]{0:T(128)}, u32[]{:S(2)}) copy-start(f32[5]{0:T(128)} %span_ref.5) | copy-start | bytes 64
  24.4 11.5 %collective-permute-start.9 = (f32[2,5,16,512]{3,2,1,0:T(8,128)S(1)}, f32[2,5,16,512]{3,2,1,0:T(8,128)S(1)}, u32[]{:S(2)}, u32[]{:S(2)}) collective-permute-start(f32[2,5,16,512]{3,2,1,0:T(8,128)S(1)} %get-tuple-element.58), channel_id=1, source_target_pairs={{0,1},{1,0},{2,3},{3,2},{4,5},{5,4},{6,7},{7,6},{8,9},{9,8},{10,11... | collective-permute-start | bytes 983048 | tf_op jit(solution)/shard_map/ppermute | solution.py:378
  26.4 9.6 %collective-permute-start.10 = (f32[2,5,16,512]{3,2,1,0:T(8,128)S(1)}, f32[2,5,16,512]{3,2,1,0:T(8,128)S(1)}, u32[]{:S(2)}, u32[]{:S(2)}) collective-permute-start(f32[2,5,16,512]{3,2,1,0:T(8,128)S(1)} %get-tuple-element.59), channel_id=1, source_target_pairs={{0,0},{1,2},{2,1},{3,3},{4,4},{5,6},{6,5},{7,7},{8,8},{9,10},{10,9... | collective-permute-start | bytes 983048 | tf_op jit(solution)/shard_map/ppermute | solution.py:378
  27.0 1.3 %collective-permute-start.7 = (f32[5,16,128]{2,1,0:T(8,128)S(1)}, f32[5,16,128]{2,1,0:T(8,128)S(1)}, u32[]{:S(2)}, u32[]{:S(2)}) collective-permute-start(f32[5,16,128]{2,1,0:T(8,128)S(1)} %get-tuple-element.51.tail_ref), channel_id=1, source_target_pairs={{0,4},{4,0},{1,5},{5,1},{2,6},{6,2},{3,7},{7,3},{8,12},{12,8},{9,1... | collective-permute-start | bytes 122888 | tf_op jit(solution)/shard_map/ppermute | solution.py:312
  27.2 1.3 %collective-permute-start.8 = (f32[5,16,128]{2,1,0:T(8,128)S(1)}, f32[5,16,128]{2,1,0:T(8,128)S(1)}, u32[]{:S(2)}, u32[]{:S(2)}) collective-permute-start(f32[5,16,128]{2,1,0:T(8,128)S(1)} %get-tuple-element.52.head_ref), channel_id=1, source_target_pairs={{0,4},{4,0},{1,5},{5,1},{2,6},{6,2},{3,7},{7,3},{8,12},{12,8},{9,1... | collective-permute-start | bytes 122888 | tf_op jit(solution)/shard_map/ppermute | solution.py:312
  36.1 15.4 %collective-permute-start.13 = (f32[3,16,512]{2,1,0:T(8,128)S(1)}, f32[3,16,512]{2,1,0:T(8,128)S(1)}, u32[]{:S(2)}, u32[]{:S(2)}) collective-permute-start(f32[3,16,512]{2,1,0:T(8,128)S(1)} %get-tuple-element.68), channel_id=1, source_target_pairs={{0,3},{1,0},{2,1},{3,2},{4,7},{5,4},{6,5},{7,6},{8,11},{9,8},{10,9... | collective-permute-start | bytes 294920 | tf_op jit(solution)/shard_map/ppermute | solution.py:312
  38.6 13.5 %collective-permute-start.12 = (f32[3,16,512]{2,1,0:T(8,128)S(1)}, f32[3,16,512]{2,1,0:T(8,128)S(1)}, u32[]{:S(2)}, u32[]{:S(2)}) collective-permute-start(f32[3,16,512]{2,1,0:T(8,128)S(1)} %get-tuple-element.67), channel_id=1, source_target_pairs={{0,2},{1,3},{2,0},{3,1},{4,6},{5,7},{6,4},{7,5},{8,10},{9,11},{10,... | collective-permute-start | bytes 294920 | tf_op jit(solution)/shard_map/ppermute | solution.py:312
  41.7 10.4 %collective-permute-start.11 = (f32[3,16,512]{2,1,0:T(8,128)S(1)}, f32[3,16,512]{2,1,0:T(8,128)S(1)}, u32[]{:S(2)}, u32[]{:S(2)}) collective-permute-start(f32[3,16,512]{2,1,0:T(8,128)S(1)} %get-tuple-element.67), channel_id=1, source_target_pairs={{0,1},{1,2},{2,3},{3,0},{4,5},{5,6},{6,7},{7,4},{8,9},{9,10},{10,1... | collective-permute-start | bytes 294920 | tf_op jit(solution)/shard_map/ppermute | solution.py:312
  48.5 6.4 %collective-permute-start.16 = (f32[2,16,512]{2,1,0:T(8,128)S(1)}, f32[2,16,512]{2,1,0:T(8,128)S(1)}, u32[]{:S(2)}, u32[]{:S(2)}) collective-permute-start(f32[2,16,512]{2,1,0:T(8,128)S(1)} %get-tuple-element.70), channel_id=1, source_target_pairs={{0,3},{1,0},{2,1},{3,2},{4,7},{5,4},{6,5},{7,6},{8,11},{9,8},{10,9... | collective-permute-start | bytes 196616 | tf_op jit(solution)/shard_map/ppermute | solution.py:312
  51.5 6.2 %collective-permute-start.15 = (f32[2,16,512]{2,1,0:T(8,128)S(1)}, f32[2,16,512]{2,1,0:T(8,128)S(1)}, u32[]{:S(2)}, u32[]{:S(2)}) collective-permute-start(f32[2,16,512]{2,1,0:T(8,128)S(1)} %get-tuple-element.69), channel_id=1, source_target_pairs={{0,2},{1,3},{2,0},{3,1},{4,6},{5,7},{6,4},{7,5},{8,10},{9,11},{10,... | collective-permute-start | bytes 196616 | tf_op jit(solution)/shard_map/ppermute | solution.py:312
  51.5 6.2 %collective-permute-start.14 = (f32[2,16,512]{2,1,0:T(8,128)S(1)}, f32[2,16,512]{2,1,0:T(8,128)S(1)}, u32[]{:S(2)}, u32[]{:S(2)}) collective-permute-start(f32[2,16,512]{2,1,0:T(8,128)S(1)} %get-tuple-element.69), channel_id=1, source_target_pairs={{0,1},{1,2},{2,3},{3,0},{4,5},{5,6},{6,7},{7,4},{8,9},{9,10},{10,1... | collective-permute-start | bytes 196616 | tf_op jit(solution)/shard_map/ppermute | solution.py:312

commit v8 on v6

--- a/solution.py
+++ b/solution.py
@@ -137,16 +137,14 @@
                     filled_ref[x, v, y, :] = mixed[2 * v + i]
 
 
-def last_fill_kernel(turns, total_ref, *refs):
+def last_fill_kernel(turns, *refs):
     *fill_refs, rows_ref, even_ref, odd_ref, tail_ref, head_ref = refs
     fill_kernel(turns, *fill_refs)
     filled_ref = fill_refs[-1]
     width_x, components, rows_y, width_z = filled_ref.shape
     odd = lax.axis_index("stream") % 2
-    even_ref[0] = filled_ref[(width_x - 1) * (1 - odd)]
-    odd_ref[0] = filled_ref[(width_x - 1) * odd]
-    even_ref[1] = total_ref[...]
-    odd_ref[1] = total_ref[...]
+    even_ref[...] = filled_ref[(width_x - 1) * (1 - odd)]
+    odd_ref[...] = filled_ref[(width_x - 1) * odd]
     lane = lax.broadcasted_iota(jnp.int32, (rows_y, LANES), 1)
     for v in range(components):
 
@@ -246,18 +244,18 @@
 
 def edge_kernel(
     lowest, flux_ref, total_ref, last_ref, rows_ref, even_ref, odd_ref,
-    flux_out, beyond_out, first_out, last_out,
+    even_total_ref, odd_total_ref, flux_out, beyond_out, first_out, last_out,
 ):
     part = pl.ds(lowest, flux_ref.shape[0])
-    behind = beside("behind", even_ref.at[0, part], odd_ref.at[0, part]) * inside("stream", 1)
-    ahead = beside("ahead", even_ref.at[0, part], odd_ref.at[0, part]) * inside("stream", -1)
+    behind = beside("behind", even_ref.at[part], odd_ref.at[part]) * inside("stream", 1)
+    ahead = beside("ahead", even_ref.at[part], odd_ref.at[part]) * inside("stream", -1)
     row = [rows_ref[k, part] for k in range(4)]
     slope_first = limited(0.5 * (row[0] - behind), 0.5 * (row[1] - row[0]))
     slope_last = limited(0.5 * (row[3] - row[2]), 0.5 * (ahead - row[3]))
     kept = last_ref[part] * slope_last
     flux = flux_ref[...] + total_ref[part] * slope_first + kept
     flux_out[...] = flux
-    beyond_out[...] = beside("ahead", even_ref.at[1, part], odd_ref.at[1, part]) * flux
+    beyond_out[...] = beside("ahead", even_total_ref.at[part], odd_total_ref.at[part]) * flux
     first_out[...] = slope_first
     last_out[...] = kept
 
@@ -268,7 +266,7 @@
     components = first_ref.shape[0]
     flux = [present(ref, "stream", i + 1) for i, ref in enumerate(flux_refs)]
     beyond = sum(flux[2:], flux[1]) if len(flux) > 1 else 0.0
-    behind = beside("behind", *(ref.at[1, pl.ds(lowest, components)] for ref in (even_ref, odd_ref)))
+    behind = beside("behind", *(ref.at[pl.ds(lowest, components)] for ref in (even_ref, odd_ref)))
     inflow_ref[...] = first_ref[...] + flux[0] + behind * beyond
     part = 4
 
@@ -309,6 +307,12 @@
 def moved(value, axis, distance):
     count = lax.axis_size(axis)
     return lax.ppermute(value, axis, [(i, (i + distance) % count) for i in range(count)])
+
+
+def meet(value, shift):
+    count = lax.axis_size("stream")
+    others = [((i + shift) ^ 1) - shift for i in range(count)]
+    return lax.ppermute(value, "stream", [(i, k if 0 <= k < count else i) for i, k in enumerate(others)])
 
 
 def on_device(
@@ -331,6 +335,7 @@
     far = lambda turn: bin(turn >> 1).count("1")
     order = sorted(range(1, peers), key=lambda turn: (turn == 1, turn & 1, -far(turn), turn))
     near = peers // 2 - 1
+    send_hbm = pltpu.with_memory_space_constraint(send, HBM)
     arrived = {}
     groups = [order[:near], order[near:] + [0]]
     for turns in groups:
@@ -340,7 +345,7 @@
             [jax.ShapeDtypeStruct((components, capacity, width_z), F32)] * len(turns),
             [pltpu.SemaphoreType.DMA((len(turns),))],
             micros=1,
-        )(send, flow)
+        )(send_hbm, flow)
         for turn, tiles in zip(turns, outgoing):
             route = [(i, i ^ turn) for i in range(peers)]
             arrived[turn] = lax.ppermute(tiles, RING, route) if turn else tiles
@@ -353,6 +358,7 @@
         [pltpu.SemaphoreType.DMA((2,))],
         micros=5,
     )(char_scale, flow, speed)
+    odd_total, even_total = meet(total, 1), meet(total, 0)
     (partly,) = call(
         functools.partial(fill_kernel, early),
         (SMEM,) * 3 + (VMEM,) * (1 + len(early)), (VMEM,),
@@ -362,19 +368,15 @@
     )(tile, live, weight, flow_in, *(arrived[turn] for turn in early))
     filled, rows, even, odd, tail, head = call(
         functools.partial(last_fill_kernel, late),
-        (VMEM,) + (SMEM,) * 3 + (VMEM,) * (1 + len(late)), (VMEM,) * 6,
-        [hold(state), hold((4, *line)), hold((2, *line)), hold((2, *line)), hold(edge), hold(edge)],
-        aliases={4: 0},
+        (SMEM,) * 3 + (VMEM,) * (1 + len(late)), (VMEM,) * 6,
+        [hold(state), hold((4, *line)), hold(line), hold(line), hold(edge), hold(edge)],
+        aliases={3: 0},
         micros=4,
-    )(total, tile, live, weight, partly, *(arrived[turn] for turn in late))
+    )(tile, live, weight, partly, *(arrived[turn] for turn in late))
     before = moved(tail, "span", 1)
     after = moved(head, "span", -1)
-    met = []
-    for message, shift in ((odd, 1), (even, 0)):
-        others = [((i + shift) ^ 1) - shift for i in range(sections)]
-        route = [(i, k if 0 <= k < sections else i) for i, k in enumerate(others)]
-        met.append(lax.ppermute(message, "stream", route))
-    odd, even = met
+    odd = meet(odd, 1)
+    even = meet(even, 0)
     assert sections <= 4
     split = (components + 1) // 2
     state_now, parts = filled, []
@@ -390,9 +392,9 @@
         )(char_scale, span_ratio, state_now, ratio, speed_in, tail, head, before, after)
         flux, beyond, first_slope, last_slope = call(
             functools.partial(edge_kernel, lowest),
-            (VMEM,) * 6, (VMEM,) * 4,
+            (VMEM,) * 8, (VMEM,) * 4,
             [jax.ShapeDtypeStruct(some, F32)] * 4,
-        )(flux, total, last, rows, even, odd)
+        )(flux, total, last, rows, even, odd, even_total, odd_total)
         fluxes = [moved(flux if d < 3 else beyond, "stream", d) for d in range(1, sections)]
         parts.append((lowest, some, first_slope, last_slope, fluxes))
     begun = ()
@@ -409,7 +411,7 @@
             aliases={6: 0} if begun else None,
             limit=12 << 20,
             micros=some[0],
-        )(state_now, ratio, first_slope, last_slope, even, odd, *begun, *fluxes)
+        )(state_now, ratio, first_slope, last_slope, even_total, odd_total, *begun, *fluxes)
     (done,) = begun
     return jnp.transpose(done, (0, 2, 1, 3))[None]
 

time: 59.9 us -> 63.5 us (1.060)
  starting transfers between devices: 21.1 us -> 23.7 us
  waiting for transfers between devices: 5.73 us -> 7.01 us
  local copies, waits for them, and re-layouts: 0.71 us -> 0.02 us
    ppermute x2 -> x4, starting transfers between devices: 2.62 us -> 6.19 us  [meet(): lax.ppermute(value, 'stream', [(i, k if 0 <= k < count else i) for i, k i...]
    ppermute x8, waiting for transfers between devices: 3.7 us -> 5.21 us  [moved(): lax.ppermute(value, axis, [(i, (i + distance) % count) for i in range(cou...]
    ppermute x8, starting transfers between devices: 10.7 us -> 9.64 us  [moved(): lax.ppermute(value, axis, [(i, (i + distance) % count) for i in range(cou...]
    unnamed x14 -> x12, local copies, waits for them, and re-layouts: 0.71 us -> 0.02 us
  transfers between devices with their start and end apart: 17 -> 19, of which waited for: 5 -> 4; matrix products, arithmetic and copies ran while one was open for 0% -> 0% of each run, Pallas kernels for 41% -> 44%
where the time goes in v8:
time: 63.5 us; the launch traced here: 63.1 us
  Pallas kernels  32.2 us (51%)
  starting transfers between devices  23.7 us (37%)
  waiting for transfers between devices  7.01 us (11%)
    pallas_call x2, Pallas kernels, on_device(): call(functools.partial(scan_kernel, lowest), (SMEM, SMEM) + (VMEM,) * 7,...  12.6 us
    ppermute x8, starting transfers between devices, moved(): lax.ppermute(value, axis, [(i, (i + distance) % count) for i in range(cou...  9.64 us
    ppermute x7, starting transfers between devices, on_device(): arrived[turn] = lax.ppermute(tiles, RING, route) if turn else tiles  7.83 us
    ppermute x4, starting transfers between devices, meet(): lax.ppermute(value, 'stream', [(i, k if 0 <= k < count else i) for i, k i...  6.19 us
    ppermute x8, waiting for transfers between devices, moved(): lax.ppermute(value, axis, [(i, (i + distance) % count) for i in range(cou...  5.21 us
    pallas_call x2, Pallas kernels, on_device(): call(functools.partial(gather_kernel, turns), (SMEM, HBM), (VMEM,) * len(...  5.04 us
    pallas_call x2, Pallas kernels, on_device(): call(functools.partial(combine_kernel, lowest, len(begun)), (VMEM,) * 6 +...  4.83 us
    pallas_call x1, Pallas kernels, on_device(): call(growth_kernel, (SMEM, HBM, HBM), (VMEM,) * 5, [hold(state), hold(spe...  4.68 us
  transfers between devices with their start and end apart: 19, of which 4 were waited for; matrix products, arithmetic and copies ran while one was open for 0% of the time, Pallas kernels for 44%

profile of v8, /device:TPU:0, one launch (start us, length us, event | category | flops | bytes accessed | tf_op | source)
XLA Modules:
  0.0 63.1 jit_solution(9126725720137783678)
XLA Ops:
  0.0 2.4 %shard_map.83 = (f32[5,16,512]{2,1,0:T(8,128)S(1)}, f32[5,16,512]{2,1,0:T(8,128)S(1)}, f32[5,16,512]{2,1,0:T(8,128)S(1)}) custom-call(s32[8,16]{1,0:T(8,128)} %bitcast.21, f32[64,5,16,512]{3,2,1,0:T(8,128)} %bitcast.18), custom_call_target="tpu_custom_call" | custom-call | bytes 3000000 | tf_op jit(solution)/shard_map/pallas_call | solution.py:342
  2.4 4.0 %collective-permute-start = (f32[5,16,512]{2,1,0:T(8,128)S(1)}, f32[5,16,512]{2,1,0:T(8,128)S(1)}, u32[]{:S(2)}, u32[]{:S(2)}) collective-permute-start(f32[5,16,512]{2,1,0:T(8,128)S(1)} %get-tuple-element.37), channel_id=1, source_target_pairs={{0,24},{4,28},{8,16},{12,20},{16,8},{20,12},{24,0},{28,4},{1,25},{... | collective-permute-start | bytes 491528 | tf_op jit(solution)/shard_map/ppermute | solution.py:351
  7.0 2.7 %shard_map.84 = (f32[5,16,512]{2,1,0:T(8,128)S(1)}, f32[5,16,512]{2,1,0:T(8,128)S(1)}, f32[5,16,512]{2,1,0:T(8,128)S(1)}, f32[5,16,512]{2,1,0:T(8,128)S(1)}, f32[5,16,512]{2,1,0:T(8,128)S(1)}) custom-call(s32[8,16]{1,0:T(8,128)} %bitcast.22, f32[64,5,16,512]{3,2,1,0:T(8,128)} %bitcast.19), custom_call_target="tpu_custom_call" | custom-call | bytes 3000000 | tf_op jit(solution)/shard_map/pallas_call | solution.py:342
  9.7 1.5 %collective-permute-start.3 = (f32[5,16,512]{2,1,0:T(8,128)S(1)}, f32[5,16,512]{2,1,0:T(8,128)S(1)}, u32[]{:S(2)}, u32[]{:S(2)}) collective-permute-start(f32[5,16,512]{2,1,0:T(8,128)S(1)} %get-tuple-element.40), channel_id=1, source_target_pairs={{0,28},{4,24},{8,20},{12,16},{16,12},{20,8},{24,4},{28,0},{1,29},{... | collective-permute-start | bytes 491528 | tf_op jit(solution)/shard_map/ppermute | solution.py:351
  11.2 1.5 %collective-permute-start.4 = (f32[5,16,512]{2,1,0:T(8,128)S(1)}, f32[5,16,512]{2,1,0:T(8,128)S(1)}, u32[]{:S(2)}, u32[]{:S(2)}) collective-permute-start(f32[5,16,512]{2,1,0:T(8,128)S(1)} %get-tuple-element.41), channel_id=1, source_target_pairs={{0,4},{4,0},{8,12},{12,8},{16,20},{20,16},{24,28},{28,24},{1,5},{5... | collective-permute-start | bytes 491528 | tf_op jit(solution)/shard_map/ppermute | solution.py:351
  12.9 1.8 %collective-permute-done.1.refs_1_ = f32[5,16,512]{2,1,0:T(8,128)S(1)} collective-permute-done((f32[5,16,512]{2,1,0:T(8,128)S(1)}, f32[5,16,512]{2,1,0:T(8,128)S(1)}, u32[]{:S(2)}, u32[]{:S(2)}) %collective-permute-start.1) | collective-permute-done | bytes 163872 | tf_op jit(solution)/shard_map/ppermute | solution.py:351
  14.7 4.7 %shard_map.82 = (f32[64,5,16,512]{3,2,1,0:T(8,128)S(1)}, f32[64,16,512]{2,1,0:T(8,128)S(1)}, f32[64,5,16,512]{3,2,1,0:T(8,128)S(1)}, f32[5,16,512]{2,1,0:T(8,128)S(1)}, f32[5,16,512]{2,1,0:T(8,128)S(1)}) custom-call(f32[5]{0:T(128)S(1)} %copy-done.4, f32[64,5,16,512]{3,2,1,0:T(8,128)} %bitcast.20, f32[64,16,512]{2,1,0:T(8,128)S(1)} %bitcast.11), custom_call_target="tpu_custom_call" | custom-call | bytes 15000000 | tf_op jit(solution)/shard_map/pallas_call | solution.py:354
  19.4 0.7 %collective-permute-start.12 = (f32[5,16,512]{2,1,0:T(8,128)S(1)}, f32[5,16,512]{2,1,0:T(8,128)S(1)}, u32[]{:S(2)}, u32[]{:S(2)}) collective-permute-start(f32[5,16,512]{2,1,0:T(8,128)S(1)} %get-tuple-element.53.total_ref), channel_id=1, source_target_pairs={{0,0},{1,2},{2,1},{3,3},{4,4},{5,6},{6,5},{7,7},{8,8},{9,10},{10,9... | collective-permute-start | bytes 491528 | tf_op jit(solution)/shard_map/ppermute | solution.py:315
  20.1 4.5 %collective-permute-start.11 = (f32[5,16,512]{2,1,0:T(8,128)S(1)}, f32[5,16,512]{2,1,0:T(8,128)S(1)}, u32[]{:S(2)}, u32[]{:S(2)}) collective-permute-start(f32[5,16,512]{2,1,0:T(8,128)S(1)} %get-tuple-element.53.total_ref), channel_id=1, source_target_pairs={{0,1},{1,0},{2,3},{3,2},{4,5},{5,4},{6,7},{7,6},{8,9},{9,8},{10,11... | collective-permute-start | bytes 491528 | tf_op jit(solution)/shard_map/ppermute | solution.py:315
  24.5 1.9 %shard_map.85.refs_3_ = f32[64,5,16,512]{3,2,1,0:T(8,128)S(1)} custom-call(s32[8,16]{1,0:T(8,128)S(1)} %bitcast.12, s32[8,16]{1,0:T(8,128)S(1)} %bitcast.14, f32[8,16]{1,0:T(8,128)S(1)} %bitcast.16, f32[64,5,16,512]{3,2,1,0:T(8,128)S(1)} %get-tuple-element.36.flow_ref, ...), custom_call_target="tpu_custom_call", output_to_operand_aliasing={{}: (3, {})} | custom-call | bytes 6000000 | tf_op jit(solution)/shard_map/pallas_call | solution.py:362
  26.5 3.0 %shard_map.86 = (f32[64,5,16,512]{3,2,1,0:T(8,128)S(1)}, f32[4,5,16,512]{3,2,1,0:T(8,128)S(1)}, f32[5,16,512]{2,1,0:T(8,128)S(1)}, f32[5,16,512]{2,1,0:T(8,128)S...) custom-call(s32[8,16]{1,0:T(8,128)S(1)} %bitcast.13, ...), custom_call_target="tpu_custom_call", output_to_operand_aliasing={{0}: (3, {})} | custom-call | bytes 12000000 | tf_op jit(solution)/shard_map/pallas_call | solution.py:369
  29.9 0.7 %collective-permute-start.10 = (f32[5,16,512]{2,1,0:T(8,128)S(1)}, f32[5,16,512]{2,1,0:T(8,128)S(1)}, u32[]{:S(2)}, u32[]{:S(2)}) collective-permute-start(f32[5,16,512]{2,1,0:T(8,128)S(1)} %get-tuple-element.57), channel_id=1, source_target_pairs={{0,0},{1,2},{2,1},{3,3},{4,4},{5,6},{6,5},{7,7},{8,8},{9,10},{10,9... | collective-permute-start | bytes 491528 | tf_op jit(solution)/shard_map/ppermute | solution.py:315
  30.7 1.2 %collective-permute-done.7.before_ref = f32[5,16,128]{2,1,0:T(8,128)S(1)} collective-permute-done((f32[5,16,128]{2,1,0:T(8,128)S(1)}, f32[5,16,128]{2,1,0:T(8,128)S(1)}, u32[]{:S(2)}, u32[]{:S(2)}) %collective-permute-start.7) | collective-permute-done | bytes 40992 | tf_op jit(solution)/shard_map/ppermute | solution.py:309
  32.0 1.1 %collective-permute-done.8.after_ref = f32[5,16,128]{2,1,0:T(8,128)S(1)} collective-permute-done((f32[5,16,128]{2,1,0:T(8,128)S(1)}, f32[5,16,128]{2,1,0:T(8,128)S(1)}, u32[]{:S(2)}, u32[]{:S(2)}) %collective-permute-start.8) | collective-permute-done | bytes 40992 | tf_op jit(solution)/shard_map/ppermute | solution.py:309
  33.1 7.4 %shard_map.87 = (f32[64,5,16,512]{3,2,1,0:T(8,128)S(1)}, f32[3,16,512]{2,1,0:T(8,128)S(1)}) custom-call(f32[5]{0:T(128)S(1)} %copy-done.4, f32[5]{0:T(128)S(1)} %copy-done.5, f32[64,5,16,512]{3,2,1,0:T(8,128)S(1)} %get-tuple-element.45.filled_ref, f32[64,5,16,512]{3,2,1,0:T(8,128)S(1)} %get-tuple-element.46.ratio_ref, ...), custom_call_target="tpu_custom_call", output_to_operand_aliasing={{0}: (2, {})} | custom-call | bytes 27000000 | tf_op jit(solution)/shard_map/pallas_call | solution.py:385
  40.7 1.2 %collective-permute-start.15 = (f32[3,16,512]{2,1,0:T(8,128)S(1)}, f32[3,16,512]{2,1,0:T(8,128)S(1)}, u32[]{:S(2)}, u32[]{:S(2)}) collective-permute-start(f32[3,16,512]{2,1,0:T(8,128)S(1)} %get-tuple-element.64), channel_id=1, source_target_pairs={{0,3},{1,0},{2,1},{3,2},{4,7},{5,4},{6,5},{7,6},{8,11},{9,8},{10,9... | collective-permute-start | bytes 294920 | tf_op jit(solution)/shard_map/ppermute | solution.py:309
  41.8 3.7 %collective-permute-start.14 = (f32[3,16,512]{2,1,0:T(8,128)S(1)}, f32[3,16,512]{2,1,0:T(8,128)S(1)}, u32[]{:S(2)}, u32[]{:S(2)}) collective-permute-start(f32[3,16,512]{2,1,0:T(8,128)S(1)} %get-tuple-element.63), channel_id=1, source_target_pairs={{0,2},{1,3},{2,0},{3,1},{4,6},{5,7},{6,4},{7,5},{8,10},{9,11},{10,... | collective-permute-start | bytes 294920 | tf_op jit(solution)/shard_map/ppermute | solution.py:309
  45.6 1.6 %collective-permute-start.13 = (f32[3,16,512]{2,1,0:T(8,128)S(1)}, f32[3,16,512]{2,1,0:T(8,128)S(1)}, u32[]{:S(2)}, u32[]{:S(2)}) collective-permute-start(f32[3,16,512]{2,1,0:T(8,128)S(1)} %get-tuple-element.63), channel_id=1, source_target_pairs={{0,1},{1,2},{2,3},{3,0},{4,5},{5,6},{6,7},{7,4},{8,9},{9,10},{10,1... | collective-permute-start | bytes 294920 | tf_op jit(solution)/shard_map/ppermute | solution.py:309
  47.1 5.2 %shard_map.88 = (f32[64,5,16,512]{3,2,1,0:T(8,128)S(1)}, f32[2,16,512]{2,1,0:T(8,128)S(1)}) custom-call(f32[5]{0:T(128)S(1)} %copy-done.4, f32[5]{0:T(128)S(1)} %copy-done.5, f32[64,5,16,512]{3,2,1,0:T(8,128)S(1)} %get-tuple-element.50.filled_ref, f32[64,5,16,512]{3,2,1,0:T(8,128)S(1)} %get-tuple-element.46.ratio_ref, ...), custom_call_target="tpu_custom_call", output_to_operand_aliasing={{0}: (2, {})} | custom-call | bytes 18000000 | tf_op jit(solution)/shard_map/pallas_call | solution.py:385
  52.4 2.3 %collective-permute-start.18 = (f32[2,16,512]{2,1,0:T(8,128)S(1)}, f32[2,16,512]{2,1,0:T(8,128)S(1)}, u32[]{:S(2)}, u32[]{:S(2)}) collective-permute-start(f32[2,16,512]{2,1,0:T(8,128)S(1)} %get-tuple-element.66), channel_id=1, source_target_pairs={{0,3},{1,0},{2,1},{3,2},{4,7},{5,4},{6,5},{7,6},{8,11},{9,8},{10,9... | collective-permute-start | bytes 196616 | tf_op jit(solution)/shard_map/ppermute | solution.py:309
  54.7 0.6 %collective-permute-start.16 = (f32[2,16,512]{2,1,0:T(8,128)S(1)}, f32[2,16,512]{2,1,0:T(8,128)S(1)}, u32[]{:S(2)}, u32[]{:S(2)}) collective-permute-start(f32[2,16,512]{2,1,0:T(8,128)S(1)} %get-tuple-element.65), channel_id=1, source_target_pairs={{0,1},{1,2},{2,3},{3,0},{4,5},{5,6},{6,7},{7,4},{8,9},{9,10},{10,1... | collective-permute-start | bytes 196616 | tf_op jit(solution)/shard_map/ppermute | solution.py:309
  55.4 2.8 %shard_map.91.refs_0_ = f32[64,5,16,512]{3,2,1,0:T(8,128)} custom-call(f32[64,5,16,512]{3,2,1,0:T(8,128)S(1)} %get-tuple-element.51.local_ref, f32[64,5,16,512]{3,2,1,0:T(8,128)S(1)} %get-tuple-element.46.ratio_ref, f32[3,16,512]{2,1,0:T(8,128)S(1)} %get-tuple-element.61.first_ref, f32[3,16,512]{2,1,0:T(8,128)S(1)} %get-tuple-element.62.last_ref, ...), custom_call_target="tpu_custom_call" | custom-call | bytes 9000000 | tf_op jit(solution)/shard_map/pallas_call | solution.py:402
  58.1 2.9 %collective-permute-done.17.refs_2_ = f32[2,16,512]{2,1,0:T(8,128)S(1)} collective-permute-done((f32[2,16,512]{2,1,0:T(8,128)S(1)}, f32[2,16,512]{2,1,0:T(8,128)S(1)}, u32[]{:S(2)}, u32[]{:S(2)}) %collective-permute-start.17) | collective-permute-done | bytes 65568 | tf_op jit(solution)/shard_map/ppermute | solution.py:309
  61.0 2.1 %shard_map.92 = f32[64,5,16,512]{3,2,1,0:T(8,128)} custom-call(f32[64,5,16,512]{3,2,1,0:T(8,128)S(1)} %get-tuple-element.51.local_ref, f32[64,5,16,512]{3,2,1,0:T(8,128)S(1)} %get-tuple-element.46.ratio_ref, f32[2,16,512]{2,1,0:T(8,128)S(1)} %get-tuple-element.58.first_ref, ...), custom_call_target="tpu_custom_call", output_to_operand_aliasing={{}: (6, {})} | custom-call | bytes 6000000 | tf_op jit(solution)/shard_map/pallas_call | solution.py:402
  (37 shorter events, 1.7 us)
Async XLA Ops:
  0.0 14.7 %copy-start = (f32[1,64,16,512]{3,2,1,0:T(8,128)S(1)}, f32[1,64,16,512]{3,2,1,0:T(8,128)}, u32[]{:S(2)}) copy-start(f32[1,64,16,512]{3,2,1,0:T(8,128)} %param.9) | copy-start | bytes 6291460
  0.0 14.7 %copy-start.4 = (f32[5]{0:T(128)S(1)}, f32[5]{0:T(128)}, u32[]{:S(2)}) copy-start(f32[5]{0:T(128)} %scale_ref.5) | copy-start | bytes 64
  2.4 10.3 %collective-permute-start = (f32[5,16,512]{2,1,0:T(8,128)S(1)}, f32[5,16,512]{2,1,0:T(8,128)S(1)}, u32[]{:S(2)}, u32[]{:S(2)}) collective-permute-start(f32[5,16,512]{2,1,0:T(8,128)S(1)} %get-tuple-element.37), channel_id=1, source_target_pairs={{0,24},{4,28},{8,16},{12,20},{16,8},{20,12},{24,0},{28,4},{1,25},{... | collective-permute-start | bytes 491528 | tf_op jit(solution)/shard_map/ppermute | solution.py:351
  6.4 8.3 %collective-permute-start.1 = (f32[5,16,512]{2,1,0:T(8,128)S(1)}, f32[5,16,512]{2,1,0:T(8,128)S(1)}, u32[]{:S(2)}, u32[]{:S(2)}) collective-permute-start(f32[5,16,512]{2,1,0:T(8,128)S(1)} %get-tuple-element.38), channel_id=1, source_target_pairs={{0,8},{4,12},{8,0},{12,4},{16,24},{20,28},{24,16},{28,20},{1,9},{5... | collective-permute-start | bytes 491528 | tf_op jit(solution)/shard_map/ppermute | solution.py:351
  6.9 17.6 %copy-start.1 = (s32[1,1,1,8,16]{4,3,2,1,0:T(8,128)S(1)}, s32[1,1,1,8,16]{4,3,2,1,0:T(8,128)}, u32[]{:S(2)}) copy-start(s32[1,1,1,8,16]{4,3,2,1,0:T(8,128)} %param.13) | copy-start | bytes 1540
  6.9 17.6 %copy-start.2 = (s32[1,1,1,8,16]{4,3,2,1,0:T(8,128)S(1)}, s32[1,1,1,8,16]{4,3,2,1,0:T(8,128)}, u32[]{:S(2)}) copy-start(s32[1,1,1,8,16]{4,3,2,1,0:T(8,128)} %param.14) | copy-start | bytes 1540
  6.9 17.6 %copy-start.3 = (f32[1,1,1,8,16]{4,3,2,1,0:T(8,128)S(1)}, f32[1,1,1,8,16]{4,3,2,1,0:T(8,128)}, u32[]{:S(2)}) copy-start(f32[1,1,1,8,16]{4,3,2,1,0:T(8,128)} %param.15) | copy-start | bytes 1540
  6.9 12.4 %collective-permute-start.2 = (f32[5,16,512]{2,1,0:T(8,128)S(1)}, f32[5,16,512]{2,1,0:T(8,128)S(1)}, u32[]{:S(2)}, u32[]{:S(2)}) collective-permute-start(f32[5,16,512]{2,1,0:T(8,128)S(1)} %get-tuple-element.39), channel_id=1, source_target_pairs={{0,16},{4,20},{8,24},{12,28},{16,0},{20,4},{24,8},{28,12},{1,17},{... | collective-permute-start | bytes 491528 | tf_op jit(solution)/shard_map/ppermute | solution.py:351
  9.7 10.4 %collective-permute-start.3 = (f32[5,16,512]{2,1,0:T(8,128)S(1)}, f32[5,16,512]{2,1,0:T(8,128)S(1)}, u32[]{:S(2)}, u32[]{:S(2)}) collective-permute-start(f32[5,16,512]{2,1,0:T(8,128)S(1)} %get-tuple-element.40), channel_id=1, source_target_pairs={{0,28},{4,24},{8,20},{12,16},{16,12},{20,8},{24,4},{28,0},{1,29},{... | collective-permute-start | bytes 491528 | tf_op jit(solution)/shard_map/ppermute | solution.py:351
  11.2 13.3 %collective-permute-start.4 = (f32[5,16,512]{2,1,0:T(8,128)S(1)}, f32[5,16,512]{2,1,0:T(8,128)S(1)}, u32[]{:S(2)}, u32[]{:S(2)}) collective-permute-start(f32[5,16,512]{2,1,0:T(8,128)S(1)} %get-tuple-element.41), channel_id=1, source_target_pairs={{0,4},{4,0},{8,12},{12,8},{16,20},{20,16},{24,28},{28,24},{1,5},{5... | collective-permute-start | bytes 491528 | tf_op jit(solution)/shard_map/ppermute | solution.py:351
  12.7 13.8 %collective-permute-start.5 = (f32[5,16,512]{2,1,0:T(8,128)S(1)}, f32[5,16,512]{2,1,0:T(8,128)S(1)}, u32[]{:S(2)}, u32[]{:S(2)}) collective-permute-start(f32[5,16,512]{2,1,0:T(8,128)S(1)} %get-tuple-element.43), channel_id=1, source_target_pairs={{0,12},{4,8},{8,4},{12,0},{16,28},{20,24},{24,20},{28,16},{1,13},{... | collective-permute-start | bytes 491528 | tf_op jit(solution)/shard_map/ppermute | solution.py:351
  14.6 11.9 %collective-permute-start.6 = (f32[5,16,512]{2,1,0:T(8,128)S(1)}, f32[5,16,512]{2,1,0:T(8,128)S(1)}, u32[]{:S(2)}, u32[]{:S(2)}) collective-permute-start(f32[5,16,512]{2,1,0:T(8,128)S(1)} %get-tuple-element.44), channel_id=1, source_target_pairs={{0,20},{4,16},{8,28},{12,24},{16,4},{20,0},{24,12},{28,8},{1,21},{... | collective-permute-start | bytes 491528 | tf_op jit(solution)/shard_map/ppermute | solution.py:351
  19.4 21.1 %collective-permute-start.12 = (f32[5,16,512]{2,1,0:T(8,128)S(1)}, f32[5,16,512]{2,1,0:T(8,128)S(1)}, u32[]{:S(2)}, u32[]{:S(2)}) collective-permute-start(f32[5,16,512]{2,1,0:T(8,128)S(1)} %get-tuple-element.53.total_ref), channel_id=1, source_target_pairs={{0,0},{1,2},{2,1},{3,3},{4,4},{5,6},{6,5},{7,7},{8,8},{9,10},{10,9... | collective-permute-start | bytes 491528 | tf_op jit(solution)/shard_map/ppermute | solution.py:315
  20.1 20.5 %collective-permute-start.11 = (f32[5,16,512]{2,1,0:T(8,128)S(1)}, f32[5,16,512]{2,1,0:T(8,128)S(1)}, u32[]{:S(2)}, u32[]{:S(2)}) collective-permute-start(f32[5,16,512]{2,1,0:T(8,128)S(1)} %get-tuple-element.53.total_ref), channel_id=1, source_target_pairs={{0,1},{1,0},{2,3},{3,2},{4,5},{5,4},{6,7},{7,6},{8,9},{9,8},{10,11... | collective-permute-start | bytes 491528 | tf_op jit(solution)/shard_map/ppermute | solution.py:315
  29.5 11.0 %collective-permute-start.9 = (f32[5,16,512]{2,1,0:T(8,128)S(1)}, f32[5,16,512]{2,1,0:T(8,128)S(1)}, u32[]{:S(2)}, u32[]{:S(2)}) collective-permute-start(f32[5,16,512]{2,1,0:T(8,128)S(1)} %get-tuple-element.56), channel_id=1, source_target_pairs={{0,1},{1,0},{2,3},{3,2},{4,5},{5,4},{6,7},{7,6},{8,9},{9,8},{10,11... | collective-permute-start | bytes 491528 | tf_op jit(solution)/shard_map/ppermute | solution.py:315
  29.9 10.6 %collective-permute-start.10 = (f32[5,16,512]{2,1,0:T(8,128)S(1)}, f32[5,16,512]{2,1,0:T(8,128)S(1)}, u32[]{:S(2)}, u32[]{:S(2)}) collective-permute-start(f32[5,16,512]{2,1,0:T(8,128)S(1)} %get-tuple-element.57), channel_id=1, source_target_pairs={{0,0},{1,2},{2,1},{3,3},{4,4},{5,6},{6,5},{7,7},{8,8},{9,10},{10,9... | collective-permute-start | bytes 491528 | tf_op jit(solution)/shard_map/ppermute | solution.py:315
  30.6 1.3 %collective-permute-start.7 = (f32[5,16,128]{2,1,0:T(8,128)S(1)}, f32[5,16,128]{2,1,0:T(8,128)S(1)}, u32[]{:S(2)}, u32[]{:S(2)}) collective-permute-start(f32[5,16,128]{2,1,0:T(8,128)S(1)} %get-tuple-element.48.tail_ref), channel_id=1, source_target_pairs={{0,4},{4,0},{1,5},{5,1},{2,6},{6,2},{3,7},{7,3},{8,12},{12,8},{9,1... | collective-permute-start | bytes 122888 | tf_op jit(solution)/shard_map/ppermute | solution.py:309
  31.9 1.2 %collective-permute-start.8 = (f32[5,16,128]{2,1,0:T(8,128)S(1)}, f32[5,16,128]{2,1,0:T(8,128)S(1)}, u32[]{:S(2)}, u32[]{:S(2)}) collective-permute-start(f32[5,16,128]{2,1,0:T(8,128)S(1)} %get-tuple-element.49.head_ref), channel_id=1, source_target_pairs={{0,4},{4,0},{1,5},{5,1},{2,6},{6,2},{3,7},{7,3},{8,12},{12,8},{9,1... | collective-permute-start | bytes 122888 | tf_op jit(solution)/shard_map/ppermute | solution.py:309
  40.7 14.0 %collective-permute-start.15 = (f32[3,16,512]{2,1,0:T(8,128)S(1)}, f32[3,16,512]{2,1,0:T(8,128)S(1)}, u32[]{:S(2)}, u32[]{:S(2)}) collective-permute-start(f32[3,16,512]{2,1,0:T(8,128)S(1)} %get-tuple-element.64), channel_id=1, source_target_pairs={{0,3},{1,0},{2,1},{3,2},{4,7},{5,4},{6,5},{7,6},{8,11},{9,8},{10,9... | collective-permute-start | bytes 294920 | tf_op jit(solution)/shard_map/ppermute | solution.py:309
  41.8 13.5 %collective-permute-start.14 = (f32[3,16,512]{2,1,0:T(8,128)S(1)}, f32[3,16,512]{2,1,0:T(8,128)S(1)}, u32[]{:S(2)}, u32[]{:S(2)}) collective-permute-start(f32[3,16,512]{2,1,0:T(8,128)S(1)} %get-tuple-element.63), channel_id=1, source_target_pairs={{0,2},{1,3},{2,0},{3,1},{4,6},{5,7},{6,4},{7,5},{8,10},{9,11},{10,... | collective-permute-start | bytes 294920 | tf_op jit(solution)/shard_map/ppermute | solution.py:309
  45.6 9.8 %collective-permute-start.13 = (f32[3,16,512]{2,1,0:T(8,128)S(1)}, f32[3,16,512]{2,1,0:T(8,128)S(1)}, u32[]{:S(2)}, u32[]{:S(2)}) collective-permute-start(f32[3,16,512]{2,1,0:T(8,128)S(1)} %get-tuple-element.63), channel_id=1, source_target_pairs={{0,1},{1,2},{2,3},{3,0},{4,5},{5,6},{6,7},{7,4},{8,9},{9,10},{10,1... | collective-permute-start | bytes 294920 | tf_op jit(solution)/shard_map/ppermute | solution.py:309
  52.4 5.7 %collective-permute-start.18 = (f32[2,16,512]{2,1,0:T(8,128)S(1)}, f32[2,16,512]{2,1,0:T(8,128)S(1)}, u32[]{:S(2)}, u32[]{:S(2)}) collective-permute-start(f32[2,16,512]{2,1,0:T(8,128)S(1)} %get-tuple-element.66), channel_id=1, source_target_pairs={{0,3},{1,0},{2,1},{3,2},{4,7},{5,4},{6,5},{7,6},{8,11},{9,8},{10,9... | collective-permute-start | bytes 196616 | tf_op jit(solution)/shard_map/ppermute | solution.py:309
  54.7 6.4 %collective-permute-start.17 = (f32[2,16,512]{2,1,0:T(8,128)S(1)}, f32[2,16,512]{2,1,0:T(8,128)S(1)}, u32[]{:S(2)}, u32[]{:S(2)}) collective-permute-start(f32[2,16,512]{2,1,0:T(8,128)S(1)} %get-tuple-element.65), channel_id=1, source_target_pairs={{0,2},{1,3},{2,0},{3,1},{4,6},{5,7},{6,4},{7,5},{8,10},{9,11},{10,... | collective-permute-start | bytes 196616 | tf_op jit(solution)/shard_map/ppermute | solution.py:309
  54.7 6.4 %collective-permute-start.16 = (f32[2,16,512]{2,1,0:T(8,128)S(1)}, f32[2,16,512]{2,1,0:T(8,128)S(1)}, u32[]{:S(2)}, u32[]{:S(2)}) collective-permute-start(f32[2,16,512]{2,1,0:T(8,128)S(1)} %get-tuple-element.65), channel_id=1, source_target_pairs={{0,1},{1,2},{2,3},{3,0},{4,5},{5,6},{6,7},{7,4},{8,9},{9,10},{10,1... | collective-permute-start | bytes 196616 | tf_op jit(solution)/shard_map/ppermute | solution.py:309
  (1 other events, 6.6 us)
